TPU v7x, 32 devices: a whole 2x2x4 slice. The times are simulated.
32 devices in a mesh: seq: 4 (over y, x), batch: 8 (over z, core).
Axes of the slice: x: 2, y: 2, z: 4, core: 2. Of those that a mesh axis runs over, the one named last changes fastest.
Arguments:
- tokens: bfloat16 [8, 1024, 768], P('batch', 'seq'), may hold values from -6 to 6
- cotangent: bfloat16 [8, 1024, 768], P('batch', 'seq'), may hold values from -6 to 6
- segments: int32 [8, 1024], P('batch', 'seq'), may hold values from 0 to 2, never falling along the last dimension, each value on 1 to 512 neighbouring positions
- in_weight: bfloat16 [768, 3352], P(('seq', 'batch')), may hold values from -0.21875 to 0.21875
- out_weight: bfloat16 [1536, 768], P(('seq', 'batch')), may hold values from -0.15625 to 0.15625
- gain_in: float32 [768], replicated, may hold values from 0.5 to 1.5
- conv_weight: float32 [4, 1792], replicated, may hold values from -3 to 3
- conv_bias: float32 [1792], replicated, may hold values from -3 to 3
- dt_bias: float32 [24], replicated, may hold values from -5 to -3
- a_log: float32 [24], replicated, may hold values from -5.5 to 1
- d_skip: float32 [24], replicated, may hold values from 0.5 to 1.5
- gain_out: float32 [1536], replicated, may hold values from 0.5 to 1.5
Outputs:
- result: bfloat16 [8, 1024, 768], P('batch', 'seq')
- grad_tokens: bfloat16 [8, 1024, 768], P('batch', 'seq')
- grad_in_weight: float32 [768, 3352], P(('seq', 'batch'))
- grad_out_weight: float32 [1536, 768], P(('seq', 'batch'))
- grad_gain_in: float32 [768], replicated
- grad_conv_weight: float32 [4, 1792], replicated
- grad_conv_bias: float32 [1792], replicated
- grad_dt_bias: float32 [24], replicated
- grad_a_log: float32 [24], replicated
- grad_d_skip: float32 [24], replicated
- grad_gain_out: float32 [1536], replicated
Inputs may be any that keep to these rules, and one draw needn't show every extreme that they name: `segments`: within each sequence the numbers start at 0 and never fall; the tokens of one number form one document of 1 to 512 tokens, and one document in each sequence has exactly 512.
All inputs are finite; a program needn't handle non-finite values.
Results may differ from a plain program's by a relative error of at most 0.0064.
Values may be sent and summed in bfloat16 or wider, within the bound.
No kernel may reach another device: no remote copies, remote signals or barrier semaphores. Data moves between devices by JAX's collectives and lax.ppermute only.
A program may use at most 128 MiB of HBM per device.

v0:
```python
import jax
import jax.numpy as jnp
from jax import lax
from jax.sharding import PartitionSpec as P

HEADS = 24
HEADDIM = 64
STATE = 128
KERNEL = 4
GROUP = 128
INNER = 1536
CONV = 1792


highest = lax.Precision.HIGHEST
norm_eps = 1e-05


def shifted(value, axis, by):
    size = lax.axis_size(axis)
    pairs = [(i, i + by) for i in range(size) if 0 <= i + by < size]
    return lax.ppermute(value, axis, pairs)


def prefix(value, axis, join, neutral):
    place = lax.axis_index(axis)
    gathered = jax.tree.map(
        lambda a, kind: lax.all_gather(a.astype(kind), axis), value, (jnp.bfloat16, jnp.bfloat16)
    )
    state = jax.tree.map(lambda a, e: jnp.zeros_like(a) + jnp.asarray(e, a.dtype), value, neutral)

    def one(turn, state):
        return join(
            state,
            jax.tree.map(
                lambda a, own: lax.dynamic_index_in_dim(a, turn, 0, False).astype(own.dtype),
                gathered,
                value,
            ),
        )

    return lax.fori_loop(0, place, one, state)


def prefix_2(value, axis, join, neutral):
    count = lax.axis_size(axis)
    place = lax.axis_index(axis)
    ahead = count - 1 - place
    gathered = jax.tree.map(
        lambda a, kind: lax.all_gather(a.astype(kind), axis),
        value,
        jax.tree.map(lambda a: jnp.bfloat16 if a.dtype == jnp.float32 else a.dtype, value),
    )
    state = jax.tree.map(lambda a, e: jnp.zeros_like(a) + jnp.asarray(e, a.dtype), value, neutral)

    def one(turn, state):
        source = count - 1 - turn
        return join(
            state,
            jax.tree.map(
                lambda a, own: lax.dynamic_index_in_dim(a, source, 0, False).astype(own.dtype),
                gathered,
                value,
            ),
        )

    return lax.fori_loop(0, ahead, one, state)


def rms_scale(values, gain):
    mean_square = jnp.mean(values * values, axis=-1, keepdims=True)
    return values * lax.rsqrt(mean_square + norm_eps) * gain


def causal_conv(extended, ext_segs, conv_weight, conv_bias, row_count):
    target = ext_segs[KERNEL - 1 :]
    total = jnp.zeros((row_count, conv_weight.shape[1]), jnp.float32) + conv_bias[None, :]
    for offset in range(KERNEL):
        window = extended[offset : offset + row_count]
        same_doc = (ext_segs[offset : offset + row_count] == target).astype(jnp.float32)
        total = total + conv_weight[offset][None, :] * window * same_doc[:, None]
    return jax.nn.silu(total)


def prepare(xbc, dt_raw, edge_rows, ext_segs, conv_weight, conv_bias, dt_bias, a_log):
    row_count = xbc.shape[0]
    extended = jnp.concatenate([edge_rows, xbc], axis=0)
    mixed = causal_conv(extended, ext_segs, conv_weight, conv_bias, row_count)
    values = mixed[:, :INNER].reshape(row_count, HEADS, HEADDIM)
    key_vecs = mixed[:, INNER : INNER + STATE]
    queries = mixed[:, INNER + STATE :]
    step_sizes = jax.nn.softplus(dt_raw + dt_bias[None, :])
    log_decay = -step_sizes * jnp.exp(a_log)[None, :]
    return (values, key_vecs, queries, step_sizes, log_decay)


def group_block(carried, block_in):
    state_in, last_seg = carried
    values, key_vecs, queries, step_sizes, log_decay, seg_ids = block_in
    length_here = seg_ids.shape[0]
    cumulative = jnp.cumsum(log_decay, axis=0)
    positions = jnp.arange(length_here)
    allowed = (seg_ids[:, None] == seg_ids[None, :]) & (positions[:, None] >= positions[None, :])
    gap_logs = cumulative[:, None, :] - cumulative[None, :, :]
    decay_mask = jnp.where(allowed[:, :, None], jnp.exp(jnp.minimum(gap_logs, 0.0)), 0.0)
    scores = jnp.dot(queries, key_vecs.T, precision=highest)
    weights = decay_mask * scores[:, :, None] * step_sizes[None, :, :]
    inside = jnp.einsum("tsh,shp->thp", weights, values, precision=highest)
    keep_factor = jnp.where((seg_ids == last_seg)[:, None], jnp.exp(cumulative), 0.0)
    carried_out = (
        jnp.einsum("tn,hpn->thp", queries, state_in, precision=highest) * keep_factor[:, :, None]
    )
    to_end = (
        jnp.where(
            (seg_ids == seg_ids[-1])[:, None], jnp.exp(cumulative[-1][None, :] - cumulative), 0.0
        )
        * step_sizes
    )
    fresh_state = jnp.einsum("sh,shp,sn->hpn", to_end, values, key_vecs, precision=highest)
    new_state = state_in * keep_factor[-1][:, None, None] + fresh_state
    return ((new_state, seg_ids[-1]), inside + carried_out)


def grouped_ssd(
    values, key_vecs, queries, step_sizes, log_decay, seg_ids, d_skip, state_in, last_seg
):
    row_count = seg_ids.shape[0]
    block_count = row_count // GROUP

    def blocked(member):
        return member.reshape((block_count, GROUP) + member.shape[1:])

    inputs = (
        blocked(values),
        blocked(key_vecs),
        blocked(queries),
        blocked(step_sizes),
        blocked(log_decay),
        blocked(seg_ids),
    )
    (final_state, last_out), outputs = lax.scan(
        jax.checkpoint(group_block), (state_in, last_seg), inputs
    )
    outputs = outputs.reshape(row_count, HEADS, HEADDIM) + d_skip[None, :, None] * values
    return (outputs, final_state)


def gated_norm(mixed_out, gate_z, gain_out):
    return rms_scale(mixed_out * jax.nn.silu(gate_z), gain_out)


def chain_combine(earlier, later):
    decay_early, state_early = earlier
    decay_late, state_late = later
    return (decay_early * decay_late, decay_late[:, None, None] * state_early + state_late)


def cross_term(queries, log_decay, state_in, seg_ids, prev_seg):
    cumulative = jnp.cumsum(log_decay, axis=0)
    keep_factor = jnp.where((seg_ids == prev_seg)[:, None], jnp.exp(cumulative), 0.0)
    return jnp.einsum("tn,hpn->thp", queries, state_in, precision=highest) * keep_factor[:, :, None]


def device_decay(log_decay, seg_ids, prev_seg):
    total_log = jnp.sum(log_decay, axis=0)
    return jnp.where(seg_ids[-1] == prev_seg, jnp.exp(total_log), 0.0)


def on_device(
    tokens,
    cotangent,
    segments,
    in_weight,
    out_weight,
    gain_in,
    conv_weight,
    conv_bias,
    dt_bias,
    a_log,
    d_skip,
    gain_out,
):
    tokens_f = tokens[0].astype(jnp.float32)
    cot_low = cotangent[0]
    seg_ids = segments[0]
    row_count = seg_ids.shape[0]
    full_in, full_out = (
        lax.all_gather(in_weight, ("seq", "batch"), axis=0, tiled=True),
        lax.all_gather(out_weight, ("seq", "batch"), axis=0, tiled=True),
    )
    normed, norm_pull = jax.vjp(rms_scale, tokens_f, gain_in)
    normed_low = normed.astype(jnp.bfloat16)
    projected = jnp.dot(normed_low, full_in, preferred_element_type=jnp.float32)
    gate_z = projected[:, :INNER]
    xbc = projected[:, INNER : INNER + CONV]
    dt_raw = projected[:, INNER + CONV :]
    tail_start = row_count - KERNEL + 1
    edge_rows, edge_segs = shifted(
        (xbc[tail_start:], seg_ids[tail_start:].astype(jnp.float32)), "seq", 1
    )
    prev_segs = edge_segs.astype(jnp.int32)
    prev_seg = prev_segs[KERNEL - 2]
    ext_segs = jnp.concatenate([prev_segs, seg_ids])

    def prepare_local(xbc_in, dt_in, edge_in, weight_in, bias_in, shift_in, alog_in):
        return prepare(xbc_in, dt_in, edge_in, ext_segs, weight_in, bias_in, shift_in, alog_in)

    prepared, prepare_pull = jax.vjp(
        prepare_local, xbc, dt_raw, edge_rows, conv_weight, conv_bias, dt_bias, a_log
    )
    values, key_vecs, queries, step_sizes, log_decay = prepared
    zeros_state = jnp.zeros((HEADS, HEADDIM, STATE), jnp.float32)

    def local_ssd(values_in, keys_in, queries_in, sizes_in, logs_in, skip_in):
        return grouped_ssd(
            values_in,
            keys_in,
            queries_in,
            sizes_in,
            logs_in,
            seg_ids,
            skip_in,
            zeros_state,
            seg_ids[0],
        )

    (local_out, local_state), ssd_pull = jax.vjp(
        local_ssd, values, key_vecs, queries, step_sizes, log_decay, d_skip
    )

    def decay_local(logs_in):
        return device_decay(logs_in, seg_ids, prev_seg)

    decay_here, decay_pull = jax.vjp(decay_local, log_decay)
    identity = (jnp.ones((HEADS,), jnp.float32), zeros_state)
    decay_prefix, state_in = prefix((decay_here, local_state), "seq", chain_combine, identity)

    def cross_local(queries_in, logs_in, state_arg):
        return cross_term(queries_in, logs_in, state_arg, seg_ids, prev_seg)

    cross_out, cross_pull = jax.vjp(cross_local, queries, log_decay, state_in)
    mixed_out = (local_out + cross_out).reshape(row_count, INNER)
    gated, gated_pull = jax.vjp(gated_norm, mixed_out, gate_z, gain_out)
    gated_low = gated.astype(jnp.bfloat16)
    result = tokens_f + jnp.dot(gated_low, full_out, preferred_element_type=jnp.float32)
    back_in, back_out = (
        lax.all_gather(in_weight, ("seq", "batch"), axis=0, tiled=True),
        lax.all_gather(out_weight, ("seq", "batch"), axis=0, tiled=True),
    )
    contract_last = (((1,), (1,)), ((), ()))
    contract_first = (((0,), (0,)), ((), ()))
    grad_gated = lax.dot_general(
        cot_low, back_out, contract_last, preferred_element_type=jnp.float32
    )
    grad_mixed, grad_gate, grad_gain_out = gated_pull(grad_gated)
    grad_mixed = grad_mixed.reshape(row_count, HEADS, HEADDIM)
    grad_q_cross, grad_log_cross, grad_state_in = cross_pull(grad_mixed)
    decay_after, grad_exit = prefix_2((decay_here, grad_state_in), "seq", chain_combine, identity)
    grad_decay = jnp.sum(grad_exit * state_in, axis=(1, 2))
    grad_log_dev = decay_pull(grad_decay)[0]
    grad_values, grad_keys, grad_q_local, grad_sizes, grad_log_local, grad_skip = ssd_pull(
        (grad_mixed, grad_exit)
    )
    prep_grads = prepare_pull(
        (
            grad_values,
            grad_keys,
            grad_q_local + grad_q_cross,
            grad_sizes,
            grad_log_local + grad_log_cross + grad_log_dev,
        )
    )
    grad_xbc, grad_dt, grad_edge, grad_conv_w, grad_conv_b, grad_dt_bias, grad_a_log = prep_grads
    grad_next = shifted(grad_edge, "seq", -1)
    grad_xbc = grad_xbc.at[tail_start:].add(grad_next)
    grad_proj = jnp.concatenate([grad_gate, grad_xbc, grad_dt], axis=1).astype(jnp.bfloat16)
    grad_normed = lax.dot_general(
        grad_proj, back_in, contract_last, preferred_element_type=jnp.float32
    )
    grad_tokens_norm, grad_gain_in = norm_pull(grad_normed)
    grad_tokens = (cot_low.astype(jnp.float32) + grad_tokens_norm).astype(jnp.bfloat16)
    grad_in_w = lax.dot_general(
        normed_low, grad_proj, contract_first, preferred_element_type=jnp.float32
    )
    grad_out_w = lax.dot_general(
        gated_low, cot_low, contract_first, preferred_element_type=jnp.float32
    )
    shard_in, shard_out = (
        lax.psum_scatter(grad_in_w, ("seq", "batch"), scatter_dimension=0, tiled=True),
        lax.psum_scatter(grad_out_w, ("seq", "batch"), scatter_dimension=0, tiled=True),
    )
    summed = lax.psum(
        (
            grad_gain_in,
            grad_conv_w,
            grad_conv_b,
            grad_dt_bias,
            grad_a_log,
            grad_skip,
            grad_gain_out,
        ),
        ("seq", "batch"),
    )
    return (
        result.astype(jnp.bfloat16)[None],
        grad_tokens[None],
        shard_in,
        shard_out,
        summed[0],
        summed[1],
        summed[2],
        summed[3],
        summed[4],
        summed[5],
        summed[6],
    )


def solution(mesh):
    in_specs = (
        P("batch", "seq", None),
        P("batch", "seq", None),
        P("batch", "seq"),
        P(("seq", "batch"), None),
        P(("seq", "batch"), None),
        P(),
        P(),
        P(),
        P(),
        P(),
        P(),
        P(),
    )
    out_specs = (
        P("batch", "seq", None),
        P("batch", "seq", None),
        P(("seq", "batch"), None),
        P(("seq", "batch"), None),
        P(),
        P(),
        P(),
        P(),
        P(),
        P(),
        P(),
    )
    return jax.shard_map(
        on_device, mesh=mesh, in_specs=in_specs, out_specs=out_specs, check_vma=False
    )
```

profile of v0, /device:TPU:8, one launch (start us, length us, event | category | flops | bytes accessed | tf_op | source)
XLA Modules:
  0.0 620.5 jit_solution(6955974555531583517)
XLA Ops:
  19.0 59.2 %all-gather.8.cloned.1.call-done = bf16[768,3352]{1,0:T(8,128)(2,1)} async-done(((bf16[24,3352]{1,0:T(8,128)(2,1)}), bf16[768,3352]{1,0:T(8,128)(2,1)}) %all-gather.8.cloned.1.call-update) | async-done | bytes 5148688 | tf_op jit(solution)/shard_map/all_gather | solution.py:188
  78.2 5.0 fusion.136
  85.5 3.9 collective-permute-start
  95.2 8.2 %fusion.94 = (f32[256,1792]{0,1:T(8,128)S(1)}, f32[256,1792]{0,1:T(8,128)}) fusion(f32[256,1792]{0,1:T(8,128)} %slice.181, f32[1792]{0:T(1024)S(1)} %get-tuple-element.810, f32[256]{0:T(256)S(1)} %get-tuple-element.930, f32[3,1792]{0,1:T(8,128)S(1)} %copy.154, f32[1792]{0:T(1024)S(1)} %get-tuple-element.811, f32[256]{0:T(256)S(1)} %get-tuple-element.931, ...), kind=kLoop, calls=%fused_computation.150 | loop fusion | flops 8257536 | bytes 5565440 | tf_op jit(solution)/shard_map/jvp(jit(silu))/mul | solution.py:82
  111.7 67.4 %while.75 = (s32[]{:T(128)}, f32[24,64,128]{2,1,0:T(8,128)S(1)}, s32[]{:T(128)}, f32[2,128,24,64]{1,0,3,2:T(2,128)}, f32[2,24,64,128]{3,2,1,0:T(8,128)}, /*index...) while((s32[]{:T(128)}, f32[24,64,128]{2,1,0:T(8,128)S(1)}, ...), condition=%wide.region_3.4_spmd.clone, body=%wide.region_1.3_spmd.clone.sunk | while | flops 935126272 | bytes 10139836 | solution.py:141
  123.4 19.0 %dynamic_update_slice.88 = f32[2,128,24,64]{1,0,3,2:T(2,128)} dynamic-update-slice(f32[2,128,24,64]{1,0,3,2:T(2,128)} %get-tuple-element.1248, f32[1,128,24,64]{1,0,3,2:T(1,128)S(1)} %bitcast.392, s32[]{:T(128)S(6)} %copy.299, s32[]{:T(128)} %constant.232.clone.1..sunk.3, s32[]{:T(128)} %constant.232.clone.1..sunk.3, s32[]{:T(128)} %constant.232.clone.1..sunk.3) | dynamic-update-slice | bytes 1572868 | tf_op jit(solution)/shard_map/jvp()/while/body/jit(dynamic_update_index_in_dim)/dynamic_update_slice | solution.py:141
  157.1 19.0 %dynamic_update_slice.88 = f32[2,128,24,64]{1,0,3,2:T(2,128)} dynamic-update-slice(f32[2,128,24,64]{1,0,3,2:T(2,128)} %get-tuple-element.1248, f32[1,128,24,64]{1,0,3,2:T(1,128)S(1)} %bitcast.392, s32[]{:T(128)S(6)} %copy.299, s32[]{:T(128)} %constant.232.clone.1..sunk.3, s32[]{:T(128)} %constant.232.clone.1..sunk.3, s32[]{:T(128)} %constant.232.clone.1..sunk.3) | dynamic-update-slice | bytes 1572868 | tf_op jit(solution)/shard_map/jvp()/while/body/jit(dynamic_update_index_in_dim)/dynamic_update_slice | solution.py:141
  183.6 9.2 %all-reduce.13 = bf16[96]{0:T(256)(128)(2,1)S(1)} all-reduce(bf16[96]{0:T(256)(128)(2,1)S(1)} %dynamic-update-slice.3), channel_id=2, replica_groups=mesh['seq'=4,'batch'=8] {'seq'}, use_global_device_ids=true, to_apply=%add.13 | all-reduce | flops 96 | bytes 384
  197.0 12.5 %all-gather.12.cloned.1.call-done = bf16[96,64,128]{2,1,0:T(8,128)(2,1)} async-done(((bf16[24,64,128]{2,1,0:T(8,128)(2,1)}), bf16[96,64,128]{2,1,0:T(8,128)(2,1)}) %all-gather.12.cloned.1.call-update) | async-done | bytes 1572880 | tf_op jit(solution)/shard_map/all_gather | solution.py:28
  218.7 50.2 %all-gather.10.cloned.1.call-done = bf16[1536,768]{1,0:T(8,128)(2,1)} async-done(((bf16[48,768]{1,0:T(8,128)(2,1)}), bf16[1536,768]{1,0:T(8,128)(2,1)}) %all-gather.10.cloned.1.call-update) | async-done | bytes 2359312 | tf_op jit(solution)/shard_map/all_gather | solution.py:189
  272.9 4.2 multiply_reduce_fusion.7
  289.0 4.3 fusion.128
  293.4 16.9 %all-gather.14.cloned.1.call-done = bf16[96,64,128]{2,1,0:T(8,128)(2,1)} async-done(((bf16[24,64,128]{2,1,0:T(8,128)(2,1)}), bf16[96,64,128]{2,1,0:T(8,128)(2,1)}) %all-gather.14.cloned.1.call-update) | async-done | bytes 1572880 | tf_op jit(solution)/shard_map/all_gather | solution.py:50
  318.9 112.7 %while.74 = (s32[]{:T(128)}, f32[24,64,128]{2,1,0:T(8,128)S(1)}, f32[2,128,24,64]{1,0,3,2:T(2,128)}, f32[2,128,128]{2,1,0:T(8,128)}, f32[2,128,128]{2,1,0:T(8,12...) while((s32[]{:T(128)}, f32[24,64,128]{2,1,0:T(8,128)S(1)}, ...), condition=%wide.region_23.24_spmd, body=%wide.region_13.23_spmd.sunk | while | flops 2202327296 | bytes 47834156 | solution.py:141
  333.3 4.6 fusion.239
  356.2 19.0 %dynamic_update_slice.86 = f32[2,128,24,64]{1,0,3,2:T(2,128)} dynamic-update-slice(f32[2,128,24,64]{1,0,3,2:T(2,128)} %get-tuple-element.1347, f32[1,128,24,64]{1,0,3,2:T(1,128)} %bitcast.396, s32[]{:T(128)S(6)} %sub.287, s32[]{:T(128)} %constant.232.clone.1..sunk.2, s32[]{:T(128)} %constant.232.clone.1..sunk.2, s32[]{:T(128)} %constant.232.clone.1..sunk.2) | dynamic-update-slice | bytes 1572868 | tf_op jit(solution)/shard_map/transpose(jvp())/while/body/jit(dynamic_update_index_in_dim)/dynamic_update_slice | solution.py:141
  389.3 4.6 fusion.239
  412.2 19.0 %dynamic_update_slice.86 = f32[2,128,24,64]{1,0,3,2:T(2,128)} dynamic-update-slice(f32[2,128,24,64]{1,0,3,2:T(2,128)} %get-tuple-element.1347, f32[1,128,24,64]{1,0,3,2:T(1,128)} %bitcast.396, s32[]{:T(128)S(6)} %sub.287, s32[]{:T(128)} %constant.232.clone.1..sunk.2, s32[]{:T(128)} %constant.232.clone.1..sunk.2, s32[]{:T(128)} %constant.232.clone.1..sunk.2) | dynamic-update-slice | bytes 1572868 | tf_op jit(solution)/shard_map/transpose(jvp())/while/body/jit(dynamic_update_index_in_dim)/dynamic_update_slice | solution.py:141
  441.7 5.2 multiply_reduce_fusion.4
  460.1 4.4 scatter-add.4
  464.6 6.9 %fusion.125 = f32[768,3352]{1,0:T(8,128)} fusion(bf16[256,24]{0,1:T(8,128)(2,1)S(1)} %get-tuple-element.902, bf16[256,1792]{0,1:T(8,128)(2,1)S(1)} %scatter-add.4, bf16[256,1536]{0,1:T(8,128)(2,1)} %get-tuple-element.921, bf16[1,256,768]{2,1,0:T(8,128)(2,1)S(1)} %copy-done.22, f32[768]{0:T(1024)S(1)} %copy-done.45, f32[256]{0:T(256)S(1)} %copy-done.62), kind=kOutput, calls=%fused_computation.200 | convolution fusion | flops 1323995136 | bytes 12410880 | tf_op jit(solution)/shard_map/dot_general | solution.py:282
  476.6 4.6 fusion.117
  481.2 40.9 %all-reduce.15 = (f32[768]{0:T(1024)}, f32[4,1792]{1,0:T(4,128)}, f32[1792]{0:T(1024)}, f32[24]{0:T(128)}, f32[24]{0:T(128)}, /*index=5*/f32[24]{0:T(128)}, f32[1536]{0:T(1024)}) all-reduce(f32[768]{0:T(1024)S(1)} %get-tuple-element.806, f32[4,1792]{1,0:T(4,128)S(1)} %pad_add_fusion.1, ...), channel_id=1, replica_groups=mesh['seq'=4,'batch'=8] {'seq','batch'}, use_global_device_ids=true, to_apply=%region_32.33 | all-reduce | flops 11336 | bytes 90688 | tf_op jit(solution)/shard_map/psum | solution.py:292
  523.2 90.3 %reduce-scatter.7.cloned.1.call-done = f32[24,3352]{1,0:T(8,128)} async-done(((f32[768,3352]{1,0:T(8,128)}), f32[24,3352]{1,0:T(8,128)}) %reduce-scatter.7.cloned.1.call-update) | async-done | bytes 321808
  (455 shorter events, 194.3 us)
Async XLA Ops:
  7.2 71.0 %all-gather.8.cloned.1.call-start = ((), (), s32[]{:S(2)}) async-start(), calls=%async_computation.2 | async-start | bytes 5474304 | tf_op jit(solution)/shard_map/all_gather | solution.py:188
  7.9 201.6 %all-gather.12.cloned.1.call-start = ((), (), s32[]{:S(2)}) async-start(), calls=%async_computation.5 | async-start | bytes 1966080 | tf_op jit(solution)/shard_map/all_gather | solution.py:28
  8.7 7.5 %collective-permute-start.1 = (f32[3]{0:T(128)S(1)}, f32[3]{0:T(128)S(1)}, u32[]{:S(2)}, u32[]{:S(2)}) collective-permute-start(f32[3]{0:T(128)S(1)} %convert_bitcast_fusion), channel_id=1, source_target_pairs={{0,8},{8,16},{16,24},{1,9},{9,17},{17,25},{2,10},{10,18},{18,26},{... | collective-permute-start | bytes 44 | tf_op jit(solution)/shard_map/ppermute | solution.py:22
  12.8 76.6 %copy-start.82 = (f32[24]{0:T(128)}, f32[24]{0:T(128)S(1)}, u32[]{:S(2)}) copy-start(f32[24]{0:T(128)S(1)} %exp.98) | copy-start | bytes 292
  15.0 80.1 %copy-start.53 = (f32[1792]{0:T(1024)}, f32[1792]{0:T(1024)S(1)}, u32[]{:S(2)}) copy-start(f32[1792]{0:T(1024)S(1)} %get-tuple-element.808) | copy-start | bytes 21508
  15.0 80.1 %copy-start.55 = (f32[1792]{0:T(1024)}, f32[1792]{0:T(1024)S(1)}, u32[]{:S(2)}) copy-start(f32[1792]{0:T(1024)S(1)} %get-tuple-element.809) | copy-start | bytes 21508
  15.0 80.1 %copy-start.57 = (f32[1792]{0:T(1024)}, f32[1792]{0:T(1024)S(1)}, u32[]{:S(2)}) copy-start(f32[1792]{0:T(1024)S(1)} %get-tuple-element.810) | copy-start | bytes 21508
  15.0 80.1 %copy-start.59 = (f32[1792]{0:T(1024)}, f32[1792]{0:T(1024)S(1)}, u32[]{:S(2)}) copy-start(f32[1792]{0:T(1024)S(1)} %get-tuple-element.811) | copy-start | bytes 21508
  16.2 66.9 %copy-start.61 = (f32[256]{0:T(256)}, f32[256]{0:T(256)S(1)}, u32[]{:S(2)}) copy-start(f32[256]{0:T(256)S(1)} %fusion.145) | copy-start | bytes 3076
  19.0 76.1 %copy-start.68 = (f32[256]{0:T(256)}, f32[256]{0:T(256)S(1)}, u32[]{:S(2)}) copy-start(f32[256]{0:T(256)S(1)} %get-tuple-element.929) | copy-start | bytes 3076
  19.0 76.1 %copy-start.70 = (f32[256]{0:T(256)}, f32[256]{0:T(256)S(1)}, u32[]{:S(2)}) copy-start(f32[256]{0:T(256)S(1)} %get-tuple-element.930) | copy-start | bytes 3076
  19.0 76.2 %copy-start.72 = (f32[256]{0:T(256)}, f32[256]{0:T(256)S(1)}, u32[]{:S(2)}) copy-start(f32[256]{0:T(256)S(1)} %get-tuple-element.931) | copy-start | bytes 3076
  19.0 174.6 %copy-start.77 = (pred[256]{0:T(512)(128)(4,1)}, pred[256]{0:T(512)(128)(4,1)S(1)}, u32[]{:S(2)}) copy-start(pred[256]{0:T(512)(128)(4,1)S(1)} %get-tuple-element.932) | copy-start | bytes 772
  85.5 9.3 %collective-permute-start = (f32[3,1792]{1,0:T(4,128)S(1)}, f32[3,1792]{1,0:T(4,128)S(1)}, u32[]{:S(2)}, u32[]{:S(2)}) collective-permute-start(f32[3,1792]{1,0:T(4,128)S(1)} %copy.153), channel_id=1, source_target_pairs={{0,8},{8,16},{16,24},{1,9},{9,17},{17,25},{2,10},{10,18},{18,26},{... | collective-permute-start | bytes 64520 | tf_op jit(solution)/shard_map/ppermute | solution.py:22
  90.3 93.0 %copy-start.85 = (f32[24]{0:T(128)}, f32[24]{0:T(128)S(1)}, u32[]{:S(2)}) copy-start(f32[24]{0:T(128)S(1)} %get-tuple-element.908) | copy-start | bytes 292
  179.9 89.0 %all-gather.10.cloned.1.call-start = ((), (), s32[]{:S(2)}) async-start(), calls=%async_computation.3 | async-start | bytes 2433024 | tf_op jit(solution)/shard_map/all_gather | solution.py:189
  180.7 129.7 %all-gather.14.cloned.1.call-start = ((), (), s32[]{:S(2)}) async-start(), calls=%async_computation.6 | async-start | bytes 1966080 | tf_op jit(solution)/shard_map/all_gather | solution.py:50
  215.0 54.0 %copy-start.28 = (bf16[1,256,768]{2,1,0:T(8,128)(2,1)S(1)}, bf16[1,256,768]{2,1,0:T(8,128)(2,1)}, u32[]{:S(2)}) copy-start(bf16[1,256,768]{2,1,0:T(8,128)(2,1)} %param.23) | copy-start | bytes 1179652
  215.0 53.9 %copy-start.50 = (f32[1536]{0:T(1024)S(1)}, f32[1536]{0:T(1024)}, u32[]{:S(2)}) copy-start(f32[1536]{0:T(1024)} %param.33) | copy-start | bytes 18436
  218.7 70.3 %copy-start.63 = (f32[256]{0:T(256)}, f32[256]{0:T(256)S(1)}, u32[]{:S(2)}) copy-start(f32[256]{0:T(256)S(1)} %fusion.146) | copy-start | bytes 3076
  279.3 243.9 %reduce-scatter.5.cloned.1.call-start = ((), (), s32[]{:S(2)}) async-start(), calls=%async_computation.4 | async-start | bytes 4866048 | tf_op jit(solution)/shard_map/reduce_scatter | solution.py:290
  293.4 320.1 %reduce-scatter.7.cloned.1.call-start = ((), (), s32[]{:S(2)}) async-start(), calls=%async_computation.7 | async-start | bytes 10948608
  452.6 5.9 collective-permute-start.2
  476.6 45.6 %copy-start.29 = (bf16[1,256,768]{2,1,0:T(8,128)(2,1)S(1)}, bf16[1,256,768]{2,1,0:T(8,128)(2,1)}, u32[]{:S(2)}) copy-start(bf16[1,256,768]{2,1,0:T(8,128)(2,1)} %param.23) | copy-start | bytes 1179652
  (97 other events, 492.4 us)
Sparse Core Ops, SparseCore 0:
  10.9 67.2 all-gather.7
  180.1 29.4 all-gather.11
  212.6 56.3 all-gather.9
  279.4 30.9 all-gather.13
  316.3 106.8 reduce-scatter.4
  471.7 141.7 reduce-scatter.6
where the time goes:
time: 633 us; the launch traced here: 620 us
  waiting for transfers between devices  232 us (37%)
  local copies, waits for them, and re-layouts  157 us (25%)
  matrix products  83.1 us (13%)
  other arithmetic  71.3 us (11%)
  blocking collectives  50.1 us (8%)
  between operations  17.4 us (3%)
  starting transfers between devices  8.9 us (1%)
    unnamed x7, waiting for transfers between devices  91.7 us
    dynamic_update_slice x6, local copies, waits for them, and re-layouts, grouped_ssd(): lax.scan(jax.checkpoint(group_block), (state_in, last_seg), inputs)  77.5 us
    all_gather x1, waiting for transfers between devices, on_device(): lax.all_gather(in_weight, ('seq', 'batch'), axis=0, tiled=True)  59.2 us
    all_gather x1, waiting for transfers between devices, on_device(): lax.all_gather(out_weight, ('seq', 'batch'), axis=0, tiled=True)  50.2 us
    psum x1, blocking collectives, on_device(): lax.psum((grad_gain_in, grad_conv_w, grad_conv_b, grad_dt_bias, grad_a_lo...  40.9 us
    dot_general x6, matrix products, group_block(): inside = jnp.einsum('tsh,shp->thp', weights, values, precision=highest)  21.4 us
    all_gather x1, waiting for transfers between devices, prefix_2(): lax.all_gather(a.astype(kind), axis)  16.9 us
  transfers between devices with their start and end apart: 9, of which 6 were waited for; matrix products, arithmetic and copies ran while one was open for 33% of the time, Pallas kernels for 0%

commit v1 on v0

--- a/solution.py
+++ b/solution.py
@@ -1,6 +1,10 @@
+import functools
+
 import jax
 import jax.numpy as jnp
 from jax import lax
+from jax.experimental import pallas as pl
+from jax.experimental.pallas import tpu as pltpu
 from jax.sharding import PartitionSpec as P
 
 HEADS = 24
@@ -10,10 +14,790 @@
 GROUP = 128
 INNER = 1536
 CONV = 1792
+WIDTH = 768
+LANES = 128
+LEAD = 8
 
 
 highest = lax.Precision.HIGHEST
 norm_eps = 1e-05
+f32 = jnp.float32
+bf16 = jnp.bfloat16
+contract_last = (((1,), (1,)), ((), ()))
+contract_first = (((0,), (0,)), ((), ()))
+
+
+def mm(a, b):
+    return jnp.dot(a.astype(bf16), b.astype(bf16), preferred_element_type=f32)
+
+
+def mm_nt(a, b):
+    return lax.dot_general(
+        a.astype(bf16), b.astype(bf16), contract_last, preferred_element_type=f32
+    )
+
+
+def mm_tn(a, b):
+    return lax.dot_general(
+        a.astype(bf16), b.astype(bf16), contract_first, preferred_element_type=f32
+    )
+
+
+def mm_exact(a, b):
+    return jnp.dot(a, b, precision=highest, preferred_element_type=f32)
+
+
+def iota(shape, dim):
+    return lax.broadcasted_iota(jnp.int32, shape, dim)
+
+
+def aligned(value, unit):
+    return pl.multiple_of(value, unit)
+
+
+def wide(columns, count):
+    rows = columns.shape[0]
+    low = iota((rows, LANES), 1) < HEADDIM
+    parts = []
+    for pair in range(count // 2):
+        left = jnp.broadcast_to(columns[:, 2 * pair : 2 * pair + 1], (rows, LANES))
+        right = jnp.broadcast_to(columns[:, 2 * pair + 1 : 2 * pair + 2], (rows, LANES))
+        parts.append(jnp.where(low, left, right))
+    return jnp.concatenate(parts, axis=1)
+
+
+def softplus(value):
+    return jnp.maximum(value, 0.0) + jnp.log1p(jnp.exp(-jnp.abs(value)))
+
+
+def sigmoid(value):
+    return 1.0 / (1.0 + jnp.exp(-value))
+
+
+class Plan:
+    def __init__(self, mesh_seq, mesh_batch, rows, in_rows, out_rows):
+        self.seq = mesh_seq
+        self.batch = mesh_batch
+        self.line = mesh_batch // 2
+        self.rows = rows
+        self.total = rows * mesh_seq
+        self.blocks = self.total // GROUP
+        self.heads = HEADS // mesh_seq
+        self.chan = self.heads * HEADDIM
+        self.mixed = self.chan + 2 * STATE
+        self.cols = self.mixed + LANES
+        self.in_rows = in_rows
+        self.out_rows = out_rows
+
+
+def place():
+    s = lax.axis_index("seq")
+    b = lax.axis_index("batch")
+    return s, lax.shift_right_logical(b, 1), lax.bitwise_and(b, 1)
+
+
+def in_place(plan, ids, line_xor, core_xor, seq_xor):
+    s, z, c = ids
+    owner = (s ^ seq_xor) * plan.batch + (z ^ line_xor) * 2 + (c ^ core_xor)
+    return aligned(owner * plan.in_rows, 8)
+
+
+def block_values(plan, b, x_ref, segc_ref, segr_ref, dt_ref, convw, convb, heads_ref):
+    base = aligned(b * GROUP, GROUP)
+    win = x_ref[pl.ds(base, GROUP + LEAD), :]
+    segw = segc_ref[pl.ds(base, GROUP + LEAD), :]
+    seg = segw[LEAD:]
+    prev = segw[LEAD - 1 : LEAD]
+    repeat = plan.mixed // LANES
+    pre = jnp.broadcast_to(convb, (GROUP, plan.mixed))
+    shifts = []
+    for k in range(KERNEL):
+        start = LEAD - KERNEL + 1 + k
+        part = win[start : start + GROUP]
+        if k < KERNEL - 1:
+            same = (segw[start : start + GROUP] == seg).astype(f32)
+            part = part * jnp.concatenate([same] * repeat, axis=1)
+        shifts.append(part)
+        pre = pre + convw[k : k + 1] * part
+    sig = sigmoid(pre)
+    mixed = pre * sig
+    values = mixed[:, : plan.chan]
+    keys = mixed[:, plan.chan : plan.chan + STATE]
+    queries = mixed[:, plan.chan + STATE :]
+    dt_in = dt_ref[pl.ds(base, GROUP), :] + heads_ref[0:1, :LANES]
+    steps = softplus(dt_in)
+    decay = -steps * jnp.exp(heads_ref[1:2, :LANES])
+    row = iota((GROUP, GROUP), 0)
+    col = iota((GROUP, GROUP), 1)
+    tri = (row >= col).astype(f32)
+    cum = mm_exact(tri, decay)
+    cum_t = cum.T
+    steps_t = steps.T
+    segr = segr_ref[pl.ds(b, 1), :]
+    allowed = (seg == segr) & (row >= col)
+    scores = mm_nt(queries, keys)
+    keep = jnp.where(seg == prev, jnp.exp(cum), 0.0)
+    last = cum[GROUP - 1 :]
+    to_last = jnp.where(seg == seg[GROUP - 1 :], jnp.exp(last - cum), 0.0)
+    return dict(
+        base=base, seg=seg, shifts=shifts, pre=pre, sig=sig, values=values, keys=keys,
+        queries=queries, dt_in=dt_in, steps=steps, decay=decay, tri=tri, cum=cum, cum_t=cum_t,
+        steps_t=steps_t, allowed=allowed, scores=scores, keep=keep, to_last=to_last,
+    )
+
+
+def head_decay(v, h):
+    gap = v["cum"][:, h : h + 1] - v["cum_t"][h : h + 1, :]
+    return jnp.where(v["allowed"], jnp.exp(jnp.minimum(gap, 0.0)), 0.0)
+
+
+def split_pair(pair):
+    low = iota(pair.shape, 1) < HEADDIM
+    return jnp.concatenate([jnp.where(low, pair, 0.0), jnp.where(low, 0.0, pair)], axis=0)
+
+
+def fill_segments(plan, s, pieces, segc_ref, segr_ref):
+    per = plan.rows // GROUP
+    segc_ref[...] = jnp.zeros_like(segc_ref)
+    segr_ref[...] = jnp.zeros_like(segr_ref)
+    for m in range(plan.seq):
+        line = pieces[m][plan.in_rows : plan.in_rows + 1, : plan.rows].astype(f32)
+        for j in range(per):
+            b = (s ^ m) * per + j
+            segr_ref[pl.ds(b, 1), :] = line[:, j * GROUP : (j + 1) * GROUP]
+    every = segr_ref[...]
+    turned = jnp.concatenate(
+        [every, jnp.zeros((LANES - every.shape[0], GROUP), f32)], axis=0
+    ).T
+    for b in range(plan.blocks):
+        segc_ref[LEAD + b * GROUP : LEAD + (b + 1) * GROUP, :] = jnp.broadcast_to(
+            turned[:, b : b + 1], (GROUP, LANES)
+        )
+
+
+def forward_kernel(plan, *refs):
+    n = plan.seq
+    toks, refs = refs[:n], refs[n:]
+    pieces, refs = refs[:n], refs[n:]
+    weights, refs = refs[: 2 * plan.line], refs[2 * plan.line :]
+    gain_ref, convw_ref, convb_ref, heads_ref = refs[:4]
+    normed_ref, w_ref, x_ref, dt_ref, y_ref, states_ref, segc_ref, segr_ref = refs[4:12]
+    wf_ref, state_ref = refs[12:]
+    ids = place()
+    s = ids[0]
+    fill_segments(plan, s, pieces, segc_ref, segr_ref)
+    for core_xor in range(2):
+        for line_xor in range(plan.line):
+            piece = weights[core_xor * plan.line + line_xor]
+            for m in range(n):
+                dest = pl.ds(in_place(plan, ids, line_xor, core_xor, m), plan.in_rows)
+                wf_ref[dest, :] = piece[m * plan.in_rows : (m + 1) * plan.in_rows, :].astype(f32)
+    w_ref[...] = wf_ref[...].astype(bf16)
+    x_ref[0:LEAD, :] = jnp.zeros((LEAD, plan.mixed), f32)
+    for m in range(n):
+        tok = toks[m][...].astype(f32)
+        scale = lax.rsqrt(jnp.mean(tok * tok, axis=1, keepdims=True) + norm_eps)
+        low = (tok * scale * gain_ref[...]).astype(bf16)
+        start = (s ^ m) * plan.rows
+        normed_ref[pl.ds(aligned(start, plan.rows), plan.rows), :] = low
+        out = jnp.dot(low, w_ref[...], preferred_element_type=f32)
+        x_ref[pl.ds(aligned(start + LEAD, 8), plan.rows), :] = out[:, : plan.mixed]
+        dt_ref[pl.ds(aligned(start, plan.rows), plan.rows), :] = out[:, plan.mixed :]
+    state_ref[...] = jnp.zeros_like(state_ref)
+    convw = convw_ref[...]
+    convb = convb_ref[...]
+
+    def step(b, carry):
+        v = block_values(plan, b, x_ref, segc_ref, segr_ref, dt_ref, convw, convb, heads_ref)
+        state = state_ref[...]
+        states_ref[b] = state
+        parts = []
+        for pair in range(plan.heads // 2):
+            lanes = slice(pair * LANES, (pair + 1) * LANES)
+            weights_pair = []
+            for h in (2 * pair, 2 * pair + 1):
+                decay = head_decay(v, h)
+                weights_pair.append(decay * v["scores"] * v["steps_t"][h : h + 1, :])
+            parts.append(
+                mm(jnp.concatenate(weights_pair, axis=1), split_pair(v["values"][:, lanes]))
+            )
+        inside = jnp.concatenate(parts, axis=1)
+        keep = wide(v["keep"], plan.heads)
+        carried = mm(v["queries"], state) * keep
+        y_ref[pl.ds(v["base"], GROUP), :] = inside + carried + heads_ref[2:3, :] * v["values"]
+        to_end = wide(v["to_last"] * v["steps"], plan.heads)
+        state_ref[...] = state * keep[GROUP - 1 :] + mm_tn(v["keys"], v["values"] * to_end)
+        return carry
+
+    lax.fori_loop(0, plan.blocks, step, 0)
+
+
+def gate_kernel(plan, *refs):
+    n = plan.seq
+    normed_ref, y_ref = refs[:2]
+    weights = refs[2 : 2 + 2 * plan.line]
+    cots = refs[2 + 2 * plan.line : 2 + 2 * plan.line + n]
+    gain_ref = refs[2 + 2 * plan.line + n]
+    outs = refs[3 + 2 * plan.line + n :]
+    wz_ref, z_ref, du_ref, stats_ref = outs[:4]
+    parts = outs[4 : 4 + n]
+    wf_ref, wo_ref = outs[4 + n :]
+    ids = place()
+    s, z, c = ids
+    half = plan.in_rows * n // 2
+    for core_xor in range(2):
+        for line_xor in range(plan.line):
+            piece = weights[core_xor * plan.line + line_xor]
+            for m in range(n):
+                dest = pl.ds(in_place(plan, ids, line_xor, core_xor, m), plan.in_rows)
+                top = (m // 2) * plan.in_rows
+                left = (m % 2) * plan.chan
+                wf_ref[dest, :] = piece[
+                    top : top + plan.in_rows, left : left + plan.chan
+                ].astype(f32)
+            start = ((z ^ line_xor) * 2 + (c ^ core_xor)) * plan.out_rows
+            wo_ref[pl.ds(aligned(start, 16), plan.out_rows), :] = piece[
+                half : half + plan.out_rows, :
+            ]
+    wz_ref[...] = wf_ref[...].astype(bf16)
+    gain = gain_ref[...]
+    lane = iota((plan.rows, LANES), 1)
+    square = jnp.zeros((GROUP, LANES), f32)
+    lane = iota((GROUP, LANES), 1)
+    per = plan.rows // GROUP
+    for m in range(n):
+        start = aligned((s ^ m) * plan.rows, plan.rows)
+        gate = jnp.dot(
+            normed_ref[pl.ds(start, plan.rows), :], wz_ref[...], preferred_element_type=f32
+        )
+        z_ref[pl.ds(start, plan.rows), :] = gate
+        gated = y_ref[pl.ds(start, plan.rows), :] * gate * sigmoid(gate)
+        scaled = gated * gain
+        parts[m][...] = mm(scaled, wo_ref[...]).astype(parts[m].dtype)
+        du = mm_nt(cots[m][...], wo_ref[...])
+        du_ref[pl.ds(start, plan.rows), :] = du
+        norm = jnp.sum(gated * gated, axis=1, keepdims=True)
+        dots = jnp.sum(du * scaled, axis=1, keepdims=True)
+        for j in range(per):
+            b = (s ^ m) * per + j
+            rows = slice(j * GROUP, (j + 1) * GROUP)
+            square = square + jnp.where(lane == b, norm[rows], 0.0)
+            square = square + jnp.where(lane == b + plan.blocks, dots[rows], 0.0)
+    stats_ref[...] = square.T[: 2 * plan.blocks]
+
+
+def emit_rows(plan, ids, source_ref, put):
+    for core_xor in range(2):
+        for line_xor in range(plan.line):
+            for m in range(plan.seq):
+                rows = source_ref[
+                    pl.ds(in_place(plan, ids, line_xor, core_xor, m), plan.in_rows), :
+                ]
+                put(core_xor, line_xor, m, rows)
+
+
+def regate_kernel(plan, *refs):
+    n = plan.seq
+    stats = refs[:n]
+    normed_ref, y_ref, z_ref, du_ref = refs[n : n + 4]
+    cots = refs[n + 4 : 2 * n + 4]
+    gain_ref = refs[2 * n + 4]
+    dy_ref, dz_ref, scale_ref, gain_out_ref, keep_ref, send_ref = refs[2 * n + 5 : 2 * n + 11]
+    gated_ref, gz_ref, go_ref = refs[2 * n + 11 :]
+    ids = place()
+    s, z, c = ids
+    total = stats[0][...]
+    for m in range(1, n):
+        total = total + stats[m][...]
+    turned = jnp.concatenate(
+        [total, jnp.zeros((LANES - total.shape[0], GROUP), f32)], axis=0
+    ).T
+    gain = gain_ref[...]
+    sums = jnp.zeros((1, plan.chan), f32)
+    for b in range(plan.blocks):
+        rows = slice(b * GROUP, (b + 1) * GROUP)
+        r = lax.rsqrt(turned[:, b : b + 1] / INNER + norm_eps)
+        dot = turned[:, plan.blocks + b : plan.blocks + b + 1] / INNER
+        scale_ref[rows, :] = jnp.broadcast_to(r, (GROUP, LANES))
+        gate = z_ref[rows, :]
+        sig = sigmoid(gate)
+        silu = gate * sig
+        y = y_ref[rows, :]
+        gated = y * silu
+        du = du_ref[rows, :]
+        normal = gated * r
+        grad_pre = r * (du * gain) - normal * (r * r * dot)
+        dy_ref[rows, :] = grad_pre * silu
+        dz_ref[rows, :] = (grad_pre * y * sig * (1.0 + gate * (1.0 - sig))).astype(bf16)
+        gated_ref[rows, :] = (normal * gain).astype(bf16)
+        sums = sums + jnp.sum(du * normal, axis=0, keepdims=True)
+    gain_out_ref[...] = sums
+    gz_ref[...] = mm_tn(normed_ref[...], dz_ref[...])
+    out = None
+    for m in range(n):
+        start = aligned((s ^ m) * plan.rows, plan.rows)
+        one = mm_tn(gated_ref[pl.ds(start, plan.rows), :], cots[m][...])
+        out = one if out is None else out + one
+    go_ref[...] = out
+    half = plan.in_rows * n // 2
+    both = (keep_ref, send_ref)
+
+    def put(core_xor, line_xor, m, rows):
+        top = (m // 2) * plan.in_rows
+        left = (m % 2) * plan.chan
+        both[core_xor][line_xor, top : top + plan.in_rows, left : left + plan.chan] = rows.astype(
+            bf16
+        )
+
+    emit_rows(plan, ids, gz_ref, put)
+    for core_xor in range(2):
+        for line_xor in range(plan.line):
+            start = ((z ^ line_xor) * 2 + (c ^ core_xor)) * plan.out_rows
+            both[core_xor][line_xor, half : half + plan.out_rows, :] = go_ref[
+                pl.ds(aligned(start, 16), plan.out_rows), :
+            ].astype(bf16)
+
+
+def backward_kernel(plan, *refs):
+    n = plan.seq
+    toks = refs[:n]
+    normed_ref, w_ref, wz_ref, x_ref, dt_ref, states_ref, segc_ref, segr_ref = refs[n : n + 8]
+    dy_ref, dz_ref, gain_out_ref, convw_ref, convb_ref, heads_ref = refs[n + 8 : n + 14]
+    outs = refs[n + 14 :]
+    grads, outs = outs[:n], outs[n:]
+    keep_ref, send_ref, small_ref = outs[:3]
+    gp_ref, gw_ref, gn_ref, adj_ref, edge_ref, acc_ref, head_ref = outs[3:]
+    ids = place()
+    s = ids[0]
+    convw = convw_ref[...]
+    convb = convb_ref[...]
+    adj_ref[...] = jnp.zeros_like(adj_ref)
+    edge_ref[...] = jnp.zeros_like(edge_ref)
+    acc_ref[...] = jnp.zeros_like(acc_ref)
+    head_ref[...] = jnp.zeros_like(head_ref)
+    repeat = plan.mixed // LANES
+    pick = (iota((plan.chan, LANES), 0) // HEADDIM == iota((plan.chan, LANES), 1)).astype(f32)
+    lane = iota((GROUP, LANES), 1)
+
+    def step(turn, carry):
+        b = plan.blocks - 1 - turn
+        v = block_values(plan, b, x_ref, segc_ref, segr_ref, dt_ref, convw, convb, heads_ref)
+        base = v["base"]
+        state = states_ref[b]
+        adj = adj_ref[...]
+        dy = dy_ref[pl.ds(base, GROUP), :]
+        values = v["values"]
+        keep = wide(v["keep"], plan.heads)
+        to_end = wide(v["to_last"] * v["steps"], plan.heads)
+        kept = dy * keep
+        dq = mm_nt(kept, state)
+        cross = kept * mm(v["queries"], state)
+        fed = mm(v["keys"], adj)
+        dk = mm_nt(values * to_end, adj)
+        adj_ref[...] = adj * keep[GROUP - 1 :] + mm_tn(v["queries"], kept)
+        ended = jnp.sum(state * adj, axis=0, keepdims=True)
+        pushed = fed * values
+        skipped = jnp.sum(dy * values, axis=0, keepdims=True)
+        few = jnp.concatenate([ended, skipped, jnp.zeros((6, plan.chan), f32)], axis=0)
+        sums = mm_exact(jnp.concatenate([cross, pushed, few], axis=0), pick)
+        cross_h = sums[:GROUP]
+        pushed_h = sums[GROUP : 2 * GROUP]
+        ended_h = sums[2 * GROUP : 2 * GROUP + 1]
+        skipped_h = sums[2 * GROUP + 1 : 2 * GROUP + 2]
+        grad_steps = pushed_h * v["to_last"]
+        pulled = grad_steps * v["steps"]
+        dcum = cross_h - pulled
+        at_end = jnp.sum(pulled, axis=0, keepdims=True) + v["keep"][GROUP - 1 :] * ended_h
+        dscores = jnp.zeros((GROUP, GROUP), f32)
+        columns = []
+        dvs = []
+        for pair in range(plan.heads // 2):
+            lanes = slice(pair * LANES, (pair + 1) * LANES)
+            dy_pair = split_pair(dy[:, lanes])
+            products = mm_nt(dy_pair, values[:, lanes])
+            stacked = []
+            for j, h in enumerate((2 * pair, 2 * pair + 1)):
+                decay = head_decay(v, h)
+                steps_row = v["steps_t"][h : h + 1, :]
+                weighted = decay * products[j * GROUP : (j + 1) * GROUP]
+                direct = weighted * v["scores"]
+                dscores = dscores + weighted * steps_row
+                rowsum = jnp.sum(direct * steps_row, axis=1, keepdims=True)
+                dcum = dcum + jnp.where(lane == h, rowsum, 0.0)
+                columns.append(jnp.sum(direct, axis=0, keepdims=True))
+                stacked.append(decay * v["scores"] * steps_row)
+            dvs.append(mm_tn(jnp.concatenate(stacked, axis=0), dy_pair))
+        dv = jnp.concatenate(dvs, axis=1) + fed * to_end + heads_ref[2:3, :] * dy
+        columns.append(jnp.zeros((LANES - plan.heads, GROUP), f32))
+        down = jnp.concatenate(columns, axis=0).T
+        grad_steps = grad_steps + down
+        dcum = dcum - down * v["steps"]
+        row = iota((GROUP, LANES), 0)
+        dcum = dcum + jnp.where(row == GROUP - 1, at_end, 0.0)
+        dk = dk + mm_tn(dscores, v["queries"])
+        dq = dq + mm(dscores, v["keys"])
+        ddecay = lax.dot_general(
+            v["tri"], dcum, contract_first, precision=highest, preferred_element_type=f32
+        )
+        grad_steps = grad_steps - ddecay * jnp.exp(heads_ref[1:2, :LANES])
+        grad_dt = grad_steps * sigmoid(v["dt_in"])
+        head_ref[0:1, :] += jnp.sum(grad_dt, axis=0, keepdims=True)
+        head_ref[1:2, :] += jnp.sum(ddecay * v["decay"], axis=0, keepdims=True)
+        head_ref[2:3, :] += skipped_h
+        dmixed = jnp.concatenate([dv, dk, dq], axis=1)
+        pre, sig = v["pre"], v["sig"]
+        dpre = dmixed * (sig * (1.0 + pre * (1.0 - sig)))
+        acc_ref[4:5, :] += jnp.sum(dpre, axis=0, keepdims=True)
+        longer = jnp.concatenate([dpre, edge_ref[...]], axis=0)
+        edge_ref[...] = dpre[:LEAD]
+        segn = segc_ref[pl.ds(aligned(base + LEAD, 8), GROUP + LEAD), :]
+        dx = jnp.zeros((GROUP, plan.mixed), f32)
+        for k in range(KERNEL):
+            acc_ref[k : k + 1, :] += jnp.sum(dpre * v["shifts"][k], axis=0, keepdims=True)
+            ahead = KERNEL - 1 - k
+            part = longer[ahead : ahead + GROUP]
+            if ahead:
+                same = (segn[ahead : ahead + GROUP] == v["seg"]).astype(f32)
+                part = part * jnp.concatenate([same] * repeat, axis=1)
+            dx = dx + convw[k : k + 1] * part
+        live = jnp.where(lane < plan.heads, grad_dt, 0.0)
+        gp_ref[pl.ds(base, GROUP), :] = jnp.concatenate([dx, live], axis=1).astype(bf16)
+        return carry
+
+    lax.fori_loop(0, plan.blocks, step, 0)
+    gn_ref[...] = mm_nt(gp_ref[...], w_ref[...]) + mm_nt(dz_ref[...], wz_ref[...])
+    gain_in = jnp.zeros((1, WIDTH), f32)
+    for m in range(n):
+        tok = toks[m][...].astype(f32)
+        scale = lax.rsqrt(jnp.mean(tok * tok, axis=1, keepdims=True) + norm_eps)
+        part = gn_ref[pl.ds(aligned((s ^ m) * plan.rows, plan.rows), plan.rows), :]
+        gain_in = gain_in + jnp.sum(part * (tok * scale), axis=0, keepdims=True)
+        grads[m][...] = part.astype(grads[m].dtype)
+    gw_ref[...] = mm_tn(normed_ref[...], gp_ref[...])
+    both = (keep_ref, send_ref)
+
+    def put(core_xor, line_xor, m, rows):
+        top = m * plan.in_rows
+        both[core_xor][line_xor, top : top + plan.in_rows, :] = rows.astype(bf16)
+
+    emit_rows(plan, ids, gw_ref, put)
+    small_ref[...] = jnp.zeros_like(small_ref)
+    small_ref[0:1, :WIDTH] = gain_in
+    small_ref[1:6, : plan.mixed] = acc_ref[0:5, :]
+    small_ref[6:7, : plan.chan] = gain_out_ref[...]
+    for j in range(3):
+        small_ref[7:8, j * LANES : (j + 1) * LANES] = head_ref[j : j + 1, :]
+
+
+def add_split_kernel(count, keep_ref, got_ref, *outs):
+    for m in range(count):
+        outs[m][...] = (keep_ref[m].astype(f32) + got_ref[m].astype(f32)).astype(bf16)
+
+
+def gate_sum_kernel(plan, *refs):
+    parts, outs = refs[: plan.line], refs[plan.line :]
+    total = parts[0][...].astype(f32)
+    for part in parts[1:]:
+        total = total + part[...].astype(f32)
+    half = plan.in_rows * plan.seq // 2
+    for m in range(plan.seq):
+        top = (m // 2) * plan.in_rows
+        left = (m % 2) * plan.chan
+        outs[m][...] = total[top : top + plan.in_rows, left : left + plan.chan].astype(bf16)
+    outs[plan.seq][...] = total[half : half + plan.out_rows]
+
+
+def row_sum_kernel(plan, *refs):
+    parts, outs = refs[: plan.line], refs[plan.line :]
+    for m in range(plan.seq):
+        rows = slice(m * plan.in_rows, (m + 1) * plan.in_rows)
+        total = parts[0][rows, :].astype(f32)
+        for part in parts[1:]:
+            total = total + part[rows, :].astype(f32)
+        outs[m][...] = total.astype(bf16)
+
+
+def columns_kernel(plan, *refs):
+    n = plan.seq
+    gates, mains = refs[:n], refs[n : 2 * n]
+    out_ref, gate_ref, main_ref = refs[2 * n :]
+    s = lax.axis_index("seq")
+    for m in range(n):
+        gate_ref[m] = gates[m][...].astype(f32)
+        main_ref[m] = mains[m][...].astype(f32)
+    shared = jnp.zeros((plan.in_rows, 2 * STATE), f32)
+    lane = iota((plan.in_rows, LANES), 1)
+    dts = jnp.zeros((plan.in_rows, LANES), f32)
+    for g in range(n):
+        out_ref[:, g * plan.chan : (g + 1) * plan.chan] = gate_ref[s ^ g]
+        main = main_ref[s ^ g]
+        out_ref[:, INNER + g * plan.chan : INNER + (g + 1) * plan.chan] = main[:, : plan.chan]
+        shared = shared + main[:, plan.chan : plan.mixed]
+        one = main[:, plan.mixed :]
+        moved = one if g == 0 else pltpu.roll(one, g * plan.heads, 1)
+        dts = jnp.where(lane // plan.heads == g, moved, dts)
+    out_ref[:, 2 * INNER : INNER + CONV] = shared
+    out_ref[:, INNER + CONV :] = dts[:, :HEADS]
+
+
+def small_kernel(plan, *refs):
+    n = plan.seq
+    parts = refs[:n]
+    gain_in_ref, convw_ref, convb_ref, dtb_ref, alog_ref, skip_ref, gain_out_ref, all_ref = refs[n:]
+    s = lax.axis_index("seq")
+    for m in range(n):
+        all_ref[m] = parts[m][...]
+    gain_in = jnp.zeros((1, WIDTH), f32)
+    shared = jnp.zeros((5, 2 * STATE), f32)
+    lane = iota((1, LANES), 1)
+    heads = [jnp.zeros((1, LANES), f32) for _ in range(3)]
+    for g in range(n):
+        part = all_ref[s ^ g]
+        gain_in = gain_in + part[0:1, :WIDTH]
+        cols = slice(g * plan.chan, (g + 1) * plan.chan)
+        convw_ref[:, cols] = part[1:5, : plan.chan]
+        convb_ref[:, cols] = part[5:6, : plan.chan]
+        gain_out_ref[:, cols] = part[6:7, : plan.chan]
+        shared = shared + part[1:6, plan.chan : plan.mixed]
+        for j in range(3):
+            one = part[7:8, j * LANES : (j + 1) * LANES]
+            moved = one if g == 0 else pltpu.roll(one, g * plan.heads, 1)
+            heads[j] = jnp.where(lane // plan.heads == g, moved, heads[j])
+    gain_in_ref[...] = gain_in
+    convw_ref[:, INNER:] = shared[:4]
+    convb_ref[:, INNER:] = shared[4:]
+    dtb_ref[...] = heads[0][:, :HEADS]
+    alog_ref[...] = heads[1][:, :HEADS]
+    skip_ref[...] = heads[2][:, :HEADS]
+
+
+def result_kernel(plan, tok_ref, scale_ref, *refs):
+    parts, out_ref = refs[: plan.seq], refs[plan.seq]
+    s = lax.axis_index("seq")
+    total = parts[0][...].astype(f32)
+    for part in parts[1:]:
+        total = total + part[...].astype(f32)
+    r = scale_ref[pl.ds(aligned(s * plan.rows, plan.rows), plan.rows), :]
+    r = jnp.concatenate([r] * (WIDTH // LANES), axis=1)
+    out_ref[...] = (tok_ref[...].astype(f32) + total * r).astype(bf16)
+
+
+def token_kernel(plan, tok_ref, cot_ref, gain_ref, *refs):
+    parts, out_ref = refs[: plan.seq], refs[plan.seq]
+    total = parts[0][...].astype(f32)
+    for part in parts[1:]:
+        total = total + part[...].astype(f32)
+    tok = tok_ref[...].astype(f32)
+    q = lax.rsqrt(jnp.mean(tok * tok, axis=1, keepdims=True) + norm_eps)
+    w = total * gain_ref[...]
+    mean = jnp.mean(w * tok, axis=1, keepdims=True)
+    grad = cot_ref[...].astype(f32) + q * w - tok * (q * q * q * mean)
+    out_ref[...] = grad.astype(bf16)
+
+
+def call(body, plan, outs, scratch, *args, flops=0, name=None):
+    shapes = [jax.ShapeDtypeStruct(shape, kind) for shape, kind in outs]
+    size = sum(a.size * a.dtype.itemsize for a in args)
+    size += sum(a.size * a.dtype.itemsize for a in shapes)
+    return pl.pallas_call(
+        functools.partial(body, plan),
+        out_shape=shapes,
+        in_specs=[pl.BlockSpec(memory_space=pltpu.VMEM)] * len(args),
+        out_specs=[pl.BlockSpec(memory_space=pltpu.VMEM)] * len(shapes),
+        scratch_shapes=[pltpu.VMEM(shape, kind) for shape, kind in scratch],
+        compiler_params=pltpu.CompilerParams(vmem_limit_bytes=VMEM_LIMIT),
+        cost_estimate=pl.CostEstimate(flops=flops, bytes_accessed=size, transcendentals=0),
+        name=name,
+    )(*args)
+
+
+VMEM_LIMIT = 48 * 1024 * 1024
+
+
+def swap(value, axis, by):
+    size = lax.axis_size(axis)
+    return lax.ppermute(value, axis, [(i, i ^ by) for i in range(size)])
+
+
+def after(value, *others):
+    return lax.optimization_barrier((value, *others))[0]
+
+
+def head_parallel(
+    tokens, cotangent, segments, in_weight, out_weight, gain_in, conv_weight, conv_bias,
+    dt_bias, a_log, d_skip, gain_out,
+):
+    rows = tokens.shape[1]
+    plan = Plan(
+        lax.axis_size("seq"), lax.axis_size("batch"), rows, in_weight.shape[0], out_weight.shape[0]
+    )
+    n, line, chan, heads = plan.seq, plan.line, plan.chan, plan.heads
+    s = lax.axis_index("seq")
+    tok, cot = tokens[0], cotangent[0]
+
+    seg_row = jnp.pad(segments.astype(bf16), ((0, 7), (0, plan.cols + chan - rows)))
+    blocks = []
+    for g in range(n):
+        main = [
+            in_weight[:, INNER + g * chan : INNER + (g + 1) * chan],
+            in_weight[:, 2 * INNER : INNER + CONV],
+            jnp.pad(
+                in_weight[:, INNER + CONV + g * heads : INNER + CONV + (g + 1) * heads],
+                ((0, 0), (0, LANES - heads)),
+            ),
+            in_weight[:, g * chan : (g + 1) * chan],
+        ]
+        blocks.append(jnp.concatenate([jnp.concatenate(main, axis=1), seg_row], axis=0))
+    blocks = jnp.stack(blocks)
+    own = [lax.dynamic_index_in_dim(blocks, s ^ m, 0, False) for m in range(n)]
+    pieces = [own[0]] + [swap(own[m], "seq", m) for m in range(1, n)]
+    toks = [tok] + [swap(tok, "seq", m) for m in range(1, n)]
+
+    r = plan.in_rows
+    main_shard = jnp.concatenate([p[:r, : plan.cols] for p in pieces], axis=0)
+    gate_cols = [p[:r, plan.cols :] for p in pieces]
+    gate_shard = jnp.concatenate(
+        [jnp.concatenate(gate_cols[i : i + 2], axis=1) for i in range(0, n, 2)] + [out_weight],
+        axis=0,
+    )
+
+    def spread(shard):
+        mine = [shard] + [swap(shard, "batch", 2 * m) for m in range(1, line)]
+        return mine + [swap(one, "batch", 1) for one in mine]
+
+    main_parts = spread(main_shard)
+    later = after(gate_shard, *main_parts[:line])
+    gate_parts = spread(later)
+    cot_later = after(cot, *toks)
+    cots = [cot] + [swap(cot_later, "seq", m) for m in range(1, n)]
+
+    def own_cols(value):
+        group = lax.dynamic_slice_in_dim(value, s * chan, chan, value.ndim - 1)
+        return jnp.concatenate([group, value[..., INNER:]], axis=-1)
+
+    convw = own_cols(conv_weight)
+    convb = own_cols(conv_bias)[None]
+    own_gain = lax.dynamic_slice_in_dim(gain_out, s * chan, chan, 0)[None]
+
+    def own_heads(value):
+        return lax.dynamic_slice_in_dim(value, s * heads, heads, 0)
+
+    def padded(value):
+        return jnp.pad(value, (0, chan - value.shape[0]))[None]
+
+    per_head = jnp.concatenate(
+        [
+            padded(own_heads(dt_bias)),
+            padded(own_heads(a_log)),
+            jnp.repeat(own_heads(d_skip), HEADDIM)[None],
+            jnp.zeros((5, chan), f32),
+        ],
+        axis=0,
+    )
+    gain_row = gain_in[None]
+    total = plan.total
+    seg_rows = -(-plan.blocks // 8) * 8
+    normed, w_main, x, dt_raw, y, states, segc, segr = call(
+        forward_kernel, plan,
+        [
+            ((total, WIDTH), bf16), ((WIDTH, plan.cols), bf16),
+            ((total + LEAD, plan.mixed), f32), ((total, LANES), f32), ((total, chan), f32),
+            ((plan.blocks, STATE, chan), f32), ((total + 2 * LEAD, LANES), f32),
+            ((seg_rows, GROUP), f32),
+        ],
+        [((WIDTH, plan.cols), f32), ((STATE, chan), f32)],
+        *toks, *pieces, *main_parts, gain_row, convw, convb, per_head,
+        flops=2 * total * WIDTH * plan.cols, name="ssd_forward",
+    )
+    piece_shape = (rows, WIDTH)
+    w_gate, z, du, stats, *outs = call(
+        gate_kernel, plan,
+        [
+            ((WIDTH, chan), bf16), ((total, chan), f32), ((total, chan), f32),
+            ((2 * plan.blocks, GROUP), f32),
+        ] + [(piece_shape, bf16)] * n,
+        [((WIDTH, chan), f32), ((chan, WIDTH), bf16)],
+        normed, y, *gate_parts, *cots, own_gain,
+        flops=6 * total * WIDTH * chan, name="gate_forward",
+    )
+    all_stats = [stats] + [swap(stats, "seq", m) for m in range(1, n)]
+    dy, dz, scale, gain_out_grad, keep, send = call(
+        regate_kernel, plan,
+        [
+            ((total, chan), f32), ((total, chan), bf16), ((total, LANES), f32), ((1, chan), f32),
+            ((line, n * r // 2 + plan.out_rows, WIDTH), bf16),
+            ((line, n * r // 2 + plan.out_rows, WIDTH), bf16),
+        ],
+        [((total, chan), bf16), ((WIDTH, chan), f32), ((chan, WIDTH), f32)],
+        *all_stats, normed, y, z, du, *cots, own_gain,
+        flops=4 * total * WIDTH * chan, name="gate_backward",
+    )
+
+    def reduce_line(keep, send, width):
+        got = swap(send, "batch", 1)
+        rows_here = keep.shape[1]
+        parts = call(
+            lambda count, *refs: add_split_kernel(count, *refs), line,
+            [((rows_here, width), bf16)] * line, [], keep, got, name="core_sum",
+        )
+        return [parts[0]] + [swap(parts[m], "batch", 2 * m) for m in range(1, line)]
+
+    out_late = [after(o, dy) for o in outs[1:]]
+    out_parts = [outs[0]] + [swap(out_late[m - 1], "seq", m) for m in range(1, n)]
+    gate_lines = reduce_line(keep, send, WIDTH)
+    *gate_grads, shard_out = call(
+        gate_sum_kernel, plan,
+        [((r, chan), bf16)] * n + [((plan.out_rows, WIDTH), f32)], [], *gate_lines,
+        name="gate_sum",
+    )
+    gate_grads = [gate_grads[0]] + [swap(gate_grads[m], "seq", m) for m in range(1, n)]
+    (result,) = call(
+        result_kernel, plan, [(piece_shape, bf16)], [], tok, scale, *out_parts, name="result"
+    )
+
+    *grads, keep, send, small = call(
+        backward_kernel, plan,
+        [(piece_shape, bf16)] * n
+        + [((line, n * r, plan.cols), bf16)] * 2
+        + [((8, max(WIDTH, plan.mixed)), f32)],
+        [
+            ((total, plan.cols), bf16), ((WIDTH, plan.cols), f32), ((total, WIDTH), f32),
+            ((STATE, chan), f32), ((LEAD, plan.mixed), f32), ((8, plan.mixed), f32),
+            ((8, LANES), f32),
+        ],
+        *toks, normed, w_main, w_gate, x, dt_raw, states, segc, segr, dy, dz, gain_out_grad,
+        convw, convb, per_head,
+        flops=2 * total * WIDTH * (2 * plan.cols + chan), name="ssd_backward",
+    )
+    main_lines = reduce_line(keep, send, plan.cols)
+    grad_parts = [grads[0]] + [swap(grads[m], "seq", m) for m in range(1, n)]
+    small = small + swap(small, "batch", 1)
+    small = sum([swap(small, "batch", 2 * m) for m in range(1, line)], small)
+    small_parts = [small] + [swap(small, "seq", m) for m in range(1, n)]
+    main_grads = call(
+        row_sum_kernel, plan, [((r, plan.cols), bf16)] * n, [], *main_lines, name="main_sum"
+    )
+    main_grads = [main_grads[0]] + [swap(main_grads[m], "seq", m) for m in range(1, n)]
+    (grad_tokens,) = call(
+        token_kernel, plan, [(piece_shape, bf16)], [], tok, cot, gain_row, *grad_parts,
+        name="token_grad",
+    )
+    (shard_in,) = call(
+        columns_kernel, plan, [((r, in_weight.shape[1]), f32)],
+        [((n, r, chan), f32), ((n, r, plan.cols), f32)], *gate_grads, *main_grads, name="columns",
+    )
+    smalls = call(
+        small_kernel, plan,
+        [
+            ((1, WIDTH), f32), ((KERNEL, CONV), f32), ((1, CONV), f32), ((1, HEADS), f32),
+            ((1, HEADS), f32), ((1, HEADS), f32), ((1, INNER), f32),
+        ],
+        [((n,) + small.shape, f32)], *small_parts, name="small_grads",
+    )
+    return (
+        result[None], grad_tokens[None], shard_in, shard_out, smalls[0][0], smalls[1],
+        smalls[2][0], smalls[3][0], smalls[4][0], smalls[5][0], smalls[6][0],
+    )
 
 
 def shifted(value, axis, by):
@@ -344,6 +1128,8 @@
         P(),
         P(),
     )
+    count = mesh.shape["seq"]
+    even = HEADS % (2 * count) == 0 and count & (count - 1) == 0
     return jax.shard_map(
-        on_device, mesh=mesh, in_specs=in_specs, out_specs=out_specs, check_vma=False
-    )
+        head_parallel if even else on_device, mesh=mesh, in_specs=in_specs, out_specs=out_specs, check_vma=False
+    )

time: 633 us -> 203 us (0.32); the launches traced: 620 us -> 200 us
  waiting for transfers between devices: 232 us -> 57.7 us
  local copies, waits for them, and re-layouts: 157 us -> 29.6 us
  matrix products: 83.1 us -> 0 us
  other arithmetic: 71.3 us -> 2.73 us
  Pallas kernels: 0 us -> 55.9 us
  blocking collectives: 50.1 us -> 0 us
  starting transfers between devices: 8.9 us -> 53.2 us
  between operations: 17.4 us -> 1.05 us
    all_gather x4 -> x0, waiting for transfers between devices: 139 us -> none  [the longest x1 59.2 us: on_device(): lax.all_gather(in_weight, ('seq', 'batch'), axis=0, tiled=True)]
    unnamed x7 -> x0, waiting for transfers between devices: 91.7 us -> none
    dot_general x37 -> x0, matrix products: 83.1 us -> none  [the longest x6 21.4 us: group_block(): inside = jnp.einsum('tsh,shp->thp', weights, values, precision=highest)]
    dynamic_update_slice x6 -> x0, local copies, waits for them, and re-layouts: 77.5 us -> none  [grouped_ssd(): lax.scan(jax.checkpoint(group_block), (state_in, last_seg), inputs)]
    ppermute x3 -> x53, waiting for transfers between devices: 1.04 us -> 57.7 us  [swap(): return lax.ppermute(value, axis, [(i, i ^ by) for i in range(size)])]
    pallas_call x0 -> x12, Pallas kernels: none -> 55.9 us  [call(): pl.pallas_call(functools.partial(body, plan), out_shape=shapes, in_specs=...]
    ppermute x3 -> x53, starting transfers between devices: 8.66 us -> 53.2 us  [swap(): return lax.ppermute(value, axis, [(i, i ^ by) for i in range(size)])]
    psum x1 -> x0, blocking collectives: 40.9 us -> none  [on_device(): lax.psum((grad_gain_in, grad_conv_w, grad_conv_b, grad_dt_bias, grad_a_lo...]
  transfers between devices with their start and end apart: 9 -> 53, of which waited for: 6 -> 20; matrix products, arithmetic and copies ran while one was open for 33% -> 3% of each run, Pallas kernels for 0% -> 9%
where the time goes in v1:
time: 203 us; the launch traced here: 200 us
  waiting for transfers between devices  57.7 us (28%)
  Pallas kernels  55.9 us (28%)
  starting transfers between devices  53.2 us (26%)
  local copies, waits for them, and re-layouts  29.6 us (15%)
  other arithmetic  2.73 us (1%)
    ppermute x53, waiting for transfers between devices, swap(): return lax.ppermute(value, axis, [(i, i ^ by) for i in range(size)])  57.7 us
    pallas_call x12, Pallas kernels, call(): pl.pallas_call(functools.partial(body, plan), out_shape=shapes, in_specs=...  55.9 us
    ppermute x53, starting transfers between devices, swap(): return lax.ppermute(value, axis, [(i, i ^ by) for i in range(size)])  53.2 us
    unnamed x88, local copies, waits for them, and re-layouts  22.8 us
  transfers between devices with their start and end apart: 53, of which 20 were waited for; matrix products, arithmetic and copies ran while one was open for 3% of the time, Pallas kernels for 9%

profile of v1, /device:TPU:8, one launch (start us, length us, event | category | flops | bytes accessed | tf_op | source)
XLA Modules:
  0.0 200.2 jit_solution(4601366443551751043)
XLA Ops:
  4.9 2.5 %collective-permute-start.5 = (bf16[32,1152]{1,0:T(8,128)(2,1)S(1)}, bf16[32,1152]{1,0:T(8,128)(2,1)S(1)}, u32[]{:S(2)}, u32[]{:S(2)}) collective-permute-start(bf16[32,1152]{1,0:T(8,128)(2,1)S(1)} %get-tuple-element.127), channel_id=1, source_target_pairs={{0,24},{8,16},{16,8},{24,0},{1,25},{9,17},{17,9},{25,1},{2,26},{10... | collective-permute-start | bytes 221192 | tf_op jit(solution)/shard_map/ppermute | solution.py:619
  8.5 1.8 collective-permute-done.5.refs_7_
  12.3 1.6 collective-permute-start.8
  18.7 5.4 %collective-permute-done.8.refs_11_ = bf16[96,768]{1,0:T(8,128)(2,1)S(1)} collective-permute-done((bf16[96,768]{1,0:T(8,128)(2,1)S(1)}, bf16[96,768]{1,0:T(8,128)(2,1)S(1)}, u32[]{:S(2)}, u32[]{:S(2)}) %collective-permute-start.8) | collective-permute-done | bytes 147488 | tf_op jit(solution)/shard_map/ppermute | solution.py:619
  24.1 1.8 collective-permute-done.7.refs_10_
  25.9 3.4 %collective-permute-done.6.refs_9_ = bf16[96,768]{1,0:T(8,128)(2,1)} collective-permute-done((bf16[96,768]{1,0:T(8,128)(2,1)S(1)}, bf16[96,768]{1,0:T(8,128)(2,1)}, u32[]{:S(2)}, u32[]{:S(2)}) %collective-permute-start.6) | collective-permute-done | bytes 147488 | tf_op jit(solution)/shard_map/ppermute | solution.py:619
  31.8 2.5 %collective-permute-start.15 = (bf16[96,768]{1,0:T(8,128)(2,1)S(1)}, bf16[96,768]{1,0:T(8,128)(2,1)S(1)}, u32[]{:S(2)}, u32[]{:S(2)}) collective-permute-start(bf16[96,768]{1,0:T(8,128)(2,1)S(1)} %pad_maximum_fusion.2.refs_2_), channel_id=1, source_target_pairs={{0,6},{1,7},{2,4},{3,5},{4,2},{5,3},{6,0},{7,1},{8,14},{9,15},{10,... | collective-permute-start | bytes 442376 | tf_op jit(solution)/shard_map/ppermute | solution.py:619
  38.6 6.0 %collective-permute-done.15.refs_5_ = bf16[96,768]{1,0:T(8,128)(2,1)S(1)} collective-permute-done((bf16[96,768]{1,0:T(8,128)(2,1)S(1)}, bf16[96,768]{1,0:T(8,128)(2,1)S(1)}, u32[]{:S(2)}, u32[]{:S(2)}) %collective-permute-start.15) | collective-permute-done | bytes 147488 | tf_op jit(solution)/shard_map/ppermute | solution.py:619
  61.5 13.0 %ssd_forward.1 = (bf16[1024,768]{1,0:T(8,128)(2,1)}, bf16[768,768]{1,0:T(8,128)(2,1)S(1)}, f32[1032,640]{1,0:T(8,128)}, f32[1024,128]{1,0:T(8,128)S(1)}, f32[102...) custom-call(bf16[256,768]{1,0:T(8,128)(2,1)S(1)} %bitcast.26, ...), custom_call_target="tpu_custom_call" | custom-call | flops 1207959552 | bytes 12676608 | tf_op jit(solution)/shard_map/ssd_forward/pallas_call | solution.py:602
  75.7 6.6 %gate_forward.1 = (bf16[768,384]{1,0:T(8,128)(2,1)S(1)}, f32[1024,384]{1,0:T(8,128)}, f32[1024,384]{1,0:T(8,128)}, f32[16,128]{1,0:T(8,128)S(1)}, bf16[256,768]{...) custom-call(bf16[1024,768]{1,0:T(8,128)(2,1)} %get-tuple-element.69., ...), custom_call_target="tpu_custom_call" | custom-call | flops 1811939328 | bytes 11216384 | tf_op jit(solution)/shard_map/gate_forward/pallas_call | solution.py:602
  90.7 5.7 %gate_backward.1 = (f32[1024,384]{1,0:T(8,128)S(1)}, bf16[1024,384]{1,0:T(8,128)(2,1)S(1)}, f32[1024,128]{1,0:T(8,128)S(1)}, f32[1,384]{1,0:T(1,128)S(1)}, bf16[...) custom-call(f32[16,128]{1,0:T(8,128)S(1)} %get-tuple-element.73.refs_0_, ...), custom_call_target="tpu_custom_call" | custom-call | flops 1207959552 | bytes 11963392 | tf_op jit(solution)/shard_map/gate_backward/pallas_call | solution.py:602
  98.5 25.2 %ssd_backward.1 = (bf16[256,768]{1,0:T(8,128)(2,1)S(1)}, bf16[256,768]{1,0:T(8,128)(2,1)S(1)}, bf16[256,768]{1,0:T(8,128)(2,1)S(1)}, bf16[256,768]{1,0:T(8,128)(...) custom-call(bf16[256,768]{1,0:T(8,128)(2,1)S(1)} %bitcast.27, ...), custom_call_target="tpu_custom_call" | custom-call | flops 3019898880 | bytes 15353856 | tf_op jit(solution)/shard_map/ssd_backward/pallas_call | solution.py:602
  124.8 1.9 collective-permute-done.46
  128.1 2.6 %collective-permute-start.48 = (f32[8,768]{1,0:T(8,128)S(1)}, f32[8,768]{1,0:T(8,128)S(1)}, u32[]{:S(2)}, u32[]{:S(2)}) collective-permute-start(f32[8,768]{1,0:T(8,128)S(1)} %add.58), channel_id=1, source_target_pairs={{0,4},{1,5},{2,6},{3,7},{4,0},{5,1},{6,2},{7,3},{8,12},{9,13},{10,... | collective-permute-start | bytes 73736 | tf_op jit(solution)/shard_map/ppermute | solution.py:619
  131.3 2.8 %collective-permute-start.40 = (bf16[96,768]{1,0:T(8,128)(2,1)S(1)}, bf16[96,768]{1,0:T(8,128)(2,1)S(1)}, u32[]{:S(2)}, u32[]{:S(2)}) collective-permute-start(bf16[96,768]{1,0:T(8,128)(2,1)S(1)} %get-tuple-element.111), channel_id=1, source_target_pairs={{0,2},{1,3},{2,0},{3,1},{4,6},{5,7},{6,4},{7,5},{8,10},{9,11},{10,... | collective-permute-start | bytes 442376 | tf_op jit(solution)/shard_map/ppermute | solution.py:619
  142.3 1.7 collective-permute-start.33
  145.9 6.6 %collective-permute-done.41.refs_2_ = bf16[96,768]{1,0:T(8,128)(2,1)S(1)} collective-permute-done((bf16[96,768]{1,0:T(8,128)(2,1)S(1)}, bf16[96,768]{1,0:T(8,128)(2,1)S(1)}, u32[]{:S(2)}, u32[]{:S(2)}) %collective-permute-start.41) | collective-permute-done | bytes 147488 | tf_op jit(solution)/shard_map/ppermute | solution.py:619
  153.1 7.4 %collective-permute-done.42.refs_3_ = bf16[96,768]{1,0:T(8,128)(2,1)S(1)} collective-permute-done((bf16[96,768]{1,0:T(8,128)(2,1)S(1)}, bf16[96,768]{1,0:T(8,128)(2,1)S(1)}, u32[]{:S(2)}, u32[]{:S(2)}) %collective-permute-start.42) | collective-permute-done | bytes 147488 | tf_op jit(solution)/shard_map/ppermute | solution.py:619
  164.0 1.6 collective-permute-done.35.refs_3_
  169.0 4.4 %collective-permute-done.28.refs_3_ = bf16[256,768]{1,0:T(8,128)(2,1)S(1)} collective-permute-done((bf16[256,768]{1,0:T(8,128)(2,1)S(1)}, bf16[256,768]{1,0:T(8,128)(2,1)S(1)}, u32[]{:S(2)}, u32[]{:S(2)}) %collective-permute-start.28) | collective-permute-done | bytes 393248 | tf_op jit(solution)/shard_map/ppermute | solution.py:619
  174.4 6.6 %collective-permute-done.29.refs_1_ = bf16[256,768]{1,0:T(8,128)(2,1)S(1)} collective-permute-done((bf16[256,768]{1,0:T(8,128)(2,1)S(1)}, bf16[256,768]{1,0:T(8,128)(2,1)S(1)}, u32[]{:S(2)}, u32[]{:S(2)}) %collective-permute-start.29) | collective-permute-done | bytes 393248 | tf_op jit(solution)/shard_map/ppermute | solution.py:619
  183.9 1.6 collective-permute-start.45
  185.5 2.5 %collective-permute-done.31.refs_3_ = bf16[256,768]{1,0:T(8,128)(2,1)S(1)} collective-permute-done((bf16[256,768]{1,0:T(8,128)(2,1)S(1)}, bf16[256,768]{1,0:T(8,128)(2,1)S(1)}, u32[]{:S(2)}, u32[]{:S(2)}) %collective-permute-start.31) | collective-permute-done | bytes 393248 | tf_op jit(solution)/shard_map/ppermute | solution.py:619
  189.4 2.2 %collective-permute-start.38 = (bf16[24,384]{1,0:T(8,128)(2,1)S(1)}, bf16[24,384]{1,0:T(8,128)(2,1)S(1)}, u32[]{:S(2)}, u32[]{:S(2)}) collective-permute-start(bf16[24,384]{1,0:T(8,128)(2,1)S(1)} %get-tuple-element.107), channel_id=1, source_target_pairs={{0,24},{8,16},{16,8},{24,0},{1,25},{9,17},{17,9},{25,1},{2,26},{10... | collective-permute-start | bytes 55304 | tf_op jit(solution)/shard_map/ppermute | solution.py:619
  (228 shorter events, 81.6 us)
Async XLA Ops:
  14.0 20.3 %collective-permute-start.2 = (bf16[256,768]{1,0:T(8,128)(2,1)S(1)}, bf16[256,768]{1,0:T(8,128)(2,1)S(1)}, u32[]{:S(2)}, u32[]{:S(2)}) collective-permute-start(bf16[256,768]{1,0:T(8,128)(2,1)S(1)} %bitcast.23), channel_id=1, source_target_pairs={{0,24},{8,16},{16,8},{24,0},{1,25},{9,17},{17,9},{25,1},{2,26},{10... | collective-permute-start | bytes 1179656 | tf_op jit(solution)/shard_map/ppermute | solution.py:619
  15.4 19.0 %collective-permute-start.1 = (bf16[256,768]{1,0:T(8,128)(2,1)S(1)}, bf16[256,768]{1,0:T(8,128)(2,1)S(1)}, u32[]{:S(2)}, u32[]{:S(2)}) collective-permute-start(bf16[256,768]{1,0:T(8,128)(2,1)S(1)} %bitcast.24), channel_id=1, source_target_pairs={{0,16},{8,24},{16,0},{24,8},{1,17},{9,25},{17,1},{25,9},{2,18},{10... | collective-permute-start | bytes 1179656 | tf_op jit(solution)/shard_map/ppermute | solution.py:619
  16.1 20.2 %collective-permute-start = (bf16[256,768]{1,0:T(8,128)(2,1)S(1)}, bf16[256,768]{1,0:T(8,128)(2,1)S(1)}, u32[]{:S(2)}, u32[]{:S(2)}) collective-permute-start(bf16[256,768]{1,0:T(8,128)(2,1)S(1)} %bitcast.25), channel_id=1, source_target_pairs={{0,8},{8,0},{16,24},{24,16},{1,9},{9,1},{17,25},{25,17},{2,10},{10... | collective-permute-start | bytes 1179656 | tf_op jit(solution)/shard_map/ppermute | solution.py:619
  30.6 14.7 %collective-permute-start.16 = (bf16[96,768]{1,0:T(8,128)(2,1)S(1)}, bf16[96,768]{1,0:T(8,128)(2,1)S(1)}, u32[]{:S(2)}, u32[]{:S(2)}) collective-permute-start(bf16[96,768]{1,0:T(8,128)(2,1)S(1)} %pad_maximum_fusion.2.refs_2_), channel_id=1, source_target_pairs={{0,1},{1,0},{2,3},{3,2},{4,5},{5,4},{6,7},{7,6},{8,9},{9,8},{10,11... | collective-permute-start | bytes 442376 | tf_op jit(solution)/shard_map/ppermute | solution.py:619
  34.4 14.5 %collective-permute-start.13 = (bf16[96,768]{1,0:T(8,128)(2,1)S(1)}, bf16[96,768]{1,0:T(8,128)(2,1)}, u32[]{:S(2)}, u32[]{:S(2)}) collective-permute-start(bf16[96,768]{1,0:T(8,128)(2,1)S(1)} %pad_maximum_fusion.2.refs_2_), channel_id=1, source_target_pairs={{0,2},{1,3},{2,0},{3,1},{4,6},{5,7},{6,4},{7,5},{8,10},{9,11},{10,... | collective-permute-start | bytes 442376 | tf_op jit(solution)/shard_map/ppermute | solution.py:619
  46.0 29.6 %collective-permute-start.22 = (bf16[256,768]{1,0:T(8,128)(2,1)S(1)}, bf16[256,768]{1,0:T(8,128)(2,1)S(1)}, u32[]{:S(2)}, u32[]{:S(2)}) collective-permute-start(bf16[256,768]{1,0:T(8,128)(2,1)S(1)} %bitcast.30), channel_id=1, source_target_pairs={{0,24},{8,16},{16,8},{24,0},{1,25},{9,17},{17,9},{25,1},{2,26},{10... | collective-permute-start | bytes 1179656 | tf_op jit(solution)/shard_map/ppermute | solution.py:619
  47.4 28.2 %collective-permute-start.21 = (bf16[256,768]{1,0:T(8,128)(2,1)S(1)}, bf16[256,768]{1,0:T(8,128)(2,1)S(1)}, u32[]{:S(2)}, u32[]{:S(2)}) collective-permute-start(bf16[256,768]{1,0:T(8,128)(2,1)S(1)} %bitcast.31), channel_id=1, source_target_pairs={{0,16},{8,24},{16,0},{24,8},{1,17},{9,25},{17,1},{25,9},{2,18},{10... | collective-permute-start | bytes 1179656 | tf_op jit(solution)/shard_map/ppermute | solution.py:619
  48.9 26.7 %collective-permute-start.20 = (bf16[256,768]{1,0:T(8,128)(2,1)S(1)}, bf16[256,768]{1,0:T(8,128)(2,1)S(1)}, u32[]{:S(2)}, u32[]{:S(2)}) collective-permute-start(bf16[256,768]{1,0:T(8,128)(2,1)S(1)} %bitcast.32), channel_id=1, source_target_pairs={{0,8},{8,0},{16,24},{24,16},{1,9},{9,1},{17,25},{25,17},{2,10},{10... | collective-permute-start | bytes 1179656 | tf_op jit(solution)/shard_map/ppermute | solution.py:619
  51.6 24.0 %collective-permute-start.18 = (bf16[96,768]{1,0:T(8,128)(2,1)}, bf16[96,768]{1,0:T(8,128)(2,1)}, u32[]{:S(2)}, u32[]{:S(2)}) collective-permute-start(bf16[96,768]{1,0:T(8,128)(2,1)} %collective-permute-done.14.refs_4_), channel_id=1, source_target_pairs={{0,1},{1,0},{2,3},{3,2},{4,5},{5,4},{6,7},{7,6},{8,9},{9,8},{10,11... | collective-permute-start | bytes 442376 | tf_op jit(solution)/shard_map/ppermute | solution.py:619
  52.3 23.3 %collective-permute-start.17 = (bf16[96,768]{1,0:T(8,128)(2,1)}, bf16[96,768]{1,0:T(8,128)(2,1)}, u32[]{:S(2)}, u32[]{:S(2)}) collective-permute-start(bf16[96,768]{1,0:T(8,128)(2,1)} %collective-permute-done.13.refs_3_), channel_id=1, source_target_pairs={{0,1},{1,0},{2,3},{3,2},{4,5},{5,4},{6,7},{7,6},{8,9},{9,8},{10,11... | collective-permute-start | bytes 442376 | tf_op jit(solution)/shard_map/ppermute | solution.py:619
  124.3 19.7 %collective-permute-start.26 = (bf16[256,768]{1,0:T(8,128)(2,1)S(1)}, bf16[256,768]{1,0:T(8,128)(2,1)S(1)}, u32[]{:S(2)}, u32[]{:S(2)}) collective-permute-start(bf16[256,768]{1,0:T(8,128)(2,1)S(1)} %get-tuple-element.80), channel_id=1, source_target_pairs={{0,8},{8,0},{16,24},{24,16},{1,9},{9,1},{17,25},{25,17},{2,10},{10... | collective-permute-start | bytes 1179656 | tf_op jit(solution)/shard_map/ppermute | solution.py:619
  131.3 14.0 %collective-permute-start.40 = (bf16[96,768]{1,0:T(8,128)(2,1)S(1)}, bf16[96,768]{1,0:T(8,128)(2,1)S(1)}, u32[]{:S(2)}, u32[]{:S(2)}) collective-permute-start(bf16[96,768]{1,0:T(8,128)(2,1)S(1)} %get-tuple-element.111), channel_id=1, source_target_pairs={{0,2},{1,3},{2,0},{3,1},{4,6},{5,7},{6,4},{7,5},{8,10},{9,11},{10,... | collective-permute-start | bytes 442376 | tf_op jit(solution)/shard_map/ppermute | solution.py:619
  140.8 19.7 %collective-permute-start.42 = (bf16[96,768]{1,0:T(8,128)(2,1)S(1)}, bf16[96,768]{1,0:T(8,128)(2,1)S(1)}, u32[]{:S(2)}, u32[]{:S(2)}) collective-permute-start(bf16[96,768]{1,0:T(8,128)(2,1)S(1)} %get-tuple-element.113), channel_id=1, source_target_pairs={{0,6},{1,7},{2,4},{3,5},{4,2},{5,3},{6,0},{7,1},{8,14},{9,15},{10,... | collective-permute-start | bytes 442376 | tf_op jit(solution)/shard_map/ppermute | solution.py:619
  142.3 19.2 %collective-permute-start.33 = (bf16[96,768]{1,0:T(8,128)(2,1)S(1)}, bf16[96,768]{1,0:T(8,128)(2,1)S(1)}, u32[]{:S(2)}, u32[]{:S(2)}) collective-permute-start(bf16[96,768]{1,0:T(8,128)(2,1)S(1)} %get-tuple-element.101), channel_id=1, source_target_pairs={{0,2},{1,3},{2,0},{3,1},{4,6},{5,7},{6,4},{7,5},{8,10},{9,11},{10,... | collective-permute-start | bytes 442376 | tf_op jit(solution)/shard_map/ppermute | solution.py:619
  144.0 18.6 %collective-permute-start.34 = (bf16[96,768]{1,0:T(8,128)(2,1)S(1)}, bf16[96,768]{1,0:T(8,128)(2,1)S(1)}, u32[]{:S(2)}, u32[]{:S(2)}) collective-permute-start(bf16[96,768]{1,0:T(8,128)(2,1)S(1)} %get-tuple-element.102), channel_id=1, source_target_pairs={{0,4},{1,5},{2,6},{3,7},{4,0},{5,1},{6,2},{7,3},{8,12},{9,13},{10,... | collective-permute-start | bytes 442376 | tf_op jit(solution)/shard_map/ppermute | solution.py:619
  145.3 20.3 %collective-permute-start.35 = (bf16[96,768]{1,0:T(8,128)(2,1)S(1)}, bf16[96,768]{1,0:T(8,128)(2,1)S(1)}, u32[]{:S(2)}, u32[]{:S(2)}) collective-permute-start(bf16[96,768]{1,0:T(8,128)(2,1)S(1)} %get-tuple-element.103), channel_id=1, source_target_pairs={{0,6},{1,7},{2,4},{3,5},{4,2},{5,3},{6,0},{7,1},{8,14},{9,15},{10,... | collective-permute-start | bytes 442376 | tf_op jit(solution)/shard_map/ppermute | solution.py:619
  152.5 15.4 %collective-permute-start.27 = (bf16[256,768]{1,0:T(8,128)(2,1)S(1)}, bf16[256,768]{1,0:T(8,128)(2,1)S(1)}, u32[]{:S(2)}, u32[]{:S(2)}) collective-permute-start(bf16[256,768]{1,0:T(8,128)(2,1)S(1)} %get-tuple-element.82), channel_id=1, source_target_pairs={{0,16},{8,24},{16,0},{24,8},{1,17},{9,25},{17,1},{25,9},{2,18},{10... | collective-permute-start | bytes 1179656 | tf_op jit(solution)/shard_map/ppermute | solution.py:619
  161.4 19.6 %collective-permute-start.29 = (bf16[256,768]{1,0:T(8,128)(2,1)S(1)}, bf16[256,768]{1,0:T(8,128)(2,1)S(1)}, u32[]{:S(2)}, u32[]{:S(2)}) collective-permute-start(bf16[256,768]{1,0:T(8,128)(2,1)S(1)} %get-tuple-element.95), channel_id=1, source_target_pairs={{0,8},{8,0},{16,24},{24,16},{1,9},{9,1},{17,25},{25,17},{2,10},{10... | collective-permute-start | bytes 1179656 | tf_op jit(solution)/shard_map/ppermute | solution.py:619
  162.6 20.6 %collective-permute-start.30 = (bf16[256,768]{1,0:T(8,128)(2,1)S(1)}, bf16[256,768]{1,0:T(8,128)(2,1)S(1)}, u32[]{:S(2)}, u32[]{:S(2)}) collective-permute-start(bf16[256,768]{1,0:T(8,128)(2,1)S(1)} %get-tuple-element.96), channel_id=1, source_target_pairs={{0,16},{8,24},{16,0},{24,8},{1,17},{9,25},{17,1},{25,9},{2,18},{10... | collective-permute-start | bytes 1179656 | tf_op jit(solution)/shard_map/ppermute | solution.py:619
  165.6 22.5 %collective-permute-start.31 = (bf16[256,768]{1,0:T(8,128)(2,1)S(1)}, bf16[256,768]{1,0:T(8,128)(2,1)S(1)}, u32[]{:S(2)}, u32[]{:S(2)}) collective-permute-start(bf16[256,768]{1,0:T(8,128)(2,1)S(1)} %get-tuple-element.97), channel_id=1, source_target_pairs={{0,24},{8,16},{16,8},{24,0},{1,25},{9,17},{17,9},{25,1},{2,26},{10... | collective-permute-start | bytes 1179656 | tf_op jit(solution)/shard_map/ppermute | solution.py:619
  167.9 31.4 %collective-permute-start.43 = (bf16[24,768]{1,0:T(8,128)(2,1)}, bf16[24,768]{1,0:T(8,128)(2,1)S(1)}, u32[]{:S(2)}, u32[]{:S(2)}) collective-permute-start(bf16[24,768]{1,0:T(8,128)(2,1)} %get-tuple-element.115), channel_id=1, source_target_pairs={{0,8},{8,0},{16,24},{24,16},{1,9},{9,1},{17,25},{25,17},{2,10},{10... | collective-permute-start | bytes 110600 | tf_op jit(solution)/shard_map/ppermute | solution.py:619
  173.4 15.9 %collective-permute-start.36 = (bf16[24,384]{1,0:T(8,128)(2,1)S(1)}, bf16[24,384]{1,0:T(8,128)(2,1)S(1)}, u32[]{:S(2)}, u32[]{:S(2)}) collective-permute-start(bf16[24,384]{1,0:T(8,128)(2,1)S(1)} %get-tuple-element.105), channel_id=1, source_target_pairs={{0,8},{8,0},{16,24},{24,16},{1,9},{9,1},{17,25},{25,17},{2,10},{10... | collective-permute-start | bytes 55304 | tf_op jit(solution)/shard_map/ppermute | solution.py:619
  181.8 17.5 %collective-permute-start.44 = (bf16[24,768]{1,0:T(8,128)(2,1)}, bf16[24,768]{1,0:T(8,128)(2,1)S(1)}, u32[]{:S(2)}, u32[]{:S(2)}) collective-permute-start(bf16[24,768]{1,0:T(8,128)(2,1)} %get-tuple-element.116), channel_id=1, source_target_pairs={{0,16},{8,24},{16,0},{24,8},{1,17},{9,25},{17,1},{25,9},{2,18},{10... | collective-permute-start | bytes 110600 | tf_op jit(solution)/shard_map/ppermute | solution.py:619
  183.9 15.4 %collective-permute-start.45 = (bf16[24,768]{1,0:T(8,128)(2,1)}, bf16[24,768]{1,0:T(8,128)(2,1)S(1)}, u32[]{:S(2)}, u32[]{:S(2)}) collective-permute-start(bf16[24,768]{1,0:T(8,128)(2,1)} %get-tuple-element.117), channel_id=1, source_target_pairs={{0,24},{8,16},{16,8},{24,0},{1,25},{9,17},{17,9},{25,1},{2,26},{10... | collective-permute-start | bytes 110600 | tf_op jit(solution)/shard_map/ppermute | solution.py:619
  (74 other events, 665.7 us)

commit v2 on v1

--- a/solution.py
+++ b/solution.py
@@ -156,6 +156,85 @@
     return jnp.concatenate([jnp.where(low, pair, 0.0), jnp.where(low, 0.0, pair)], axis=0)
 
 
+def fetch(pairs, sems):
+    copies = [
+        pltpu.make_async_copy(src, dst, sems.at[i]) for i, (src, dst) in enumerate(pairs)
+    ]
+    for copy in copies:
+        copy.start()
+    for copy in copies:
+        copy.wait()
+
+
+def pack_kernel(plan, w_any, seg_any, *outs):
+    n, heads, chan = plan.seq, plan.heads, plan.chan
+    blocks, outs = outs[:n], outs[n:]
+    w_ref, seg_ref, sems, all_ref = outs
+    fetch([(w_any, w_ref), (seg_any, seg_ref)], sems)
+    s = lax.axis_index("seq")
+    lane = iota((plan.in_rows, LANES), 1)
+    tail = w_ref[:, INNER + CONV :].astype(f32)
+    tail = jnp.concatenate(
+        [tail, jnp.zeros((plan.in_rows, LANES - HEADS), f32)], axis=1
+    )
+    for g in range(n):
+        moved = tail if g == 0 else pltpu.roll(tail, LANES - g * heads, 1)
+        all_ref[g] = jnp.concatenate(
+            [
+                w_ref[:, INNER + g * chan : INNER + (g + 1) * chan],
+                w_ref[:, 2 * INNER : INNER + CONV],
+                jnp.where(lane < heads, moved, 0.0).astype(bf16),
+                w_ref[:, g * chan : (g + 1) * chan],
+            ],
+            axis=1,
+        )
+    seg = jnp.broadcast_to(seg_ref[...].astype(f32), (8, plan.rows)).astype(bf16)
+    for m in range(n):
+        blocks[m][0 : plan.in_rows, :] = all_ref[s ^ m]
+        blocks[m][plan.in_rows : plan.in_rows + 8, :] = jnp.zeros((8, plan.cols + chan), bf16)
+        blocks[m][plan.in_rows : plan.in_rows + 8, : plan.rows] = seg
+
+
+def own_params_kernel(
+    plan, convw_ref, convb_ref, dtb_ref, alog_ref, skip_ref, gain_ref, conv_ref, heads_ref,
+    own_gain_ref,
+):
+    n, heads, chan = plan.seq, plan.heads, plan.chan
+    s = lax.axis_index("seq")
+    own = pl.ds(aligned(s * chan, LANES), chan)
+    conv_ref[...] = jnp.zeros_like(conv_ref)
+    conv_ref[0:KERNEL, :chan] = convw_ref[:, own]
+    conv_ref[0:KERNEL, chan:] = convw_ref[:, INNER:]
+    conv_ref[KERNEL : KERNEL + 1, :chan] = convb_ref[:, own]
+    conv_ref[KERNEL : KERNEL + 1, chan:] = convb_ref[:, INNER:]
+    own_gain_ref[...] = gain_ref[:, own]
+    one_lane = iota((1, LANES), 1)
+
+    def own_heads(ref):
+        row = jnp.concatenate([ref[...], jnp.zeros((1, LANES - HEADS), f32)], axis=1)
+        found = row
+        for g in range(1, n):
+            found = jnp.where(s == g, pltpu.roll(row, LANES - g * heads, 1), found)
+        return jnp.where(one_lane < heads, found, 0.0)
+
+    heads_ref[...] = jnp.zeros_like(heads_ref)
+    heads_ref[0:1, :LANES] = own_heads(dtb_ref)
+    heads_ref[1:2, :LANES] = own_heads(alog_ref)
+    heads_ref[2:3, :] = wide(own_heads(skip_ref), heads)
+
+
+def regroup_kernel(plan, *refs):
+    n, r = plan.seq, plan.in_rows
+    pieces, out_w_ref = refs[:n], refs[n]
+    main_ref, gate_ref = refs[n + 1 :]
+    half = r * n // 2
+    for m in range(n):
+        main_ref[m * r : (m + 1) * r, :] = pieces[m][0:r, : plan.cols]
+        top, left = (m // 2) * r, (m % 2) * plan.chan
+        gate_ref[top : top + r, left : left + plan.chan] = pieces[m][0:r, plan.cols :]
+    gate_ref[half : half + plan.out_rows, :] = out_w_ref[...]
+
+
 def fill_segments(plan, s, pieces, segc_ref, segr_ref):
     per = plan.rows // GROUP
     segc_ref[...] = jnp.zeros_like(segc_ref)
@@ -175,14 +254,13 @@
         )
 
 
-def forward_kernel(plan, *refs):
+def project_kernel(plan, *refs):
     n = plan.seq
     toks, refs = refs[:n], refs[n:]
     pieces, refs = refs[:n], refs[n:]
     weights, refs = refs[: 2 * plan.line], refs[2 * plan.line :]
-    gain_ref, convw_ref, convb_ref, heads_ref = refs[:4]
-    normed_ref, w_ref, x_ref, dt_ref, y_ref, states_ref, segc_ref, segr_ref = refs[4:12]
-    wf_ref, state_ref = refs[12:]
+    gain_ref = refs[0]
+    normed_ref, w_ref, x_ref, dt_ref, segc_ref, segr_ref, wf_ref = refs[1:]
     ids = place()
     s = ids[0]
     fill_segments(plan, s, pieces, segc_ref, segr_ref)
@@ -203,9 +281,23 @@
         out = jnp.dot(low, w_ref[...], preferred_element_type=f32)
         x_ref[pl.ds(aligned(start + LEAD, 8), plan.rows), :] = out[:, : plan.mixed]
         dt_ref[pl.ds(aligned(start, plan.rows), plan.rows), :] = out[:, plan.mixed :]
-    state_ref[...] = jnp.zeros_like(state_ref)
-    convw = convw_ref[...]
-    convb = convb_ref[...]
+
+
+def scan_kernel(plan, first, last, *refs):
+    x_ref, dt_ref, segc_ref, segr_ref, conv_ref, heads_ref = refs[:6]
+    refs = refs[6:]
+    if first:
+        early_y_ref, early_states_ref, early_ref = refs[:3]
+        refs = refs[3:]
+    y_ref, states_ref, state_ref = refs
+    if first:
+        y_ref[: first * GROUP, :] = early_y_ref[...]
+        states_ref[:first] = early_states_ref[...]
+        state_ref[...] = early_ref[...]
+    else:
+        state_ref[...] = jnp.zeros_like(state_ref)
+    convw = conv_ref[0:KERNEL, :]
+    convb = conv_ref[KERNEL : KERNEL + 1, :]
 
     def step(b, carry):
         v = block_values(plan, b, x_ref, segc_ref, segr_ref, dt_ref, convw, convb, heads_ref)
@@ -229,7 +321,7 @@
         state_ref[...] = state * keep[GROUP - 1 :] + mm_tn(v["keys"], v["values"] * to_end)
         return carry
 
-    lax.fori_loop(0, plan.blocks, step, 0)
+    lax.fori_loop(first, last, step, 0)
 
 
 def gate_kernel(plan, *refs):
@@ -296,14 +388,26 @@
                 put(core_xor, line_xor, m, rows)
 
 
+def row_products(w_ref, grad_ref):
+    lane = iota((LANES, LANES), 1)
+    square = jnp.zeros((LANES, LANES), f32)
+    for i in range(w_ref.shape[0] // LANES):
+        rows = slice(i * LANES, (i + 1) * LANES)
+        product = w_ref[rows, :].astype(f32) * grad_ref[rows, :]
+        square = square + jnp.where(lane == i, jnp.sum(product, axis=1, keepdims=True), 0.0)
+    return square.T[:8]
+
+
 def regate_kernel(plan, *refs):
     n = plan.seq
     stats = refs[:n]
-    normed_ref, y_ref, z_ref, du_ref = refs[n : n + 4]
-    cots = refs[n + 4 : 2 * n + 4]
-    gain_ref = refs[2 * n + 4]
-    dy_ref, dz_ref, scale_ref, gain_out_ref, keep_ref, send_ref = refs[2 * n + 5 : 2 * n + 11]
-    gated_ref, gz_ref, go_ref = refs[2 * n + 11 :]
+    normed_ref, y_ref, z_ref, du_ref, wz_ref = refs[n : n + 5]
+    cots = refs[n + 5 : 2 * n + 5]
+    gain_ref = refs[2 * n + 5]
+    dy_ref, dz_ref, scale_ref, gain_out_ref, share_ref, keep_ref, send_ref = refs[
+        2 * n + 6 : 2 * n + 13
+    ]
+    gated_ref, gz_ref, go_ref = refs[2 * n + 13 :]
     ids = place()
     s, z, c = ids
     total = stats[0][...]
@@ -333,6 +437,7 @@
         sums = sums + jnp.sum(du * normal, axis=0, keepdims=True)
     gain_out_ref[...] = sums
     gz_ref[...] = mm_tn(normed_ref[...], dz_ref[...])
+    share_ref[...] = row_products(wz_ref, gz_ref)
     out = None
     for m in range(n):
         start = aligned((s ^ m) * plan.rows, plan.rows)
@@ -358,29 +463,33 @@
             ].astype(bf16)
 
 
-def backward_kernel(plan, *refs):
-    n = plan.seq
-    toks = refs[:n]
-    normed_ref, w_ref, wz_ref, x_ref, dt_ref, states_ref, segc_ref, segr_ref = refs[n : n + 8]
-    dy_ref, dz_ref, gain_out_ref, convw_ref, convb_ref, heads_ref = refs[n + 8 : n + 14]
-    outs = refs[n + 14 :]
-    grads, outs = outs[:n], outs[n:]
-    keep_ref, send_ref, small_ref = outs[:3]
-    gp_ref, gw_ref, gn_ref, adj_ref, edge_ref, acc_ref, head_ref = outs[3:]
-    ids = place()
-    s = ids[0]
-    convw = convw_ref[...]
-    convb = convb_ref[...]
-    adj_ref[...] = jnp.zeros_like(adj_ref)
-    edge_ref[...] = jnp.zeros_like(edge_ref)
-    acc_ref[...] = jnp.zeros_like(acc_ref)
-    head_ref[...] = jnp.zeros_like(head_ref)
+def scan_back_kernel(plan, first, last, *refs):
+    x_ref, dt_ref, states_ref, segc_ref, segr_ref, dy_ref, conv_ref, heads_ref = refs[:8]
+    refs = refs[8:]
+    later = last < plan.blocks
+    if later:
+        before, refs = refs[:5], refs[5:]
+    gp_ref, adj_ref, edge_ref, acc_ref, head_ref = refs
+    low = first * GROUP
+    if later:
+        gp_ref[(last - first) * GROUP :, :] = before[0][...]
+        adj_ref[...] = before[1][...]
+        edge_ref[...] = before[2][...]
+        acc_ref[...] = before[3][...]
+        head_ref[...] = before[4][...]
+    else:
+        adj_ref[...] = jnp.zeros_like(adj_ref)
+        edge_ref[...] = jnp.zeros_like(edge_ref)
+        acc_ref[...] = jnp.zeros_like(acc_ref)
+        head_ref[...] = jnp.zeros_like(head_ref)
+    convw = conv_ref[0:KERNEL, :]
+    convb = conv_ref[KERNEL : KERNEL + 1, :]
     repeat = plan.mixed // LANES
     pick = (iota((plan.chan, LANES), 0) // HEADDIM == iota((plan.chan, LANES), 1)).astype(f32)
     lane = iota((GROUP, LANES), 1)
 
     def step(turn, carry):
-        b = plan.blocks - 1 - turn
+        b = last - 1 - turn
         v = block_values(plan, b, x_ref, segc_ref, segr_ref, dt_ref, convw, convb, heads_ref)
         base = v["base"]
         state = states_ref[b]
@@ -461,18 +570,17 @@
                 part = part * jnp.concatenate([same] * repeat, axis=1)
             dx = dx + convw[k : k + 1] * part
         live = jnp.where(lane < plan.heads, grad_dt, 0.0)
-        gp_ref[pl.ds(base, GROUP), :] = jnp.concatenate([dx, live], axis=1).astype(bf16)
+        gp_ref[pl.ds(aligned(base - low, GROUP), GROUP), :] = jnp.concatenate([dx, live], axis=1).astype(bf16)
         return carry
 
-    lax.fori_loop(0, plan.blocks, step, 0)
-    gn_ref[...] = mm_nt(gp_ref[...], w_ref[...]) + mm_nt(dz_ref[...], wz_ref[...])
-    gain_in = jnp.zeros((1, WIDTH), f32)
-    for m in range(n):
-        tok = toks[m][...].astype(f32)
-        scale = lax.rsqrt(jnp.mean(tok * tok, axis=1, keepdims=True) + norm_eps)
-        part = gn_ref[pl.ds(aligned((s ^ m) * plan.rows, plan.rows), plan.rows), :]
-        gain_in = gain_in + jnp.sum(part * (tok * scale), axis=0, keepdims=True)
-        grads[m][...] = part.astype(grads[m].dtype)
+    lax.fori_loop(0, last - first, step, 0)
+
+
+def main_grads_kernel(
+    plan, normed_ref, gp_ref, w_ref, gain_ref, share_ref, gain_out_ref, acc_ref, head_ref,
+    keep_ref, send_ref, gw_ref, small_ref,
+):
+    ids = place()
     gw_ref[...] = mm_tn(normed_ref[...], gp_ref[...])
     both = (keep_ref, send_ref)
 
@@ -481,16 +589,53 @@
         both[core_xor][line_xor, top : top + plan.in_rows, :] = rows.astype(bf16)
 
     emit_rows(plan, ids, gw_ref, put)
+    share = share_ref[...] + row_products(w_ref, gw_ref)
     small_ref[...] = jnp.zeros_like(small_ref)
-    small_ref[0:1, :WIDTH] = gain_in
+    for i in range(WIDTH // LANES):
+        lanes = slice(i * LANES, (i + 1) * LANES)
+        small_ref[0:1, lanes] = share[i : i + 1] / gain_ref[:, lanes]
     small_ref[1:6, : plan.mixed] = acc_ref[0:5, :]
     small_ref[6:7, : plan.chan] = gain_out_ref[...]
     for j in range(3):
         small_ref[7:8, j * LANES : (j + 1) * LANES] = head_ref[j : j + 1, :]
-
-
-def add_split_kernel(count, keep_ref, got_ref, *outs):
-    for m in range(count):
+    high, low = two_parts(small_ref[...])
+    last = plan.seq * plan.in_rows
+    for ref in both:
+        for line_xor in range(plan.line):
+            ref[line_xor, last : last + 8, :] = high
+            ref[line_xor, last + 8 : last + 16, :] = low
+
+
+def normed_grads_kernel(plan, gp_ref, w_ref, dz_ref, wz_ref, *grads):
+    s = lax.axis_index("seq")
+    for m in range(plan.seq):
+        rows = pl.ds(aligned((s ^ m) * plan.rows, plan.rows), plan.rows)
+        part = mm_nt(gp_ref[rows, :], w_ref[...]) + mm_nt(dz_ref[rows, :], wz_ref[...])
+        grads[m][...] = part.astype(grads[m].dtype)
+
+
+def two_parts(value):
+    high = value.astype(bf16)
+    return high, (value - high.astype(f32)).astype(bf16)
+
+
+def joined(ref, top):
+    return ref[top : top + 8, :].astype(f32) + ref[top + 8 : top + 16, :].astype(f32)
+
+
+def main_split_kernel(plan, keep_ref, got_ref, *outs):
+    last = plan.seq * plan.in_rows
+    small = joined(keep_ref.at[0], last) + joined(got_ref.at[0], last)
+    high, low = two_parts(small)
+    for m in range(plan.line):
+        total = keep_ref[m, :last, :].astype(f32) + got_ref[m, :last, :].astype(f32)
+        outs[m][:last, :] = total.astype(bf16)
+        outs[m][last : last + 8, :] = high
+        outs[m][last + 8 :, :] = low
+
+
+def gate_split_kernel(plan, keep_ref, got_ref, *outs):
+    for m in range(plan.line):
         outs[m][...] = (keep_ref[m].astype(f32) + got_ref[m].astype(f32)).astype(bf16)
 
 
@@ -509,12 +654,19 @@
 
 def row_sum_kernel(plan, *refs):
     parts, outs = refs[: plan.line], refs[plan.line :]
+    last = plan.seq * plan.in_rows
+    small = joined(parts[0], last)
+    for part in parts[1:]:
+        small = small + joined(part, last)
+    high, low = two_parts(small)
     for m in range(plan.seq):
         rows = slice(m * plan.in_rows, (m + 1) * plan.in_rows)
         total = parts[0][rows, :].astype(f32)
         for part in parts[1:]:
             total = total + part[rows, :].astype(f32)
-        outs[m][...] = total.astype(bf16)
+        outs[m][: plan.in_rows, :] = total.astype(bf16)
+        outs[m][plan.in_rows : plan.in_rows + 8, :] = high
+        outs[m][plan.in_rows + 8 :, :] = low
 
 
 def columns_kernel(plan, *refs):
@@ -524,7 +676,7 @@
     s = lax.axis_index("seq")
     for m in range(n):
         gate_ref[m] = gates[m][...].astype(f32)
-        main_ref[m] = mains[m][...].astype(f32)
+        main_ref[m] = mains[m][: plan.in_rows, :].astype(f32)
     shared = jnp.zeros((plan.in_rows, 2 * STATE), f32)
     lane = iota((plan.in_rows, LANES), 1)
     dts = jnp.zeros((plan.in_rows, LANES), f32)
@@ -546,7 +698,7 @@
     gain_in_ref, convw_ref, convb_ref, dtb_ref, alog_ref, skip_ref, gain_out_ref, all_ref = refs[n:]
     s = lax.axis_index("seq")
     for m in range(n):
-        all_ref[m] = parts[m][...]
+        all_ref[m] = joined(parts[m], plan.in_rows)
     gain_in = jnp.zeros((1, WIDTH), f32)
     shared = jnp.zeros((5, 2 * STATE), f32)
     lane = iota((1, LANES), 1)
@@ -595,23 +747,28 @@
     out_ref[...] = grad.astype(bf16)
 
 
-def call(body, plan, outs, scratch, *args, flops=0, name=None):
+def call(body, plan, outs, scratch, *args, mib=4, micros=1, name=None, kept=0):
     shapes = [jax.ShapeDtypeStruct(shape, kind) for shape, kind in outs]
     size = sum(a.size * a.dtype.itemsize for a in args)
     size += sum(a.size * a.dtype.itemsize for a in shapes)
     return pl.pallas_call(
         functools.partial(body, plan),
         out_shape=shapes,
-        in_specs=[pl.BlockSpec(memory_space=pltpu.VMEM)] * len(args),
+        in_specs=[pl.BlockSpec(memory_space=pl.ANY)] * kept
+        + [pl.BlockSpec(memory_space=pltpu.VMEM)] * (len(args) - kept),
         out_specs=[pl.BlockSpec(memory_space=pltpu.VMEM)] * len(shapes),
-        scratch_shapes=[pltpu.VMEM(shape, kind) for shape, kind in scratch],
-        compiler_params=pltpu.CompilerParams(vmem_limit_bytes=VMEM_LIMIT),
-        cost_estimate=pl.CostEstimate(flops=flops, bytes_accessed=size, transcendentals=0),
+        scratch_shapes=[
+            pltpu.VMEM(*one) if isinstance(one, tuple) else one for one in scratch
+        ],
+        compiler_params=pltpu.CompilerParams(vmem_limit_bytes=mib * 2**20),
+        cost_estimate=pl.CostEstimate(
+            flops=micros * FLOPS_PER_MICRO, bytes_accessed=size, transcendentals=0
+        ),
         name=name,
     )(*args)
 
 
-VMEM_LIMIT = 48 * 1024 * 1024
+FLOPS_PER_MICRO = 1_000_000_000
 
 
 def swap(value, axis, by):
@@ -635,80 +792,70 @@
     s = lax.axis_index("seq")
     tok, cot = tokens[0], cotangent[0]
 
-    seg_row = jnp.pad(segments.astype(bf16), ((0, 7), (0, plan.cols + chan - rows)))
-    blocks = []
-    for g in range(n):
-        main = [
-            in_weight[:, INNER + g * chan : INNER + (g + 1) * chan],
-            in_weight[:, 2 * INNER : INNER + CONV],
-            jnp.pad(
-                in_weight[:, INNER + CONV + g * heads : INNER + CONV + (g + 1) * heads],
-                ((0, 0), (0, LANES - heads)),
-            ),
-            in_weight[:, g * chan : (g + 1) * chan],
-        ]
-        blocks.append(jnp.concatenate([jnp.concatenate(main, axis=1), seg_row], axis=0))
-    blocks = jnp.stack(blocks)
-    own = [lax.dynamic_index_in_dim(blocks, s ^ m, 0, False) for m in range(n)]
+    r = plan.in_rows
+    own = call(
+        pack_kernel, plan, [((r + 8, plan.cols + chan), bf16)] * n,
+        [
+            (in_weight.shape, bf16), (segments.shape, jnp.int32), pltpu.SemaphoreType.DMA((2,)),
+            ((n, r, plan.cols + chan), bf16),
+        ],
+        in_weight, segments, name="pack", kept=2,
+    )
     pieces = [own[0]] + [swap(own[m], "seq", m) for m in range(1, n)]
     toks = [tok] + [swap(tok, "seq", m) for m in range(1, n)]
-
-    r = plan.in_rows
-    main_shard = jnp.concatenate([p[:r, : plan.cols] for p in pieces], axis=0)
-    gate_cols = [p[:r, plan.cols :] for p in pieces]
-    gate_shard = jnp.concatenate(
-        [jnp.concatenate(gate_cols[i : i + 2], axis=1) for i in range(0, n, 2)] + [out_weight],
-        axis=0,
-    )
-
-    def spread(shard):
-        mine = [shard] + [swap(shard, "batch", 2 * m) for m in range(1, line)]
-        return mine + [swap(one, "batch", 1) for one in mine]
-
-    main_parts = spread(main_shard)
-    later = after(gate_shard, *main_parts[:line])
-    gate_parts = spread(later)
-    cot_later = after(cot, *toks)
-    cots = [cot] + [swap(cot_later, "seq", m) for m in range(1, n)]
-
-    def own_cols(value):
-        group = lax.dynamic_slice_in_dim(value, s * chan, chan, value.ndim - 1)
-        return jnp.concatenate([group, value[..., INNER:]], axis=-1)
-
-    convw = own_cols(conv_weight)
-    convb = own_cols(conv_bias)[None]
-    own_gain = lax.dynamic_slice_in_dim(gain_out, s * chan, chan, 0)[None]
-
-    def own_heads(value):
-        return lax.dynamic_slice_in_dim(value, s * heads, heads, 0)
-
-    def padded(value):
-        return jnp.pad(value, (0, chan - value.shape[0]))[None]
-
-    per_head = jnp.concatenate(
-        [
-            padded(own_heads(dt_bias)),
-            padded(own_heads(a_log)),
-            jnp.repeat(own_heads(d_skip), HEADDIM)[None],
-            jnp.zeros((5, chan), f32),
-        ],
-        axis=0,
+    main_shard, gate_shard = call(
+        regroup_kernel, plan,
+        [((n * r, plan.cols), bf16), ((n * r // 2 + plan.out_rows, WIDTH), bf16)], [],
+        *pieces, out_weight, name="regroup",
+    )
+
+    def along(shard):
+        return [shard] + [swap(shard, "batch", 2 * m) for m in range(1, line)]
+
+    def both_cores(parts):
+        return parts + [swap(one, "batch", 1) for one in parts]
+
+    main_line = along(main_shard)
+    main_parts = both_cores(main_line)
+    gate_line = along(after(gate_shard, *main_line))
+    cot_near = after(cot, *toks)
+    conv, per_head, own_gain = call(
+        own_params_kernel, plan,
+        [((8, plan.mixed), f32), ((8, chan), f32), ((1, chan), f32)], [],
+        conv_weight, conv_bias[None], dt_bias[None], a_log[None], d_skip[None], gain_out[None],
+        name="own_params",
     )
     gain_row = gain_in[None]
     total = plan.total
     seg_rows = -(-plan.blocks // 8) * 8
-    normed, w_main, x, dt_raw, y, states, segc, segr = call(
-        forward_kernel, plan,
+    normed, w_main, x, dt_raw, segc, segr = call(
+        project_kernel, plan,
         [
             ((total, WIDTH), bf16), ((WIDTH, plan.cols), bf16),
-            ((total + LEAD, plan.mixed), f32), ((total, LANES), f32), ((total, chan), f32),
-            ((plan.blocks, STATE, chan), f32), ((total + 2 * LEAD, LANES), f32),
-            ((seg_rows, GROUP), f32),
+            ((total + LEAD, plan.mixed), f32), ((total, LANES), f32),
+            ((total + 2 * LEAD, LANES), f32), ((seg_rows, GROUP), f32),
         ],
-        [((WIDTH, plan.cols), f32), ((STATE, chan), f32)],
-        *toks, *pieces, *main_parts, gain_row, convw, convb, per_head,
-        flops=2 * total * WIDTH * plan.cols, name="ssd_forward",
-    )
+        [((WIDTH, plan.cols), f32)],
+        *toks, *pieces, *main_parts, gain_row, mib=16, micros=5, name="project",
+    )
+    cot_far = after(cot, normed)
+    cots = [cot] + [swap(cot_near if m < 3 else cot_far, "seq", m) for m in range(1, n)]
+    half = plan.blocks // 2
+    state_shape = (STATE, chan)
+    scan_in = (x, dt_raw, segc, segr, conv, per_head)
+
+    def scan_part(first, last, *early):
+        return call(
+            lambda p, *refs: scan_kernel(p, first, last, *refs), plan,
+            [((last * GROUP, chan), f32), ((last,) + state_shape, f32), (state_shape, f32)], [],
+            *scan_in, *early, mib=12, micros=4, name="scan_forward",
+        )
+
+    early = list(scan_part(0, half))
+    gate_line = [after(one, early[2]) for one in gate_line]
+    gate_parts = both_cores(gate_line)
+    early[2] = after(early[2], *gate_line, *cots[1:3])
+    y, states, _ = scan_part(half, plan.blocks, *early)
     piece_shape = (rows, WIDTH)
     w_gate, z, du, stats, *outs = call(
         gate_kernel, plan,
@@ -718,64 +865,79 @@
         ] + [(piece_shape, bf16)] * n,
         [((WIDTH, chan), f32), ((chan, WIDTH), bf16)],
         normed, y, *gate_parts, *cots, own_gain,
-        flops=6 * total * WIDTH * chan, name="gate_forward",
+        mib=16, micros=6, name="gate_forward",
     )
     all_stats = [stats] + [swap(stats, "seq", m) for m in range(1, n)]
-    dy, dz, scale, gain_out_grad, keep, send = call(
+    dy, dz, scale, gain_out_grad, share, keep, send = call(
         regate_kernel, plan,
         [
             ((total, chan), f32), ((total, chan), bf16), ((total, LANES), f32), ((1, chan), f32),
+            ((8, LANES), f32),
             ((line, n * r // 2 + plan.out_rows, WIDTH), bf16),
             ((line, n * r // 2 + plan.out_rows, WIDTH), bf16),
         ],
         [((total, chan), bf16), ((WIDTH, chan), f32), ((chan, WIDTH), f32)],
-        *all_stats, normed, y, z, du, *cots, own_gain,
-        flops=4 * total * WIDTH * chan, name="gate_backward",
-    )
-
-    def reduce_line(keep, send, width):
+        *all_stats, normed, y, z, du, w_gate, *cots, own_gain,
+        mib=16, micros=6, name="gate_backward",
+    )
+
+    def reduce_line(keep, send, body, name):
         got = swap(send, "batch", 1)
-        rows_here = keep.shape[1]
         parts = call(
-            lambda count, *refs: add_split_kernel(count, *refs), line,
-            [((rows_here, width), bf16)] * line, [], keep, got, name="core_sum",
+            body, plan, [(keep.shape[1:], bf16)] * line, [], keep, got, name=name,
         )
+        return parts
+
+    def line_exchange(parts):
         return [parts[0]] + [swap(parts[m], "batch", 2 * m) for m in range(1, line)]
 
-    out_late = [after(o, dy) for o in outs[1:]]
-    out_parts = [outs[0]] + [swap(out_late[m - 1], "seq", m) for m in range(1, n)]
-    gate_lines = reduce_line(keep, send, WIDTH)
+    gate_half = reduce_line(keep, send, gate_split_kernel, "gate_core_sum")
+    gate_lines = line_exchange(gate_half)
+    dy = after(dy, *gate_half)
+    back_in = (x, dt_raw, states, segc, segr, dy, conv, per_head)
+
+    def scan_back_part(first, last, *before):
+        return call(
+            lambda p, *refs: scan_back_kernel(p, first, last, *refs), plan,
+            [
+                ((total - first * GROUP, plan.cols), bf16), (state_shape, f32),
+                ((LEAD, plan.mixed), f32), ((8, plan.mixed), f32), ((8, LANES), f32),
+            ], [],
+            *back_in, *before, mib=16, micros=10, name="scan_backward",
+        )
+
+    before = list(scan_back_part(half, plan.blocks))
+    out_far = after(outs[n - 1], before[1])
+    out_parts = [outs[0]] + [
+        swap(outs[m] if m < 3 else out_far, "seq", m) for m in range(1, n)
+    ]
     *gate_grads, shard_out = call(
         gate_sum_kernel, plan,
         [((r, chan), bf16)] * n + [((plan.out_rows, WIDTH), f32)], [], *gate_lines,
         name="gate_sum",
     )
+    before[1] = after(before[1], *gate_lines, *out_parts[1:3])
+    gp, _, _, acc, head_acc = scan_back_part(0, half, *before)
     gate_grads = [gate_grads[0]] + [swap(gate_grads[m], "seq", m) for m in range(1, n)]
     (result,) = call(
         result_kernel, plan, [(piece_shape, bf16)], [], tok, scale, *out_parts, name="result"
     )
 
-    *grads, keep, send, small = call(
-        backward_kernel, plan,
-        [(piece_shape, bf16)] * n
-        + [((line, n * r, plan.cols), bf16)] * 2
-        + [((8, max(WIDTH, plan.mixed)), f32)],
-        [
-            ((total, plan.cols), bf16), ((WIDTH, plan.cols), f32), ((total, WIDTH), f32),
-            ((STATE, chan), f32), ((LEAD, plan.mixed), f32), ((8, plan.mixed), f32),
-            ((8, LANES), f32),
-        ],
-        *toks, normed, w_main, w_gate, x, dt_raw, states, segc, segr, dy, dz, gain_out_grad,
-        convw, convb, per_head,
-        flops=2 * total * WIDTH * (2 * plan.cols + chan), name="ssd_backward",
-    )
-    main_lines = reduce_line(keep, send, plan.cols)
+    keep, send = call(
+        main_grads_kernel, plan, [((line, n * r + 16, plan.cols), bf16)] * 2,
+        [((WIDTH, plan.cols), f32), ((8, plan.cols), f32)],
+        normed, gp, w_main, gain_row, share, gain_out_grad, acc, head_acc,
+        mib=12, micros=4, name="main_grads",
+    )
+    grads = call(
+        normed_grads_kernel, plan, [(piece_shape, bf16)] * n, [], gp, w_main, dz, w_gate,
+        mib=12, micros=3, name="normed_grads",
+    )
+    main_lines = line_exchange(reduce_line(keep, send, main_split_kernel, "main_core_sum"))
+    grads = [after(one, *out_parts) for one in grads]
     grad_parts = [grads[0]] + [swap(grads[m], "seq", m) for m in range(1, n)]
-    small = small + swap(small, "batch", 1)
-    small = sum([swap(small, "batch", 2 * m) for m in range(1, line)], small)
-    small_parts = [small] + [swap(small, "seq", m) for m in range(1, n)]
     main_grads = call(
-        row_sum_kernel, plan, [((r, plan.cols), bf16)] * n, [], *main_lines, name="main_sum"
+        row_sum_kernel, plan, [((r + 16, plan.cols), bf16)] * n, [], *main_lines, name="main_sum"
     )
     main_grads = [main_grads[0]] + [swap(main_grads[m], "seq", m) for m in range(1, n)]
     (grad_tokens,) = call(
@@ -792,7 +954,7 @@
             ((1, WIDTH), f32), ((KERNEL, CONV), f32), ((1, CONV), f32), ((1, HEADS), f32),
             ((1, HEADS), f32), ((1, HEADS), f32), ((1, INNER), f32),
         ],
-        [((n,) + small.shape, f32)], *small_parts, name="small_grads",
+        [((n, 8, plan.cols), f32)], *main_grads, name="small_grads",
     )
     return (
         result[None], grad_tokens[None], shard_in, shard_out, smalls[0][0], smalls[1],

time: 203 us -> 144 us (0.71)
  local copies, waits for them, and re-layouts: 29.6 us -> 1.71 us
  starting transfers between devices: 53.2 us -> 39.3 us
  Pallas kernels: 55.9 us -> 43.5 us
  waiting for transfers between devices: 57.7 us -> 53.9 us
    unnamed x88 -> x24, local copies, waits for them, and re-layouts: 22.8 us -> 1.69 us
    ppermute x53 -> x46, starting transfers between devices: 53.2 us -> 39.3 us  [swap(): return lax.ppermute(value, axis, [(i, i ^ by) for i in range(size)])]
    pallas_call x12 -> x20, Pallas kernels: 55.9 us -> 43.5 us  [call(): pl.pallas_call(functools.partial(body, plan), out_shape=shapes, in_specs=...]
    slice x15 -> x0, local copies, waits for them, and re-layouts: 4.08 us -> none  [the longest x2 1.65 us: head_parallel(): in_weight[:, INNER + g * chan:INNER + (g + 1) * chan]]
    ppermute x53 -> x46, waiting for transfers between devices: 57.7 us -> 53.9 us  [swap(): return lax.ppermute(value, axis, [(i, i ^ by) for i in range(size)])]
  transfers between devices with their start and end apart: 53 -> 46, of which waited for: 20 -> 17; matrix products, arithmetic and copies ran while one was open for 3% -> 1% of each run, Pallas kernels for 9% -> 18%
where the time goes in v2:
time: 144 us; the launch traced here: 141 us
  waiting for transfers between devices  53.9 us (37%)
  Pallas kernels  43.5 us (30%)
  starting transfers between devices  39.3 us (27%)
  other arithmetic  1.84 us (1%)
  local copies, waits for them, and re-layouts  1.71 us (1%)
    ppermute x46, waiting for transfers between devices, swap(): return lax.ppermute(value, axis, [(i, i ^ by) for i in range(size)])  53.9 us
    pallas_call x20, Pallas kernels, call(): pl.pallas_call(functools.partial(body, plan), out_shape=shapes, in_specs=...  43.5 us
    ppermute x46, starting transfers between devices, swap(): return lax.ppermute(value, axis, [(i, i ^ by) for i in range(size)])  39.3 us
  transfers between devices with their start and end apart: 46, of which 17 were waited for; matrix products, arithmetic and copies ran while one was open for 1% of the time, Pallas kernels for 18%

profile of v2, /device:TPU:8, one launch (start us, length us, event | category | flops | bytes accessed | tf_op | source)
XLA Modules:
  0.0 141.3 jit_solution(3612677259057366079)
XLA Ops:
  6.2 2.5 %collective-permute-start.2 = (bf16[256,768]{1,0:T(8,128)(2,1)S(1)}, bf16[256,768]{1,0:T(8,128)(2,1)S(1)}, u32[]{:S(2)}, u32[]{:S(2)}) collective-permute-start(bf16[256,768]{1,0:T(8,128)(2,1)S(1)} %bitcast.10), channel_id=1, source_target_pairs={{0,24},{8,16},{16,8},{24,0},{1,25},{9,17},{17,9},{25,1},{2,26},{10... | collective-permute-start | bytes 1179656 | tf_op jit(solution)/shard_map/ppermute | solution.py:776
  9.1 7.5 %collective-permute-done.4.refs_2_.refs_6_ = bf16[32,1152]{1,0:T(8,128)(2,1)S(1)} collective-permute-done((bf16[32,1152]{1,0:T(8,128)(2,1)S(1)}, bf16[32,1152]{1,0:T(8,128)(2,1)S(1)}, u32[]{:S(2)}, u32[]{:S(2)}) %collective-permute-start.4) | collective-permute-done | bytes 73760 | tf_op jit(solution)/shard_map/ppermute | solution.py:776
  19.6 5.5 %collective-permute-done.8.refs_11_ = bf16[96,768]{1,0:T(8,128)(2,1)S(1)} collective-permute-done((bf16[96,768]{1,0:T(8,128)(2,1)S(1)}, bf16[96,768]{1,0:T(8,128)(2,1)S(1)}, u32[]{:S(2)}, u32[]{:S(2)}) %collective-permute-start.8) | collective-permute-done | bytes 147488 | tf_op jit(solution)/shard_map/ppermute | solution.py:776
  25.7 4.5 %collective-permute-done.6.refs_9_ = bf16[96,768]{1,0:T(8,128)(2,1)S(1)} collective-permute-done((bf16[96,768]{1,0:T(8,128)(2,1)S(1)}, bf16[96,768]{1,0:T(8,128)(2,1)S(1)}, u32[]{:S(2)}, u32[]{:S(2)}) %collective-permute-start.6) | collective-permute-done | bytes 147488 | tf_op jit(solution)/shard_map/ppermute | solution.py:776
  31.2 2.3 %collective-permute-start.14 = (bf16[96,768]{1,0:T(8,128)(2,1)S(1)}, bf16[96,768]{1,0:T(8,128)(2,1)S(1)}, u32[]{:S(2)}, u32[]{:S(2)}) collective-permute-start(bf16[96,768]{1,0:T(8,128)(2,1)S(1)} %get-tuple-element.116.refs_2_), channel_id=1, source_target_pairs={{0,4},{1,5},{2,6},{3,7},{4,0},{5,1},{6,2},{7,3},{8,12},{9,13},{10,... | collective-permute-start | bytes 442376 | tf_op jit(solution)/shard_map/ppermute | solution.py:776
  34.6 3.0 %collective-permute-start.17 = (bf16[256,768]{1,0:T(8,128)(2,1)S(1)}, bf16[256,768]{1,0:T(8,128)(2,1)S(1)}, u32[]{:S(2)}, u32[]{:S(2)}) collective-permute-start(bf16[256,768]{1,0:T(8,128)(2,1)S(1)} %bitcast.16), channel_id=1, source_target_pairs={{0,16},{8,24},{16,0},{24,8},{1,17},{9,25},{17,1},{25,9},{2,18},{10... | collective-permute-start | bytes 1179656 | tf_op jit(solution)/shard_map/ppermute | solution.py:776
  37.6 1.8 %project.1 = (bf16[1024,768]{1,0:T(8,128)(2,1)S(1)}, bf16[768,768]{1,0:T(8,128)(2,1)S(1)}, f32[1032,640]{1,0:T(8,128)S(1)}, f32[1024,128]{1,0:T(8,128)S(1)}, f32...) custom-call(bf16[256,768]{1,0:T(8,128)(2,1)S(1)} %bitcast.13, bf16[256,768]{1,0:T(8,128)(2,1)S(1)} %collective-permute-done.refs_1_, ...), custom_call_target="tpu_custom_call" | custom-call | flops 5000000000 | bytes 9505792 | tf_op jit(solution)/shard_map/project/pallas_call | solution.py:754
  39.4 4.6 %collective-permute-done.15.refs_5_ = bf16[96,768]{1,0:T(8,128)(2,1)S(1)} collective-permute-done((bf16[96,768]{1,0:T(8,128)(2,1)S(1)}, bf16[96,768]{1,0:T(8,128)(2,1)S(1)}, u32[]{:S(2)}, u32[]{:S(2)}) %collective-permute-start.15) | collective-permute-done | bytes 147488 | tf_op jit(solution)/shard_map/ppermute | solution.py:776
  44.6 4.1 %scan_forward.2 = (f32[512,384]{1,0:T(8,128)S(1)}, f32[4,128,384]{2,1,0:T(8,128)S(1)}, f32[128,384]{1,0:T(8,128)S(1)}) custom-call(f32[1032,640]{1,0:T(8,128)S(1)} %get-tuple-element.105.refs_0_, f32[1024,128]{1,0:T(8,128)S(1)} %get-tuple-element.106.refs_1_, f32[1040,128]{1,0:T(8,128)S(1)} %get-tuple-element.107.refs_2_.refs_3_, ...), custom_call_target="tpu_custom_call" | custom-call | flops 4000000000 | bytes 5505024 | tf_op jit(solution)/shard_map/scan_forward/pallas_call | solution.py:754
  49.8 4.9 %scan_forward.3 = (f32[1024,384]{1,0:T(8,128)S(1)}, f32[8,128,384]{2,1,0:T(8,128)S(1)}, f32[128,384]{1,0:T(8,128)}) custom-call(f32[1032,640]{1,0:T(8,128)S(1)} %get-tuple-element.105.refs_0_, f32[1024,128]{1,0:T(8,128)S(1)} %get-tuple-element.106.refs_1_, f32[1040,128]{1,0:T(8,128)S(1)} %get-tuple-element.107.refs_2_.refs_3_, ...), custom_call_target="tpu_custom_call" | custom-call | flops 4000000000 | bytes 8847360 | tf_op jit(solution)/shard_map/scan_forward/pallas_call | solution.py:754
  56.2 3.2 %gate_forward.1 = (bf16[768,384]{1,0:T(8,128)(2,1)S(1)}, f32[1024,384]{1,0:T(8,128)S(1)}, f32[1024,384]{1,0:T(8,128)S(1)}, f32[16,128]{1,0:T(8,128)S(1)}, bf16[2...) custom-call(bf16[1024,768]{1,0:T(8,128)(2,1)S(1)} %get-tuple-element, ...), custom_call_target="tpu_custom_call" | custom-call | flops 6000000000 | bytes 11216384 | tf_op jit(solution)/shard_map/gate_forward/pallas_call | solution.py:754
  60.8 2.5 %collective-permute-start.24 = (f32[16,128]{1,0:T(8,128)S(1)}, f32[16,128]{1,0:T(8,128)S(1)}, u32[]{:S(2)}, u32[]{:S(2)}) collective-permute-start(f32[16,128]{1,0:T(8,128)S(1)} %get-tuple-element.125.refs_0_), channel_id=1, source_target_pairs={{0,16},{8,24},{16,0},{24,8},{1,17},{9,25},{17,1},{25,9},{2,18},{10... | collective-permute-start | bytes 24584 | tf_op jit(solution)/shard_map/ppermute | solution.py:776
  64.9 2.0 %collective-permute-done.23.refs_1_ = f32[16,128]{1,0:T(8,128)S(1)} collective-permute-done((f32[16,128]{1,0:T(8,128)S(1)}, f32[16,128]{1,0:T(8,128)S(1)}, u32[]{:S(2)}, u32[]{:S(2)}) %collective-permute-start.23) | collective-permute-done | bytes 8224 | tf_op jit(solution)/shard_map/ppermute | solution.py:776
  66.9 3.0 %gate_backward.1 = (f32[1024,384]{1,0:T(8,128)S(1)}, bf16[1024,384]{1,0:T(8,128)(2,1)S(1)}, f32[1024,128]{1,0:T(8,128)S(1)}, f32[1,384]{1,0:T(1,128)S(1)}, f32[8...) custom-call(f32[16,128]{1,0:T(8,128)S(1)} %get-tuple-element.125.refs_0_, ...), custom_call_target="tpu_custom_call" | custom-call | flops 6000000000 | bytes 12557312 | tf_op jit(solution)/shard_map/gate_backward/pallas_call | solution.py:754
  75.6 8.5 %scan_backward.2 = (bf16[512,768]{1,0:T(8,128)(2,1)S(1)}, f32[128,384]{1,0:T(8,128)S(1)}, f32[8,640]{1,0:T(8,128)S(1)}, f32[8,640]{1,0:T(8,128)S(1)}, f32[8,128]{1,0:T(8,128)S(1)}) custom-call(f32[1032,640]{1,0:T(8,128)S(1)} %get-tuple-element.105.refs_0_, f32[1024,128]{1,0:T(8,128)S(1)} %get-tuple-element.106.refs_1_, ...), custom_call_target="tpu_custom_call" | custom-call | flops 10000000000 | bytes 7909376 | tf_op jit(solution)/shard_map/scan_backward/pallas_call | solution.py:754
  84.7 4.0 %collective-permute-done.32.refs_3_ = bf16[96,768]{1,0:T(8,128)(2,1)S(1)} collective-permute-done((bf16[96,768]{1,0:T(8,128)(2,1)S(1)}, bf16[96,768]{1,0:T(8,128)(2,1)S(1)}, u32[]{:S(2)}, u32[]{:S(2)}) %collective-permute-start.32) | collective-permute-done | bytes 147488 | tf_op jit(solution)/shard_map/ppermute | solution.py:776
  88.7 8.9 %scan_backward.3 = (bf16[1024,768]{1,0:T(8,128)(2,1)S(1)}, f32[128,384]{1,0:T(8,128)}, f32[8,640]{1,0:T(8,128)}, f32[8,640]{1,0:T(8,128)S(1)}, f32[8,128]{1,0:T(8,128)S(1)}) custom-call(f32[1032,640]{1,0:T(8,128)S(1)} %get-tuple-element.105.refs_0_, f32[1024,128]{1,0:T(8,128)S(1)} %get-tuple-element.106.refs_1_, ...), custom_call_target="tpu_custom_call" | custom-call | flops 10000000000 | bytes 9723904 | tf_op jit(solution)/shard_map/scan_backward/pallas_call | solution.py:754
  97.6 1.7 %main_grads.1 = (bf16[4,112,768]{2,1,0:T(8,128)(2,1)S(1)}, bf16[4,112,768]{2,1,0:T(8,128)(2,1)S(1)}) custom-call(bf16[1024,768]{1,0:T(8,128)(2,1)S(1)} %get-tuple-element.104.refs_0_.refs_4_.normed_ref, bf16[1024,768]{1,0:T(8,128)(2,1)S(1)} %get-tuple-element.150.gp_ref, bf16[768,768]{1,0:T(8,128)(2,1)S(1)} %get-tuple-element.151.w_ref, ...), custom_call_target="tpu_custom_call" | custom-call | flops 4000000000 | bytes 5734912 | tf_op jit(solution)/shard_map/main_grads/pallas_call | solution.py:754
  101.7 2.2 %normed_grads.1 = (bf16[256,768]{1,0:T(8,128)(2,1)S(1)}, bf16[256,768]{1,0:T(8,128)(2,1)S(1)}, bf16[256,768]{1,0:T(8,128)(2,1)S(1)}, bf16[256,768]{1,0:T(8,128)(2,1)S(1)}) custom-call(bf16[1024,768]{1,0:T(8,128)(2,1)S(1)} %get-tuple-element.150.gp_ref, bf16[768,768]{1,0:T(8,128)(2,1)S(1)} %get-tuple-element.151.w_ref, ...), custom_call_target="tpu_custom_call" | custom-call | flops 3000000000 | bytes 5701632 | tf_op jit(solution)/shard_map/normed_grads/pallas_call | solution.py:754
  104.0 7.8 %collective-permute-done.29.refs_3_ = bf16[256,768]{1,0:T(8,128)(2,1)S(1)} collective-permute-done((bf16[256,768]{1,0:T(8,128)(2,1)S(1)}, bf16[256,768]{1,0:T(8,128)(2,1)S(1)}, u32[]{:S(2)}, u32[]{:S(2)}) %collective-permute-start.29) | collective-permute-done | bytes 393248 | tf_op jit(solution)/shard_map/ppermute | solution.py:776
  112.0 1.7 %collective-permute-start.34 = (bf16[256,768]{1,0:T(8,128)(2,1)S(1)}, bf16[256,768]{1,0:T(8,128)(2,1)S(1)}, u32[]{:S(2)}, u32[]{:S(2)}) collective-permute-start(bf16[256,768]{1,0:T(8,128)(2,1)S(1)} %get-tuple-element.158), channel_id=1, source_target_pairs={{0,16},{8,24},{16,0},{24,8},{1,17},{9,25},{17,1},{25,9},{2,18},{10... | collective-permute-start | bytes 1179656 | tf_op jit(solution)/shard_map/ppermute | solution.py:776
  117.6 9.0 %collective-permute-done.41.refs_2_ = bf16[112,768]{1,0:T(8,128)(2,1)S(1)} collective-permute-done((bf16[112,768]{1,0:T(8,128)(2,1)S(1)}, bf16[112,768]{1,0:T(8,128)(2,1)S(1)}, u32[]{:S(2)}, u32[]{:S(2)}) %collective-permute-start.41) | collective-permute-done | bytes 172064 | tf_op jit(solution)/shard_map/ppermute | solution.py:776
  127.1 2.9 %collective-permute-done.42.refs_3_ = bf16[112,768]{1,0:T(8,128)(2,1)S(1)} collective-permute-done((bf16[112,768]{1,0:T(8,128)(2,1)S(1)}, bf16[112,768]{1,0:T(8,128)(2,1)S(1)}, u32[]{:S(2)}, u32[]{:S(2)}) %collective-permute-start.42) | collective-permute-done | bytes 172064 | tf_op jit(solution)/shard_map/ppermute | solution.py:776
  130.7 1.8 %collective-permute-start.43 = (bf16[40,768]{1,0:T(8,128)(2,1)S(1)}, bf16[40,768]{1,0:T(8,128)(2,1)S(1)}, u32[]{:S(2)}, u32[]{:S(2)}) collective-permute-start(bf16[40,768]{1,0:T(8,128)(2,1)S(1)} %get-tuple-element.176), channel_id=1, source_target_pairs={{0,8},{8,0},{16,24},{24,16},{1,9},{9,1},{17,25},{25,17},{2,10},{10... | collective-permute-start | bytes 184328 | tf_op jit(solution)/shard_map/ppermute | solution.py:776
  (118 shorter events, 40.6 us)
Async XLA Ops:
  4.2 12.4 %collective-permute-start.4 = (bf16[32,1152]{1,0:T(8,128)(2,1)S(1)}, bf16[32,1152]{1,0:T(8,128)(2,1)S(1)}, u32[]{:S(2)}, u32[]{:S(2)}) collective-permute-start(bf16[32,1152]{1,0:T(8,128)(2,1)S(1)} %get-tuple-element.101), channel_id=1, source_target_pairs={{0,16},{8,24},{16,0},{24,8},{1,17},{9,25},{17,1},{25,9},{2,18},{10... | collective-permute-start | bytes 221192 | tf_op jit(solution)/shard_map/ppermute | solution.py:776
  5.7 10.9 %collective-permute-start.5 = (bf16[32,1152]{1,0:T(8,128)(2,1)S(1)}, bf16[32,1152]{1,0:T(8,128)(2,1)S(1)}, u32[]{:S(2)}, u32[]{:S(2)}) collective-permute-start(bf16[32,1152]{1,0:T(8,128)(2,1)S(1)} %get-tuple-element.102), channel_id=1, source_target_pairs={{0,24},{8,16},{16,8},{24,0},{1,25},{9,17},{17,9},{25,1},{2,26},{10... | collective-permute-start | bytes 221192 | tf_op jit(solution)/shard_map/ppermute | solution.py:776
  6.2 24.0 %collective-permute-start.2 = (bf16[256,768]{1,0:T(8,128)(2,1)S(1)}, bf16[256,768]{1,0:T(8,128)(2,1)S(1)}, u32[]{:S(2)}, u32[]{:S(2)}) collective-permute-start(bf16[256,768]{1,0:T(8,128)(2,1)S(1)} %bitcast.10), channel_id=1, source_target_pairs={{0,24},{8,16},{16,8},{24,0},{1,25},{9,17},{17,9},{25,1},{2,26},{10... | collective-permute-start | bytes 1179656 | tf_op jit(solution)/shard_map/ppermute | solution.py:776
  8.6 22.1 %collective-permute-start.1 = (bf16[256,768]{1,0:T(8,128)(2,1)S(1)}, bf16[256,768]{1,0:T(8,128)(2,1)S(1)}, u32[]{:S(2)}, u32[]{:S(2)}) collective-permute-start(bf16[256,768]{1,0:T(8,128)(2,1)S(1)} %bitcast.11), channel_id=1, source_target_pairs={{0,16},{8,24},{16,0},{24,8},{1,17},{9,25},{17,1},{25,9},{2,18},{10... | collective-permute-start | bytes 1179656 | tf_op jit(solution)/shard_map/ppermute | solution.py:776
  18.3 12.7 %collective-permute-start = (bf16[256,768]{1,0:T(8,128)(2,1)S(1)}, bf16[256,768]{1,0:T(8,128)(2,1)S(1)}, u32[]{:S(2)}, u32[]{:S(2)}) collective-permute-start(bf16[256,768]{1,0:T(8,128)(2,1)S(1)} %bitcast.12), channel_id=1, source_target_pairs={{0,8},{8,0},{16,24},{24,16},{1,9},{9,1},{17,25},{25,17},{2,10},{10... | collective-permute-start | bytes 1179656 | tf_op jit(solution)/shard_map/ppermute | solution.py:776
  31.1 12.9 %collective-permute-start.15 = (bf16[96,768]{1,0:T(8,128)(2,1)S(1)}, bf16[96,768]{1,0:T(8,128)(2,1)S(1)}, u32[]{:S(2)}, u32[]{:S(2)}) collective-permute-start(bf16[96,768]{1,0:T(8,128)(2,1)S(1)} %get-tuple-element.116.refs_2_), channel_id=1, source_target_pairs={{0,6},{1,7},{2,4},{3,5},{4,2},{5,3},{6,0},{7,1},{8,14},{9,15},{10,... | collective-permute-start | bytes 442376 | tf_op jit(solution)/shard_map/ppermute | solution.py:776
  31.2 17.5 %collective-permute-start.14 = (bf16[96,768]{1,0:T(8,128)(2,1)S(1)}, bf16[96,768]{1,0:T(8,128)(2,1)S(1)}, u32[]{:S(2)}, u32[]{:S(2)}) collective-permute-start(bf16[96,768]{1,0:T(8,128)(2,1)S(1)} %get-tuple-element.116.refs_2_), channel_id=1, source_target_pairs={{0,4},{1,5},{2,6},{3,7},{4,0},{5,1},{6,2},{7,3},{8,12},{9,13},{10,... | collective-permute-start | bytes 442376 | tf_op jit(solution)/shard_map/ppermute | solution.py:776
  33.5 15.2 %collective-permute-start.13 = (bf16[96,768]{1,0:T(8,128)(2,1)S(1)}, bf16[96,768]{1,0:T(8,128)(2,1)S(1)}, u32[]{:S(2)}, u32[]{:S(2)}) collective-permute-start(bf16[96,768]{1,0:T(8,128)(2,1)S(1)} %get-tuple-element.116.refs_2_), channel_id=1, source_target_pairs={{0,2},{1,3},{2,0},{3,1},{4,6},{5,7},{6,4},{7,5},{8,10},{9,11},{10,... | collective-permute-start | bytes 442376 | tf_op jit(solution)/shard_map/ppermute | solution.py:776
  34.6 14.7 %collective-permute-start.17 = (bf16[256,768]{1,0:T(8,128)(2,1)S(1)}, bf16[256,768]{1,0:T(8,128)(2,1)S(1)}, u32[]{:S(2)}, u32[]{:S(2)}) collective-permute-start(bf16[256,768]{1,0:T(8,128)(2,1)S(1)} %bitcast.16), channel_id=1, source_target_pairs={{0,16},{8,24},{16,0},{24,8},{1,17},{9,25},{17,1},{25,9},{2,18},{10... | collective-permute-start | bytes 1179656 | tf_op jit(solution)/shard_map/ppermute | solution.py:776
  37.6 11.8 %collective-permute-start.16 = (bf16[256,768]{1,0:T(8,128)(2,1)S(1)}, bf16[256,768]{1,0:T(8,128)(2,1)S(1)}, u32[]{:S(2)}, u32[]{:S(2)}) collective-permute-start(bf16[256,768]{1,0:T(8,128)(2,1)S(1)} %bitcast.17), channel_id=1, source_target_pairs={{0,8},{8,0},{16,24},{24,16},{1,9},{9,1},{17,25},{25,17},{2,10},{10... | collective-permute-start | bytes 1179656 | tf_op jit(solution)/shard_map/ppermute | solution.py:776
  44.0 12.2 %collective-permute-start.22 = (bf16[256,768]{1,0:T(8,128)(2,1)S(1)}, bf16[256,768]{1,0:T(8,128)(2,1)S(1)}, u32[]{:S(2)}, u32[]{:S(2)}) collective-permute-start(bf16[256,768]{1,0:T(8,128)(2,1)S(1)} %bitcast.18), channel_id=1, source_target_pairs={{0,24},{8,16},{16,8},{24,0},{1,25},{9,17},{17,9},{25,1},{2,26},{10... | collective-permute-start | bytes 1179656 | tf_op jit(solution)/shard_map/ppermute | solution.py:776
  69.9 14.2 %collective-permute-start.26 = (bf16[256,768]{1,0:T(8,128)(2,1)S(1)}, bf16[256,768]{1,0:T(8,128)(2,1)S(1)}, u32[]{:S(2)}, u32[]{:S(2)}) collective-permute-start(bf16[256,768]{1,0:T(8,128)(2,1)S(1)} %get-tuple-element.131), channel_id=1, source_target_pairs={{0,8},{8,0},{16,24},{24,16},{1,9},{9,1},{17,25},{25,17},{2,10},{10... | collective-permute-start | bytes 1179656 | tf_op jit(solution)/shard_map/ppermute | solution.py:776
  70.0 14.2 %collective-permute-start.27 = (bf16[256,768]{1,0:T(8,128)(2,1)S(1)}, bf16[256,768]{1,0:T(8,128)(2,1)S(1)}, u32[]{:S(2)}, u32[]{:S(2)}) collective-permute-start(bf16[256,768]{1,0:T(8,128)(2,1)S(1)} %get-tuple-element.132), channel_id=1, source_target_pairs={{0,16},{8,24},{16,0},{24,8},{1,17},{9,25},{17,1},{25,9},{2,18},{10... | collective-permute-start | bytes 1179656 | tf_op jit(solution)/shard_map/ppermute | solution.py:776
  72.1 12.1 %collective-permute-start.30 = (bf16[96,768]{1,0:T(8,128)(2,1)S(1)}, bf16[96,768]{1,0:T(8,128)(2,1)S(1)}, u32[]{:S(2)}, u32[]{:S(2)}) collective-permute-start(bf16[96,768]{1,0:T(8,128)(2,1)S(1)} %get-tuple-element.139), channel_id=1, source_target_pairs={{0,2},{1,3},{2,0},{3,1},{4,6},{5,7},{6,4},{7,5},{8,10},{9,11},{10,... | collective-permute-start | bytes 442376 | tf_op jit(solution)/shard_map/ppermute | solution.py:776
  72.4 12.3 %collective-permute-start.31 = (bf16[96,768]{1,0:T(8,128)(2,1)S(1)}, bf16[96,768]{1,0:T(8,128)(2,1)S(1)}, u32[]{:S(2)}, u32[]{:S(2)}) collective-permute-start(bf16[96,768]{1,0:T(8,128)(2,1)S(1)} %get-tuple-element.140), channel_id=1, source_target_pairs={{0,4},{1,5},{2,6},{3,7},{4,0},{5,1},{6,2},{7,3},{8,12},{9,13},{10,... | collective-permute-start | bytes 442376 | tf_op jit(solution)/shard_map/ppermute | solution.py:776
  74.1 14.6 %collective-permute-start.32 = (bf16[96,768]{1,0:T(8,128)(2,1)S(1)}, bf16[96,768]{1,0:T(8,128)(2,1)S(1)}, u32[]{:S(2)}, u32[]{:S(2)}) collective-permute-start(bf16[96,768]{1,0:T(8,128)(2,1)S(1)} %get-tuple-element.141), channel_id=1, source_target_pairs={{0,6},{1,7},{2,4},{3,5},{4,2},{5,3},{6,0},{7,1},{8,14},{9,15},{10,... | collective-permute-start | bytes 442376 | tf_op jit(solution)/shard_map/ppermute | solution.py:776
  99.4 12.4 %collective-permute-start.29 = (bf16[256,768]{1,0:T(8,128)(2,1)S(1)}, bf16[256,768]{1,0:T(8,128)(2,1)S(1)}, u32[]{:S(2)}, u32[]{:S(2)}) collective-permute-start(bf16[256,768]{1,0:T(8,128)(2,1)S(1)} %get-tuple-element.144), channel_id=1, source_target_pairs={{0,24},{8,16},{16,8},{24,0},{1,25},{9,17},{17,9},{25,1},{2,26},{10... | collective-permute-start | bytes 1179656 | tf_op jit(solution)/shard_map/ppermute | solution.py:776
  101.6 13.6 %collective-permute-start.40 = (bf16[112,768]{1,0:T(8,128)(2,1)S(1)}, bf16[112,768]{1,0:T(8,128)(2,1)S(1)}, u32[]{:S(2)}, u32[]{:S(2)}) collective-permute-start(bf16[112,768]{1,0:T(8,128)(2,1)S(1)} %get-tuple-element.172), channel_id=1, source_target_pairs={{0,2},{1,3},{2,0},{3,1},{4,6},{5,7},{6,4},{7,5},{8,10},{9,11},{10,... | collective-permute-start | bytes 516104 | tf_op jit(solution)/shard_map/ppermute | solution.py:776
  111.8 18.9 %collective-permute-start.33 = (bf16[256,768]{1,0:T(8,128)(2,1)S(1)}, bf16[256,768]{1,0:T(8,128)(2,1)S(1)}, u32[]{:S(2)}, u32[]{:S(2)}) collective-permute-start(bf16[256,768]{1,0:T(8,128)(2,1)S(1)} %get-tuple-element.156), channel_id=1, source_target_pairs={{0,8},{8,0},{16,24},{24,16},{1,9},{9,1},{17,25},{25,17},{2,10},{10... | collective-permute-start | bytes 1179656 | tf_op jit(solution)/shard_map/ppermute | solution.py:776
  112.0 20.6 %collective-permute-start.34 = (bf16[256,768]{1,0:T(8,128)(2,1)S(1)}, bf16[256,768]{1,0:T(8,128)(2,1)S(1)}, u32[]{:S(2)}, u32[]{:S(2)}) collective-permute-start(bf16[256,768]{1,0:T(8,128)(2,1)S(1)} %get-tuple-element.158), channel_id=1, source_target_pairs={{0,16},{8,24},{16,0},{24,8},{1,17},{9,25},{17,1},{25,9},{2,18},{10... | collective-permute-start | bytes 1179656 | tf_op jit(solution)/shard_map/ppermute | solution.py:776
  113.7 19.1 %collective-permute-start.35 = (bf16[256,768]{1,0:T(8,128)(2,1)S(1)}, bf16[256,768]{1,0:T(8,128)(2,1)S(1)}, u32[]{:S(2)}, u32[]{:S(2)}) collective-permute-start(bf16[256,768]{1,0:T(8,128)(2,1)S(1)} %get-tuple-element.160), channel_id=1, source_target_pairs={{0,24},{8,16},{16,8},{24,0},{1,25},{9,17},{17,9},{25,1},{2,26},{10... | collective-permute-start | bytes 1179656 | tf_op jit(solution)/shard_map/ppermute | solution.py:776
  115.3 11.3 %collective-permute-start.41 = (bf16[112,768]{1,0:T(8,128)(2,1)S(1)}, bf16[112,768]{1,0:T(8,128)(2,1)S(1)}, u32[]{:S(2)}, u32[]{:S(2)}) collective-permute-start(bf16[112,768]{1,0:T(8,128)(2,1)S(1)} %get-tuple-element.173), channel_id=1, source_target_pairs={{0,4},{1,5},{2,6},{3,7},{4,0},{5,1},{6,2},{7,3},{8,12},{9,13},{10,... | collective-permute-start | bytes 516104 | tf_op jit(solution)/shard_map/ppermute | solution.py:776
  115.3 14.7 %collective-permute-start.42 = (bf16[112,768]{1,0:T(8,128)(2,1)S(1)}, bf16[112,768]{1,0:T(8,128)(2,1)S(1)}, u32[]{:S(2)}, u32[]{:S(2)}) collective-permute-start(bf16[112,768]{1,0:T(8,128)(2,1)S(1)} %get-tuple-element.174), channel_id=1, source_target_pairs={{0,6},{1,7},{2,4},{3,5},{4,2},{5,3},{6,0},{7,1},{8,14},{9,15},{10,... | collective-permute-start | bytes 516104 | tf_op jit(solution)/shard_map/ppermute | solution.py:776
  126.6 13.8 %collective-permute-start.36 = (bf16[24,384]{1,0:T(8,128)(2,1)S(1)}, bf16[24,384]{1,0:T(8,128)(2,1)S(1)}, u32[]{:S(2)}, u32[]{:S(2)}) collective-permute-start(bf16[24,384]{1,0:T(8,128)(2,1)S(1)} %get-tuple-element.162), channel_id=1, source_target_pairs={{0,8},{8,0},{16,24},{24,16},{1,9},{9,1},{17,25},{25,17},{2,10},{10... | collective-permute-start | bytes 55304 | tf_op jit(solution)/shard_map/ppermute | solution.py:776
  (34 other events, 241.1 us)

commit v3 on v2

--- a/solution.py
+++ b/solution.py
@@ -43,8 +43,15 @@
     )
 
 
-def mm_exact(a, b):
-    return jnp.dot(a, b, precision=highest, preferred_element_type=f32)
+def two_parts(value):
+    high = value.astype(bf16)
+    return high, (value - high.astype(f32)).astype(bf16)
+
+
+def mask_mm(mask, value):
+    width = value.shape[1]
+    out = mm(mask, jnp.concatenate(two_parts(value), axis=1))
+    return out[:, :width] + out[:, width:]
 
 
 def iota(shape, dim):
@@ -55,15 +62,13 @@
     return pl.multiple_of(value, unit)
 
 
-def wide(columns, count):
-    rows = columns.shape[0]
-    low = iota((rows, LANES), 1) < HEADDIM
-    parts = []
-    for pair in range(count // 2):
-        left = jnp.broadcast_to(columns[:, 2 * pair : 2 * pair + 1], (rows, LANES))
-        right = jnp.broadcast_to(columns[:, 2 * pair + 1 : 2 * pair + 2], (rows, LANES))
-        parts.append(jnp.where(low, left, right))
-    return jnp.concatenate(parts, axis=1)
+def wide(columns, chan):
+    half = LANES // 2
+    high, low = two_parts(columns)
+    low = pltpu.roll(low.astype(f32), half, 1)
+    both = jnp.where(iota(columns.shape, 1) < half, high.astype(f32), low)
+    spread = iota((LANES, chan), 1) // HEADDIM == lax.rem(iota((LANES, chan), 0), half)
+    return mm(both, spread.astype(f32))
 
 
 def softplus(value):
@@ -71,7 +76,7 @@
 
 
 def sigmoid(value):
-    return 1.0 / (1.0 + jnp.exp(-value))
+    return 0.5 + 0.5 * jnp.tanh(0.5 * value)
 
 
 class Plan:
@@ -130,9 +135,11 @@
     row = iota((GROUP, GROUP), 0)
     col = iota((GROUP, GROUP), 1)
     tri = (row >= col).astype(f32)
-    cum = mm_exact(tri, decay)
-    cum_t = cum.T
-    steps_t = steps.T
+    cum = mask_mm(tri, decay)
+    half = LANES // 2
+    turned = jnp.where(col < half, cum, pltpu.roll(steps, half, 1)).T
+    cum_t = turned[:half]
+    steps_t = turned[half:]
     segr = segr_ref[pl.ds(b, 1), :]
     allowed = (seg == segr) & (row >= col)
     scores = mm_nt(queries, keys)
@@ -220,7 +227,8 @@
     heads_ref[...] = jnp.zeros_like(heads_ref)
     heads_ref[0:1, :LANES] = own_heads(dtb_ref)
     heads_ref[1:2, :LANES] = own_heads(alog_ref)
-    heads_ref[2:3, :] = wide(own_heads(skip_ref), heads)
+    skip = jnp.broadcast_to(own_heads(skip_ref), (8, LANES))
+    heads_ref[2:3, :] = wide(skip, chan)[0:1]
 
 
 def regroup_kernel(plan, *refs):
@@ -314,14 +322,16 @@
                 mm(jnp.concatenate(weights_pair, axis=1), split_pair(v["values"][:, lanes]))
             )
         inside = jnp.concatenate(parts, axis=1)
-        keep = wide(v["keep"], plan.heads)
+        spread = wide(
+            jnp.concatenate([v["keep"], v["to_last"] * v["steps"]], axis=0), plan.chan
+        )
+        keep, to_end = spread[:GROUP], spread[GROUP:]
         carried = mm(v["queries"], state) * keep
         y_ref[pl.ds(v["base"], GROUP), :] = inside + carried + heads_ref[2:3, :] * v["values"]
-        to_end = wide(v["to_last"] * v["steps"], plan.heads)
         state_ref[...] = state * keep[GROUP - 1 :] + mm_tn(v["keys"], v["values"] * to_end)
         return carry
 
-    lax.fori_loop(first, last, step, 0)
+    lax.fori_loop(first, last, step, 0, unroll=True)
 
 
 def gate_kernel(plan, *refs):
@@ -496,8 +506,10 @@
         adj = adj_ref[...]
         dy = dy_ref[pl.ds(base, GROUP), :]
         values = v["values"]
-        keep = wide(v["keep"], plan.heads)
-        to_end = wide(v["to_last"] * v["steps"], plan.heads)
+        spread = wide(
+            jnp.concatenate([v["keep"], v["to_last"] * v["steps"]], axis=0), plan.chan
+        )
+        keep, to_end = spread[:GROUP], spread[GROUP:]
         kept = dy * keep
         dq = mm_nt(kept, state)
         cross = kept * mm(v["queries"], state)
@@ -508,11 +520,13 @@
         pushed = fed * values
         skipped = jnp.sum(dy * values, axis=0, keepdims=True)
         few = jnp.concatenate([ended, skipped, jnp.zeros((6, plan.chan), f32)], axis=0)
-        sums = mm_exact(jnp.concatenate([cross, pushed, few], axis=0), pick)
+        high = few.astype(bf16).astype(f32)
+        sums = mm(jnp.concatenate([cross, pushed, high, few - high], axis=0), pick)
         cross_h = sums[:GROUP]
         pushed_h = sums[GROUP : 2 * GROUP]
-        ended_h = sums[2 * GROUP : 2 * GROUP + 1]
-        skipped_h = sums[2 * GROUP + 1 : 2 * GROUP + 2]
+        few_h = sums[2 * GROUP : 2 * GROUP + 8] + sums[2 * GROUP + 8 :]
+        ended_h = few_h[0:1]
+        skipped_h = few_h[1:2]
         grad_steps = pushed_h * v["to_last"]
         pulled = grad_steps * v["steps"]
         dcum = cross_h - pulled
@@ -545,9 +559,7 @@
         dcum = dcum + jnp.where(row == GROUP - 1, at_end, 0.0)
         dk = dk + mm_tn(dscores, v["queries"])
         dq = dq + mm(dscores, v["keys"])
-        ddecay = lax.dot_general(
-            v["tri"], dcum, contract_first, precision=highest, preferred_element_type=f32
-        )
+        ddecay = mask_mm(iota((GROUP, GROUP), 0) <= iota((GROUP, GROUP), 1), dcum)
         grad_steps = grad_steps - ddecay * jnp.exp(heads_ref[1:2, :LANES])
         grad_dt = grad_steps * sigmoid(v["dt_in"])
         head_ref[0:1, :] += jnp.sum(grad_dt, axis=0, keepdims=True)
@@ -573,7 +585,7 @@
         gp_ref[pl.ds(aligned(base - low, GROUP), GROUP), :] = jnp.concatenate([dx, live], axis=1).astype(bf16)
         return carry
 
-    lax.fori_loop(0, last - first, step, 0)
+    lax.fori_loop(0, last - first, step, 0, unroll=True)
 
 
 def main_grads_kernel(
@@ -614,11 +626,6 @@
         grads[m][...] = part.astype(grads[m].dtype)
 
 
-def two_parts(value):
-    high = value.astype(bf16)
-    return high, (value - high.astype(f32)).astype(bf16)
-
-
 def joined(ref, top):
     return ref[top : top + 8, :].astype(f32) + ref[top + 8 : top + 16, :].astype(f32)
 
@@ -640,87 +647,80 @@
 
 
 def gate_sum_kernel(plan, *refs):
-    parts, outs = refs[: plan.line], refs[plan.line :]
+    parts, (gate_ref, out_ref) = refs[: plan.line], refs[plan.line :]
     total = parts[0][...].astype(f32)
     for part in parts[1:]:
         total = total + part[...].astype(f32)
     half = plan.in_rows * plan.seq // 2
-    for m in range(plan.seq):
-        top = (m // 2) * plan.in_rows
-        left = (m % 2) * plan.chan
-        outs[m][...] = total[top : top + plan.in_rows, left : left + plan.chan].astype(bf16)
-    outs[plan.seq][...] = total[half : half + plan.out_rows]
-
-
-def row_sum_kernel(plan, *refs):
+    gate_ref[...] = total[:half].astype(bf16)
+    out_ref[...] = total[half : half + plan.out_rows]
+
+
+def row_sum_kernel(plan, gate_ref, *refs):
     parts, outs = refs[: plan.line], refs[plan.line :]
-    last = plan.seq * plan.in_rows
+    r, chan = plan.in_rows, plan.chan
+    last = plan.seq * r
     small = joined(parts[0], last)
     for part in parts[1:]:
         small = small + joined(part, last)
     high, low = two_parts(small)
     for m in range(plan.seq):
-        rows = slice(m * plan.in_rows, (m + 1) * plan.in_rows)
+        rows = slice(m * r, (m + 1) * r)
         total = parts[0][rows, :].astype(f32)
         for part in parts[1:]:
             total = total + part[rows, :].astype(f32)
-        outs[m][: plan.in_rows, :] = total.astype(bf16)
-        outs[m][plan.in_rows : plan.in_rows + 8, :] = high
-        outs[m][plan.in_rows + 8 :, :] = low
+        outs[m][:r, :] = total.astype(bf16)
+        outs[m][r : r + 8, :] = high
+        outs[m][r + 8 : r + 16, :] = low
+        top, left = (m // 2) * r, (m % 2) * chan
+        outs[m][r + 16 :, :chan] = gate_ref[top : top + r, left : left + chan]
+        outs[m][r + 16 :, chan:] = jnp.zeros((r, plan.cols - chan), bf16)
 
 
 def columns_kernel(plan, *refs):
-    n = plan.seq
-    gates, mains = refs[:n], refs[n : 2 * n]
-    out_ref, gate_ref, main_ref = refs[2 * n :]
+    n, r, chan, heads = plan.seq, plan.in_rows, plan.chan, plan.heads
+    parts, refs = refs[:n], refs[n:]
+    out_ref, gain_in_ref, convw_ref, convb_ref, dtb_ref, alog_ref, skip_ref = refs[:7]
+    gain_out_ref, gate_ref, main_ref, small_ref = refs[7:]
     s = lax.axis_index("seq")
     for m in range(n):
-        gate_ref[m] = gates[m][...].astype(f32)
-        main_ref[m] = mains[m][: plan.in_rows, :].astype(f32)
-    shared = jnp.zeros((plan.in_rows, 2 * STATE), f32)
-    lane = iota((plan.in_rows, LANES), 1)
-    dts = jnp.zeros((plan.in_rows, LANES), f32)
+        main_ref[m] = parts[m][:r, :].astype(f32)
+        small_ref[m] = joined(parts[m], r)
+        gate_ref[m] = parts[m][r + 16 :, :chan].astype(f32)
+    shared = jnp.zeros((r, 2 * STATE), f32)
+    lane = iota((r, LANES), 1)
+    dts = jnp.zeros((r, LANES), f32)
+    gain_in = jnp.zeros((1, WIDTH), f32)
+    small_shared = jnp.zeros((5, 2 * STATE), f32)
+    one_lane = iota((1, LANES), 1)
+    rows = [jnp.zeros((1, LANES), f32) for _ in range(3)]
     for g in range(n):
-        out_ref[:, g * plan.chan : (g + 1) * plan.chan] = gate_ref[s ^ g]
+        cols = slice(g * chan, (g + 1) * chan)
+        out_ref[:, cols] = gate_ref[s ^ g]
         main = main_ref[s ^ g]
-        out_ref[:, INNER + g * plan.chan : INNER + (g + 1) * plan.chan] = main[:, : plan.chan]
-        shared = shared + main[:, plan.chan : plan.mixed]
+        out_ref[:, INNER + g * chan : INNER + (g + 1) * chan] = main[:, :chan]
+        shared = shared + main[:, chan : plan.mixed]
         one = main[:, plan.mixed :]
-        moved = one if g == 0 else pltpu.roll(one, g * plan.heads, 1)
-        dts = jnp.where(lane // plan.heads == g, moved, dts)
+        moved = one if g == 0 else pltpu.roll(one, g * heads, 1)
+        dts = jnp.where(lane // heads == g, moved, dts)
+        part = small_ref[s ^ g]
+        gain_in = gain_in + part[0:1, :WIDTH]
+        convw_ref[:, cols] = part[1:5, :chan]
+        convb_ref[cols] = part[5, :chan]
+        gain_out_ref[cols] = part[6, :chan]
+        small_shared = small_shared + part[1:6, chan : plan.mixed]
+        for j in range(3):
+            one = part[7:8, j * LANES : (j + 1) * LANES]
+            moved = one if g == 0 else pltpu.roll(one, g * heads, 1)
+            rows[j] = jnp.where(one_lane // heads == g, moved, rows[j])
     out_ref[:, 2 * INNER : INNER + CONV] = shared
     out_ref[:, INNER + CONV :] = dts[:, :HEADS]
-
-
-def small_kernel(plan, *refs):
-    n = plan.seq
-    parts = refs[:n]
-    gain_in_ref, convw_ref, convb_ref, dtb_ref, alog_ref, skip_ref, gain_out_ref, all_ref = refs[n:]
-    s = lax.axis_index("seq")
-    for m in range(n):
-        all_ref[m] = joined(parts[m], plan.in_rows)
-    gain_in = jnp.zeros((1, WIDTH), f32)
-    shared = jnp.zeros((5, 2 * STATE), f32)
-    lane = iota((1, LANES), 1)
-    heads = [jnp.zeros((1, LANES), f32) for _ in range(3)]
-    for g in range(n):
-        part = all_ref[s ^ g]
-        gain_in = gain_in + part[0:1, :WIDTH]
-        cols = slice(g * plan.chan, (g + 1) * plan.chan)
-        convw_ref[:, cols] = part[1:5, : plan.chan]
-        convb_ref[:, cols] = part[5:6, : plan.chan]
-        gain_out_ref[:, cols] = part[6:7, : plan.chan]
-        shared = shared + part[1:6, plan.chan : plan.mixed]
-        for j in range(3):
-            one = part[7:8, j * LANES : (j + 1) * LANES]
-            moved = one if g == 0 else pltpu.roll(one, g * plan.heads, 1)
-            heads[j] = jnp.where(lane // plan.heads == g, moved, heads[j])
-    gain_in_ref[...] = gain_in
-    convw_ref[:, INNER:] = shared[:4]
-    convb_ref[:, INNER:] = shared[4:]
-    dtb_ref[...] = heads[0][:, :HEADS]
-    alog_ref[...] = heads[1][:, :HEADS]
-    skip_ref[...] = heads[2][:, :HEADS]
+    gain_in_ref[...] = gain_in[0]
+    convw_ref[:, INNER:] = small_shared[:4]
+    convb_ref[INNER:] = small_shared[4]
+    dtb_ref[...] = rows[0][:, :HEADS]
+    alog_ref[...] = rows[1][:, :HEADS]
+    skip_ref[...] = rows[2][:, :HEADS]
 
 
 def result_kernel(plan, tok_ref, scale_ref, *refs):
@@ -754,7 +754,7 @@
     return pl.pallas_call(
         functools.partial(body, plan),
         out_shape=shapes,
-        in_specs=[pl.BlockSpec(memory_space=pl.ANY)] * kept
+        in_specs=[pl.BlockSpec(memory_space=pltpu.HBM)] * kept
         + [pl.BlockSpec(memory_space=pltpu.VMEM)] * (len(args) - kept),
         out_specs=[pl.BlockSpec(memory_space=pltpu.VMEM)] * len(shapes),
         scratch_shapes=[
@@ -799,10 +799,11 @@
             (in_weight.shape, bf16), (segments.shape, jnp.int32), pltpu.SemaphoreType.DMA((2,)),
             ((n, r, plan.cols + chan), bf16),
         ],
-        in_weight, segments, name="pack", kept=2,
+        in_weight, segments, mib=60, name="pack", kept=2,
     )
     pieces = [own[0]] + [swap(own[m], "seq", m) for m in range(1, n)]
-    toks = [tok] + [swap(tok, "seq", m) for m in range(1, n)]
+    tok_later = after(tok, *pieces)
+    toks = [tok] + [swap(tok_later, "seq", m) for m in range(1, n)]
     main_shard, gate_shard = call(
         regroup_kernel, plan,
         [((n * r, plan.cols), bf16), ((n * r // 2 + plan.out_rows, WIDTH), bf16)], [],
@@ -886,13 +887,12 @@
         parts = call(
             body, plan, [(keep.shape[1:], bf16)] * line, [], keep, got, name=name,
         )
-        return parts
+        return list(parts)
 
     def line_exchange(parts):
         return [parts[0]] + [swap(parts[m], "batch", 2 * m) for m in range(1, line)]
 
     gate_half = reduce_line(keep, send, gate_split_kernel, "gate_core_sum")
-    gate_lines = line_exchange(gate_half)
     dy = after(dy, *gate_half)
     back_in = (x, dt_raw, states, segc, segr, dy, conv, per_head)
 
@@ -907,58 +907,56 @@
         )
 
     before = list(scan_back_part(half, plan.blocks))
-    out_far = after(outs[n - 1], before[1])
-    out_parts = [outs[0]] + [
-        swap(outs[m] if m < 3 else out_far, "seq", m) for m in range(1, n)
-    ]
-    *gate_grads, shard_out = call(
+    out_parts = [outs[0]] + [swap(outs[m], "seq", m) for m in range(1, n)]
+    gate_half[-1] = after(gate_half[-1], before[1])
+    gate_lines = line_exchange(gate_half)
+    gate_rows, shard_out = call(
         gate_sum_kernel, plan,
-        [((r, chan), bf16)] * n + [((plan.out_rows, WIDTH), f32)], [], *gate_lines,
+        [((n * r // 2, WIDTH), bf16), ((plan.out_rows, WIDTH), f32)], [], *gate_lines,
         name="gate_sum",
     )
-    before[1] = after(before[1], *gate_lines, *out_parts[1:3])
+    before[1] = after(before[1], *gate_lines[:-1])
     gp, _, _, acc, head_acc = scan_back_part(0, half, *before)
-    gate_grads = [gate_grads[0]] + [swap(gate_grads[m], "seq", m) for m in range(1, n)]
     (result,) = call(
         result_kernel, plan, [(piece_shape, bf16)], [], tok, scale, *out_parts, name="result"
     )
 
+    grads = call(
+        normed_grads_kernel, plan, [(piece_shape, bf16)] * n, [], gp, w_main, dz, w_gate,
+        mib=12, micros=3, name="normed_grads",
+    )
+    gp_late = after(gp, *out_parts, *gate_lines, *grads)
     keep, send = call(
         main_grads_kernel, plan, [((line, n * r + 16, plan.cols), bf16)] * 2,
         [((WIDTH, plan.cols), f32), ((8, plan.cols), f32)],
-        normed, gp, w_main, gain_row, share, gain_out_grad, acc, head_acc,
+        normed, gp_late, w_main, gain_row, share, gain_out_grad, acc, head_acc,
         mib=12, micros=4, name="main_grads",
     )
-    grads = call(
-        normed_grads_kernel, plan, [(piece_shape, bf16)] * n, [], gp, w_main, dz, w_gate,
-        mib=12, micros=3, name="normed_grads",
-    )
-    main_lines = line_exchange(reduce_line(keep, send, main_split_kernel, "main_core_sum"))
-    grads = [after(one, *out_parts) for one in grads]
+    main_half = reduce_line(keep, send, main_split_kernel, "main_core_sum")
+    main_lines = line_exchange(main_half)
     grad_parts = [grads[0]] + [swap(grads[m], "seq", m) for m in range(1, n)]
-    main_grads = call(
-        row_sum_kernel, plan, [((r + 16, plan.cols), bf16)] * n, [], *main_lines, name="main_sum"
-    )
-    main_grads = [main_grads[0]] + [swap(main_grads[m], "seq", m) for m in range(1, n)]
+    last = call(
+        row_sum_kernel, plan, [((2 * r + 16, plan.cols), bf16)] * n, [], gate_rows, *main_lines,
+        name="main_sum",
+    )
+    last = [last[0]] + [swap(last[m], "seq", m) for m in range(1, n)]
     (grad_tokens,) = call(
         token_kernel, plan, [(piece_shape, bf16)], [], tok, cot, gain_row, *grad_parts,
         name="token_grad",
     )
-    (shard_in,) = call(
-        columns_kernel, plan, [((r, in_weight.shape[1]), f32)],
-        [((n, r, chan), f32), ((n, r, plan.cols), f32)], *gate_grads, *main_grads, name="columns",
-    )
-    smalls = call(
-        small_kernel, plan,
+    shard_in, *smalls = call(
+        columns_kernel, plan,
         [
-            ((1, WIDTH), f32), ((KERNEL, CONV), f32), ((1, CONV), f32), ((1, HEADS), f32),
-            ((1, HEADS), f32), ((1, HEADS), f32), ((1, INNER), f32),
+            ((r, in_weight.shape[1]), f32),
+            ((WIDTH,), f32), ((KERNEL, CONV), f32), ((CONV,), f32), ((1, HEADS), f32),
+            ((1, HEADS), f32), ((1, HEADS), f32), ((INNER,), f32),
         ],
-        [((n, 8, plan.cols), f32)], *main_grads, name="small_grads",
+        [((n, r, chan), f32), ((n, r, plan.cols), f32), ((n, 8, plan.cols), f32)],
+        *last, name="columns",
     )
     return (
-        result[None], grad_tokens[None], shard_in, shard_out, smalls[0][0], smalls[1],
-        smalls[2][0], smalls[3][0], smalls[4][0], smalls[5][0], smalls[6][0],
+        result[None], grad_tokens[None], shard_in, shard_out, smalls[0], smalls[1],
+        smalls[2], smalls[3][0], smalls[4][0], smalls[5][0], smalls[6],
     )
 
 

time: 144 us -> 128 us (0.89); the launches traced: 141 us -> 127 us
  waiting for transfers between devices: 53.9 us -> 43.8 us
  Pallas kernels: 43.5 us -> 41 us
  other arithmetic: 1.84 us -> 0 us
    ppermute x46 -> x43, waiting for transfers between devices: 53.9 us -> 43.8 us  [swap(): return lax.ppermute(value, axis, [(i, i ^ by) for i in range(size)])]
    pallas_call x20 -> x19, Pallas kernels: 43.5 us -> 41 us  [call(): pl.pallas_call(functools.partial(body, plan), out_shape=shapes, in_specs=...]
    pallas_call x3 -> x0, other arithmetic: 1.84 us -> none  [call(): pl.pallas_call(functools.partial(body, plan), out_shape=shapes, in_specs=...]
    ppermute x46 -> x43, starting transfers between devices: 39.3 us -> 40.6 us  [swap(): return lax.ppermute(value, axis, [(i, i ^ by) for i in range(size)])]
  transfers between devices with their start and end apart: 46 -> 43, of which waited for: 17 -> 14; matrix products, arithmetic and copies ran while one was open for 1% -> 0% of each run, Pallas kernels for 18% -> 24%
where the time goes in v3:
time: 128 us; the launch traced here: 127 us
  waiting for transfers between devices  43.8 us (34%)
  Pallas kernels  41 us (32%)
  starting transfers between devices  40.6 us (32%)
    ppermute x43, waiting for transfers between devices, swap(): return lax.ppermute(value, axis, [(i, i ^ by) for i in range(size)])  43.8 us
    pallas_call x19, Pallas kernels, call(): pl.pallas_call(functools.partial(body, plan), out_shape=shapes, in_specs=...  41 us
    ppermute x43, starting transfers between devices, swap(): return lax.ppermute(value, axis, [(i, i ^ by) for i in range(size)])  40.6 us
  transfers between devices with their start and end apart: 43, of which 14 were waited for; matrix products, arithmetic and copies ran while one was open for 0% of the time, Pallas kernels for 24%

profile of v3, /device:TPU:8, one launch (start us, length us, event | category | flops | bytes accessed | tf_op | source)
XLA Modules:
  0.0 127.3 jit_solution(9391055876802650726)
XLA Ops:
  0.7 1.8 %pack.1 = (bf16[32,1152]{1,0:T(8,128)(2,1)}, bf16[32,1152]{1,0:T(8,128)(2,1)}, bf16[32,1152]{1,0:T(8,128)(2,1)}, bf16[32,1152]{1,0:T(8,128)(2,1)}) custom-call(bf16[24,3352]{1,0:T(8,128)(2,1)} %w_any.1, s32[1,256]{1,0:T(1,128)} %seg_any.1), custom_call_target="tpu_custom_call" | custom-call | flops 1000000000 | bytes 456832 | tf_op jit(solution)/shard_map/pack/pallas_call | solution.py:754
  8.6 2.4 %collective-permute-done.2.refs_3_.refs_7_ = bf16[32,1152]{1,0:T(8,128)(2,1)S(1)} collective-permute-done((bf16[32,1152]{1,0:T(8,128)(2,1)}, bf16[32,1152]{1,0:T(8,128)(2,1)S(1)}, u32[]{:S(2)}, u32[]{:S(2)}) %collective-permute-start.2) | collective-permute-done | bytes 73760 | tf_op jit(solution)/shard_map/ppermute | solution.py:776
  18.4 7.2 %collective-permute-done.8.refs_11_ = bf16[96,768]{1,0:T(8,128)(2,1)S(1)} collective-permute-done((bf16[96,768]{1,0:T(8,128)(2,1)S(1)}, bf16[96,768]{1,0:T(8,128)(2,1)S(1)}, u32[]{:S(2)}, u32[]{:S(2)}) %collective-permute-start.8) | collective-permute-done | bytes 147488 | tf_op jit(solution)/shard_map/ppermute | solution.py:776
  26.8 4.0 %collective-permute-done.6.refs_9_ = bf16[96,768]{1,0:T(8,128)(2,1)S(1)} collective-permute-done((bf16[96,768]{1,0:T(8,128)(2,1)S(1)}, bf16[96,768]{1,0:T(8,128)(2,1)S(1)}, u32[]{:S(2)}, u32[]{:S(2)}) %collective-permute-start.6) | collective-permute-done | bytes 147488 | tf_op jit(solution)/shard_map/ppermute | solution.py:776
  31.7 2.1 %collective-permute-start.15 = (bf16[96,768]{1,0:T(8,128)(2,1)S(1)}, bf16[96,768]{1,0:T(8,128)(2,1)S(1)}, u32[]{:S(2)}, u32[]{:S(2)}) collective-permute-start(bf16[96,768]{1,0:T(8,128)(2,1)S(1)} %get-tuple-element.113.refs_2_), channel_id=1, source_target_pairs={{0,6},{1,7},{2,4},{3,5},{4,2},{5,3},{6,0},{7,1},{8,14},{9,15},{10,... | collective-permute-start | bytes 442376 | tf_op jit(solution)/shard_map/ppermute | solution.py:776
  37.0 1.8 %project.1 = (bf16[1024,768]{1,0:T(8,128)(2,1)S(1)}, bf16[768,768]{1,0:T(8,128)(2,1)S(1)}, f32[1032,640]{1,0:T(8,128)S(1)}, f32[1024,128]{1,0:T(8,128)S(1)}, f32...) custom-call(bf16[256,768]{1,0:T(8,128)(2,1)S(1)} %bitcast.13, bf16[256,768]{1,0:T(8,128)(2,1)S(1)} %collective-permute-done.3.refs_1_, ...), custom_call_target="tpu_custom_call" | custom-call | flops 5000000000 | bytes 9505792 | tf_op jit(solution)/shard_map/project/pallas_call | solution.py:754
  38.8 5.9 %collective-permute-done.15.refs_5_ = bf16[96,768]{1,0:T(8,128)(2,1)S(1)} collective-permute-done((bf16[96,768]{1,0:T(8,128)(2,1)S(1)}, bf16[96,768]{1,0:T(8,128)(2,1)S(1)}, u32[]{:S(2)}, u32[]{:S(2)}) %collective-permute-start.15) | collective-permute-done | bytes 147488 | tf_op jit(solution)/shard_map/ppermute | solution.py:776
  45.8 3.4 %scan_forward.2 = (f32[512,384]{1,0:T(8,128)S(1)}, f32[4,128,384]{2,1,0:T(8,128)S(1)}, f32[128,384]{1,0:T(8,128)S(1)}) custom-call(f32[1032,640]{1,0:T(8,128)S(1)} %get-tuple-element.102.refs_0_, f32[1024,128]{1,0:T(8,128)S(1)} %get-tuple-element.103.refs_1_, f32[1040,128]{1,0:T(8,128)S(1)} %get-tuple-element.104.refs_2_.refs_3_, ...), custom_call_target="tpu_custom_call" | custom-call | flops 4000000000 | bytes 5505024 | tf_op jit(solution)/shard_map/scan_forward/pallas_call | solution.py:754
  50.4 4.2 %scan_forward.3 = (f32[1024,384]{1,0:T(8,128)S(1)}, f32[8,128,384]{2,1,0:T(8,128)S(1)}, f32[128,384]{1,0:T(8,128)}) custom-call(f32[1032,640]{1,0:T(8,128)S(1)} %get-tuple-element.102.refs_0_, f32[1024,128]{1,0:T(8,128)S(1)} %get-tuple-element.103.refs_1_, f32[1040,128]{1,0:T(8,128)S(1)} %get-tuple-element.104.refs_2_.refs_3_, ...), custom_call_target="tpu_custom_call" | custom-call | flops 4000000000 | bytes 8847360 | tf_op jit(solution)/shard_map/scan_forward/pallas_call | solution.py:754
  54.7 1.8 %collective-permute-done.22.refs_13_.refs_12_ = bf16[256,768]{1,0:T(8,128)(2,1)S(1)} collective-permute-done((bf16[256,768]{1,0:T(8,128)(2,1)S(1)}, bf16[256,768]{1,0:T(8,128)(2,1)S(1)}, u32[]{:S(2)}, u32[]{:S(2)}) %collective-permute-start.22) | collective-permute-done | bytes 393248 | tf_op jit(solution)/shard_map/ppermute | solution.py:776
  56.5 3.3 %gate_forward.1 = (bf16[768,384]{1,0:T(8,128)(2,1)S(1)}, f32[1024,384]{1,0:T(8,128)S(1)}, f32[1024,384]{1,0:T(8,128)S(1)}, f32[16,128]{1,0:T(8,128)S(1)}, bf16[2...) custom-call(bf16[1024,768]{1,0:T(8,128)(2,1)S(1)} %get-tuple-element, ...), custom_call_target="tpu_custom_call" | custom-call | flops 6000000000 | bytes 11216384 | tf_op jit(solution)/shard_map/gate_forward/pallas_call | solution.py:754
  65.6 2.9 %gate_backward.1 = (f32[1024,384]{1,0:T(8,128)S(1)}, bf16[1024,384]{1,0:T(8,128)(2,1)S(1)}, f32[1024,128]{1,0:T(8,128)S(1)}, f32[1,384]{1,0:T(1,128)S(1)}, f32[8...) custom-call(f32[16,128]{1,0:T(8,128)S(1)} %get-tuple-element.122.refs_0_, ...), custom_call_target="tpu_custom_call" | custom-call | flops 6000000000 | bytes 12557312 | tf_op jit(solution)/shard_map/gate_backward/pallas_call | solution.py:754
  70.4 1.8 %collective-permute-start.28 = (bf16[256,768]{1,0:T(8,128)(2,1)S(1)}, bf16[256,768]{1,0:T(8,128)(2,1)S(1)}, u32[]{:S(2)}, u32[]{:S(2)}) collective-permute-start(bf16[256,768]{1,0:T(8,128)(2,1)S(1)} %get-tuple-element.130), channel_id=1, source_target_pairs={{0,24},{8,16},{16,8},{24,0},{1,25},{9,17},{17,9},{25,1},{2,26},{10... | collective-permute-start | bytes 1179656 | tf_op jit(solution)/shard_map/ppermute | solution.py:776
  73.2 2.3 %collective-permute-start.31 = (bf16[96,768]{1,0:T(8,128)(2,1)S(1)}, bf16[96,768]{1,0:T(8,128)(2,1)S(1)}, u32[]{:S(2)}, u32[]{:S(2)}) collective-permute-start(bf16[96,768]{1,0:T(8,128)(2,1)S(1)} %get-tuple-element.137), channel_id=1, source_target_pairs={{0,4},{1,5},{2,6},{3,7},{4,0},{5,1},{6,2},{7,3},{8,12},{9,13},{10,... | collective-permute-start | bytes 442376 | tf_op jit(solution)/shard_map/ppermute | solution.py:776
  75.6 7.2 %scan_backward.2 = (bf16[512,768]{1,0:T(8,128)(2,1)S(1)}, f32[128,384]{1,0:T(8,128)S(1)}, f32[8,640]{1,0:T(8,128)S(1)}, f32[8,640]{1,0:T(8,128)S(1)}, f32[8,128]{1,0:T(8,128)S(1)}) custom-call(f32[1032,640]{1,0:T(8,128)S(1)} %get-tuple-element.102.refs_0_, f32[1024,128]{1,0:T(8,128)S(1)} %get-tuple-element.103.refs_1_, ...), custom_call_target="tpu_custom_call" | custom-call | flops 10000000000 | bytes 7909376 | tf_op jit(solution)/shard_map/scan_backward/pallas_call | solution.py:754
  83.2 7.9 %scan_backward.3 = (bf16[1024,768]{1,0:T(8,128)(2,1)S(1)}, f32[128,384]{1,0:T(8,128)}, f32[8,640]{1,0:T(8,128)}, f32[8,640]{1,0:T(8,128)S(1)}, f32[8,128]{1,0:T(8,128)S(1)}) custom-call(f32[1032,640]{1,0:T(8,128)S(1)} %get-tuple-element.102.refs_0_, f32[1024,128]{1,0:T(8,128)S(1)} %get-tuple-element.103.refs_1_, ...), custom_call_target="tpu_custom_call" | custom-call | flops 10000000000 | bytes 9723904 | tf_op jit(solution)/shard_map/scan_backward/pallas_call | solution.py:754
  91.1 2.2 %normed_grads.1 = (bf16[256,768]{1,0:T(8,128)(2,1)S(1)}, bf16[256,768]{1,0:T(8,128)(2,1)S(1)}, bf16[256,768]{1,0:T(8,128)(2,1)S(1)}, bf16[256,768]{1,0:T(8,128)(2,1)S(1)}) custom-call(bf16[1024,768]{1,0:T(8,128)(2,1)S(1)} %get-tuple-element.155.gp_ref, bf16[768,768]{1,0:T(8,128)(2,1)S(1)} %get-tuple-element.147.w_ref, ...), custom_call_target="tpu_custom_call" | custom-call | flops 3000000000 | bytes 5701632 | tf_op jit(solution)/shard_map/normed_grads/pallas_call | solution.py:754
  93.4 1.7 %main_grads.1 = (bf16[4,112,768]{2,1,0:T(8,128)(2,1)S(1)}, bf16[4,112,768]{2,1,0:T(8,128)(2,1)S(1)}) custom-call(bf16[1024,768]{1,0:T(8,128)(2,1)S(1)} %get-tuple-element.101.refs_0_.refs_4_.normed_ref, bf16[1024,768]{1,0:T(8,128)(2,1)S(1)} %get-tuple-element.155.gp_ref, bf16[768,768]{1,0:T(8,128)(2,1)S(1)} %get-tuple-element.147.w_ref, ...), custom_call_target="tpu_custom_call" | custom-call | flops 4000000000 | bytes 5734912 | tf_op jit(solution)/shard_map/main_grads/pallas_call | solution.py:754
  95.2 2.1 %collective-permute-done.36.got_ref = bf16[4,112,768]{2,1,0:T(8,128)(2,1)S(1)} collective-permute-done((bf16[4,112,768]{2,1,0:T(8,128)(2,1)S(1)}, bf16[4,112,768]{2,1,0:T(8,128)(2,1)S(1)}, u32[]{:S(2)}, u32[]{:S(2)}) %collective-permute-start.36) | collective-permute-done | bytes 688160 | tf_op jit(solution)/shard_map/ppermute | solution.py:776
  97.5 1.8 %collective-permute-start.37 = (bf16[112,768]{1,0:T(8,128)(2,1)S(1)}, bf16[112,768]{1,0:T(8,128)(2,1)S(1)}, u32[]{:S(2)}, u32[]{:S(2)}) collective-permute-start(bf16[112,768]{1,0:T(8,128)(2,1)S(1)} %get-tuple-element.163), channel_id=1, source_target_pairs={{0,2},{1,3},{2,0},{3,1},{4,6},{5,7},{6,4},{7,5},{8,10},{9,11},{10,... | collective-permute-start | bytes 516104 | tf_op jit(solution)/shard_map/ppermute | solution.py:776
  100.2 2.5 %collective-permute-start.34 = (bf16[256,768]{1,0:T(8,128)(2,1)S(1)}, bf16[256,768]{1,0:T(8,128)(2,1)S(1)}, u32[]{:S(2)}, u32[]{:S(2)}) collective-permute-start(bf16[256,768]{1,0:T(8,128)(2,1)S(1)} %get-tuple-element.152), channel_id=1, source_target_pairs={{0,24},{8,16},{16,8},{24,0},{1,25},{9,17},{17,9},{25,1},{2,26},{10... | collective-permute-start | bytes 1179656 | tf_op jit(solution)/shard_map/ppermute | solution.py:776
  106.4 9.0 %collective-permute-done.38.refs_2_ = bf16[112,768]{1,0:T(8,128)(2,1)S(1)} collective-permute-done((bf16[112,768]{1,0:T(8,128)(2,1)S(1)}, bf16[112,768]{1,0:T(8,128)(2,1)S(1)}, u32[]{:S(2)}, u32[]{:S(2)}) %collective-permute-start.38) | collective-permute-done | bytes 172064 | tf_op jit(solution)/shard_map/ppermute | solution.py:776
  115.3 3.6 %collective-permute-done.39.refs_3_ = bf16[112,768]{1,0:T(8,128)(2,1)S(1)} collective-permute-done((bf16[112,768]{1,0:T(8,128)(2,1)S(1)}, bf16[112,768]{1,0:T(8,128)(2,1)S(1)}, u32[]{:S(2)}, u32[]{:S(2)}) %collective-permute-start.39) | collective-permute-done | bytes 172064 | tf_op jit(solution)/shard_map/ppermute | solution.py:776
  120.7 1.8 %collective-permute-start.42 = (bf16[64,768]{1,0:T(8,128)(2,1)S(1)}, bf16[64,768]{1,0:T(8,128)(2,1)S(1)}, u32[]{:S(2)}, u32[]{:S(2)}) collective-permute-start(bf16[64,768]{1,0:T(8,128)(2,1)S(1)} %get-tuple-element.169), channel_id=1, source_target_pairs={{0,24},{8,16},{16,8},{24,0},{1,25},{9,17},{17,9},{25,1},{2,26},{10... | collective-permute-start | bytes 294920 | tf_op jit(solution)/shard_map/ppermute | solution.py:776
  (108 shorter events, 41.6 us)
Async XLA Ops:
  11.0 19.7 %collective-permute-start.5 = (bf16[256,768]{1,0:T(8,128)(2,1)S(1)}, bf16[256,768]{1,0:T(8,128)(2,1)S(1)}, u32[]{:S(2)}, u32[]{:S(2)}) collective-permute-start(bf16[256,768]{1,0:T(8,128)(2,1)S(1)} %bitcast.10), channel_id=1, source_target_pairs={{0,24},{8,16},{16,8},{24,0},{1,25},{9,17},{17,9},{25,1},{2,26},{10... | collective-permute-start | bytes 1179656 | tf_op jit(solution)/shard_map/ppermute | solution.py:776
  11.6 19.7 %collective-permute-start.4 = (bf16[256,768]{1,0:T(8,128)(2,1)S(1)}, bf16[256,768]{1,0:T(8,128)(2,1)S(1)}, u32[]{:S(2)}, u32[]{:S(2)}) collective-permute-start(bf16[256,768]{1,0:T(8,128)(2,1)S(1)} %bitcast.11), channel_id=1, source_target_pairs={{0,16},{8,24},{16,0},{24,8},{1,17},{9,25},{17,1},{25,9},{2,18},{10... | collective-permute-start | bytes 1179656 | tf_op jit(solution)/shard_map/ppermute | solution.py:776
  14.0 11.6 %collective-permute-start.8 = (bf16[96,768]{1,0:T(8,128)(2,1)S(1)}, bf16[96,768]{1,0:T(8,128)(2,1)S(1)}, u32[]{:S(2)}, u32[]{:S(2)}) collective-permute-start(bf16[96,768]{1,0:T(8,128)(2,1)S(1)} %get-tuple-element.100.refs_8_), channel_id=1, source_target_pairs={{0,6},{1,7},{2,4},{3,5},{4,2},{5,3},{6,0},{7,1},{8,14},{9,15},{10,... | collective-permute-start | bytes 442376 | tf_op jit(solution)/shard_map/ppermute | solution.py:776
  15.6 16.1 %collective-permute-start.3 = (bf16[256,768]{1,0:T(8,128)(2,1)S(1)}, bf16[256,768]{1,0:T(8,128)(2,1)S(1)}, u32[]{:S(2)}, u32[]{:S(2)}) collective-permute-start(bf16[256,768]{1,0:T(8,128)(2,1)S(1)} %bitcast.12), channel_id=1, source_target_pairs={{0,8},{8,0},{16,24},{24,16},{1,9},{9,1},{17,25},{25,17},{2,10},{10... | collective-permute-start | bytes 1179656 | tf_op jit(solution)/shard_map/ppermute | solution.py:776
  17.1 9.6 %collective-permute-start.7 = (bf16[96,768]{1,0:T(8,128)(2,1)S(1)}, bf16[96,768]{1,0:T(8,128)(2,1)S(1)}, u32[]{:S(2)}, u32[]{:S(2)}) collective-permute-start(bf16[96,768]{1,0:T(8,128)(2,1)S(1)} %get-tuple-element.100.refs_8_), channel_id=1, source_target_pairs={{0,4},{1,5},{2,6},{3,7},{4,0},{5,1},{6,2},{7,3},{8,12},{9,13},{10,... | collective-permute-start | bytes 442376 | tf_op jit(solution)/shard_map/ppermute | solution.py:776
  26.8 7.0 %collective-permute-start.9 = (bf16[96,768]{1,0:T(8,128)(2,1)S(1)}, bf16[96,768]{1,0:T(8,128)(2,1)S(1)}, u32[]{:S(2)}, u32[]{:S(2)}) collective-permute-start(bf16[96,768]{1,0:T(8,128)(2,1)S(1)} %get-tuple-element.100.refs_8_), channel_id=1, source_target_pairs={{0,1},{1,0},{2,3},{3,2},{4,5},{5,4},{6,7},{7,6},{8,9},{9,8},{10,11... | collective-permute-start | bytes 442376 | tf_op jit(solution)/shard_map/ppermute | solution.py:776
  31.7 13.0 %collective-permute-start.15 = (bf16[96,768]{1,0:T(8,128)(2,1)S(1)}, bf16[96,768]{1,0:T(8,128)(2,1)S(1)}, u32[]{:S(2)}, u32[]{:S(2)}) collective-permute-start(bf16[96,768]{1,0:T(8,128)(2,1)S(1)} %get-tuple-element.113.refs_2_), channel_id=1, source_target_pairs={{0,6},{1,7},{2,4},{3,5},{4,2},{5,3},{6,0},{7,1},{8,14},{9,15},{10,... | collective-permute-start | bytes 442376 | tf_op jit(solution)/shard_map/ppermute | solution.py:776
  33.8 15.5 %collective-permute-start.14 = (bf16[96,768]{1,0:T(8,128)(2,1)S(1)}, bf16[96,768]{1,0:T(8,128)(2,1)S(1)}, u32[]{:S(2)}, u32[]{:S(2)}) collective-permute-start(bf16[96,768]{1,0:T(8,128)(2,1)S(1)} %get-tuple-element.113.refs_2_), channel_id=1, source_target_pairs={{0,4},{1,5},{2,6},{3,7},{4,0},{5,1},{6,2},{7,3},{8,12},{9,13},{10,... | collective-permute-start | bytes 442376 | tf_op jit(solution)/shard_map/ppermute | solution.py:776
  34.1 15.2 %collective-permute-start.13 = (bf16[96,768]{1,0:T(8,128)(2,1)S(1)}, bf16[96,768]{1,0:T(8,128)(2,1)S(1)}, u32[]{:S(2)}, u32[]{:S(2)}) collective-permute-start(bf16[96,768]{1,0:T(8,128)(2,1)S(1)} %get-tuple-element.113.refs_2_), channel_id=1, source_target_pairs={{0,2},{1,3},{2,0},{3,1},{4,6},{5,7},{6,4},{7,5},{8,10},{9,11},{10,... | collective-permute-start | bytes 442376 | tf_op jit(solution)/shard_map/ppermute | solution.py:776
  35.3 14.6 %collective-permute-start.17 = (bf16[256,768]{1,0:T(8,128)(2,1)S(1)}, bf16[256,768]{1,0:T(8,128)(2,1)S(1)}, u32[]{:S(2)}, u32[]{:S(2)}) collective-permute-start(bf16[256,768]{1,0:T(8,128)(2,1)S(1)} %bitcast.16), channel_id=1, source_target_pairs={{0,16},{8,24},{16,0},{24,8},{1,17},{9,25},{17,1},{25,9},{2,18},{10... | collective-permute-start | bytes 1179656 | tf_op jit(solution)/shard_map/ppermute | solution.py:776
  35.8 14.1 %collective-permute-start.16 = (bf16[256,768]{1,0:T(8,128)(2,1)S(1)}, bf16[256,768]{1,0:T(8,128)(2,1)S(1)}, u32[]{:S(2)}, u32[]{:S(2)}) collective-permute-start(bf16[256,768]{1,0:T(8,128)(2,1)S(1)} %bitcast.17), channel_id=1, source_target_pairs={{0,8},{8,0},{16,24},{24,16},{1,9},{9,1},{17,25},{25,17},{2,10},{10... | collective-permute-start | bytes 1179656 | tf_op jit(solution)/shard_map/ppermute | solution.py:776
  44.7 11.8 %collective-permute-start.22 = (bf16[256,768]{1,0:T(8,128)(2,1)S(1)}, bf16[256,768]{1,0:T(8,128)(2,1)S(1)}, u32[]{:S(2)}, u32[]{:S(2)}) collective-permute-start(bf16[256,768]{1,0:T(8,128)(2,1)S(1)} %bitcast.18), channel_id=1, source_target_pairs={{0,24},{8,16},{16,8},{24,0},{1,25},{9,17},{17,9},{25,1},{2,26},{10... | collective-permute-start | bytes 1179656 | tf_op jit(solution)/shard_map/ppermute | solution.py:776
  68.6 24.7 %collective-permute-start.26 = (bf16[256,768]{1,0:T(8,128)(2,1)S(1)}, bf16[256,768]{1,0:T(8,128)(2,1)S(1)}, u32[]{:S(2)}, u32[]{:S(2)}) collective-permute-start(bf16[256,768]{1,0:T(8,128)(2,1)S(1)} %get-tuple-element.128), channel_id=1, source_target_pairs={{0,8},{8,0},{16,24},{24,16},{1,9},{9,1},{17,25},{25,17},{2,10},{10... | collective-permute-start | bytes 1179656 | tf_op jit(solution)/shard_map/ppermute | solution.py:776
  70.0 23.4 %collective-permute-start.27 = (bf16[256,768]{1,0:T(8,128)(2,1)S(1)}, bf16[256,768]{1,0:T(8,128)(2,1)S(1)}, u32[]{:S(2)}, u32[]{:S(2)}) collective-permute-start(bf16[256,768]{1,0:T(8,128)(2,1)S(1)} %get-tuple-element.129), channel_id=1, source_target_pairs={{0,16},{8,24},{16,0},{24,8},{1,17},{9,25},{17,1},{25,9},{2,18},{10... | collective-permute-start | bytes 1179656 | tf_op jit(solution)/shard_map/ppermute | solution.py:776
  70.4 22.9 %collective-permute-start.28 = (bf16[256,768]{1,0:T(8,128)(2,1)S(1)}, bf16[256,768]{1,0:T(8,128)(2,1)S(1)}, u32[]{:S(2)}, u32[]{:S(2)}) collective-permute-start(bf16[256,768]{1,0:T(8,128)(2,1)S(1)} %get-tuple-element.130), channel_id=1, source_target_pairs={{0,24},{8,16},{16,8},{24,0},{1,25},{9,17},{17,9},{25,1},{2,26},{10... | collective-permute-start | bytes 1179656 | tf_op jit(solution)/shard_map/ppermute | solution.py:776
  72.4 10.4 %collective-permute-start.30 = (bf16[96,768]{1,0:T(8,128)(2,1)S(1)}, bf16[96,768]{1,0:T(8,128)(2,1)S(1)}, u32[]{:S(2)}, u32[]{:S(2)}) collective-permute-start(bf16[96,768]{1,0:T(8,128)(2,1)S(1)} %get-tuple-element.136), channel_id=1, source_target_pairs={{0,2},{1,3},{2,0},{3,1},{4,6},{5,7},{6,4},{7,5},{8,10},{9,11},{10,... | collective-permute-start | bytes 442376 | tf_op jit(solution)/shard_map/ppermute | solution.py:776
  73.2 9.9 %collective-permute-start.31 = (bf16[96,768]{1,0:T(8,128)(2,1)S(1)}, bf16[96,768]{1,0:T(8,128)(2,1)S(1)}, u32[]{:S(2)}, u32[]{:S(2)}) collective-permute-start(bf16[96,768]{1,0:T(8,128)(2,1)S(1)} %get-tuple-element.137), channel_id=1, source_target_pairs={{0,4},{1,5},{2,6},{3,7},{4,0},{5,1},{6,2},{7,3},{8,12},{9,13},{10,... | collective-permute-start | bytes 442376 | tf_op jit(solution)/shard_map/ppermute | solution.py:776
  82.8 10.6 %collective-permute-start.35 = (bf16[96,768]{1,0:T(8,128)(2,1)S(1)}, bf16[96,768]{1,0:T(8,128)(2,1)S(1)}, u32[]{:S(2)}, u32[]{:S(2)}) collective-permute-start(bf16[96,768]{1,0:T(8,128)(2,1)S(1)} %get-tuple-element.153), channel_id=1, source_target_pairs={{0,6},{1,7},{2,4},{3,5},{4,2},{5,3},{6,0},{7,1},{8,14},{9,15},{10,... | collective-permute-start | bytes 442376 | tf_op jit(solution)/shard_map/ppermute | solution.py:776
  97.5 6.7 %collective-permute-start.37 = (bf16[112,768]{1,0:T(8,128)(2,1)S(1)}, bf16[112,768]{1,0:T(8,128)(2,1)S(1)}, u32[]{:S(2)}, u32[]{:S(2)}) collective-permute-start(bf16[112,768]{1,0:T(8,128)(2,1)S(1)} %get-tuple-element.163), channel_id=1, source_target_pairs={{0,2},{1,3},{2,0},{3,1},{4,6},{5,7},{6,4},{7,5},{8,10},{9,11},{10,... | collective-permute-start | bytes 516104 | tf_op jit(solution)/shard_map/ppermute | solution.py:776
  99.3 21.5 %collective-permute-start.32 = (bf16[256,768]{1,0:T(8,128)(2,1)S(1)}, bf16[256,768]{1,0:T(8,128)(2,1)S(1)}, u32[]{:S(2)}, u32[]{:S(2)}) collective-permute-start(bf16[256,768]{1,0:T(8,128)(2,1)S(1)} %get-tuple-element.150), channel_id=1, source_target_pairs={{0,8},{8,0},{16,24},{24,16},{1,9},{9,1},{17,25},{25,17},{2,10},{10... | collective-permute-start | bytes 1179656 | tf_op jit(solution)/shard_map/ppermute | solution.py:776
  99.8 23.8 %collective-permute-start.33 = (bf16[256,768]{1,0:T(8,128)(2,1)S(1)}, bf16[256,768]{1,0:T(8,128)(2,1)S(1)}, u32[]{:S(2)}, u32[]{:S(2)}) collective-permute-start(bf16[256,768]{1,0:T(8,128)(2,1)S(1)} %get-tuple-element.151), channel_id=1, source_target_pairs={{0,16},{8,24},{16,0},{24,8},{1,17},{9,25},{17,1},{25,9},{2,18},{10... | collective-permute-start | bytes 1179656 | tf_op jit(solution)/shard_map/ppermute | solution.py:776
  100.2 23.3 %collective-permute-start.34 = (bf16[256,768]{1,0:T(8,128)(2,1)S(1)}, bf16[256,768]{1,0:T(8,128)(2,1)S(1)}, u32[]{:S(2)}, u32[]{:S(2)}) collective-permute-start(bf16[256,768]{1,0:T(8,128)(2,1)S(1)} %get-tuple-element.152), channel_id=1, source_target_pairs={{0,24},{8,16},{16,8},{24,0},{1,25},{9,17},{17,9},{25,1},{2,26},{10... | collective-permute-start | bytes 1179656 | tf_op jit(solution)/shard_map/ppermute | solution.py:776
  102.7 12.6 %collective-permute-start.38 = (bf16[112,768]{1,0:T(8,128)(2,1)S(1)}, bf16[112,768]{1,0:T(8,128)(2,1)S(1)}, u32[]{:S(2)}, u32[]{:S(2)}) collective-permute-start(bf16[112,768]{1,0:T(8,128)(2,1)S(1)} %get-tuple-element.164), channel_id=1, source_target_pairs={{0,4},{1,5},{2,6},{3,7},{4,0},{5,1},{6,2},{7,3},{8,12},{9,13},{10,... | collective-permute-start | bytes 516104 | tf_op jit(solution)/shard_map/ppermute | solution.py:776
  104.2 14.7 %collective-permute-start.39 = (bf16[112,768]{1,0:T(8,128)(2,1)S(1)}, bf16[112,768]{1,0:T(8,128)(2,1)S(1)}, u32[]{:S(2)}, u32[]{:S(2)}) collective-permute-start(bf16[112,768]{1,0:T(8,128)(2,1)S(1)} %get-tuple-element.165), channel_id=1, source_target_pairs={{0,6},{1,7},{2,4},{3,5},{4,2},{5,3},{6,0},{7,1},{8,14},{9,15},{10,... | collective-permute-start | bytes 516104 | tf_op jit(solution)/shard_map/ppermute | solution.py:776
  (31 other events, 254.7 us)

commit v4 on v3

--- a/solution.py
+++ b/solution.py
@@ -17,6 +17,7 @@
 WIDTH = 768
 LANES = 128
 LEAD = 8
+TINY = 1e-37
 
 
 highest = lax.Precision.HIGHEST
@@ -107,55 +108,47 @@
     return aligned(owner * plan.in_rows, 8)
 
 
-def block_values(plan, b, x_ref, segc_ref, segr_ref, dt_ref, convw, convb, heads_ref):
-    base = aligned(b * GROUP, GROUP)
+def exact_sigmoid(value):
+    return 1.0 / (1.0 + jnp.exp(-value))
+
+
+def convolved(plan, base, x_ref, segc_ref, convw, convb):
     win = x_ref[pl.ds(base, GROUP + LEAD), :]
     segw = segc_ref[pl.ds(base, GROUP + LEAD), :]
     seg = segw[LEAD:]
-    prev = segw[LEAD - 1 : LEAD]
-    repeat = plan.mixed // LANES
-    pre = jnp.broadcast_to(convb, (GROUP, plan.mixed))
-    shifts = []
-    for k in range(KERNEL):
+    pre = convb + convw[KERNEL - 1 : KERNEL] * win[LEAD:]
+    for k in range(KERNEL - 1):
         start = LEAD - KERNEL + 1 + k
-        part = win[start : start + GROUP]
-        if k < KERNEL - 1:
-            same = (segw[start : start + GROUP] == seg).astype(f32)
-            part = part * jnp.concatenate([same] * repeat, axis=1)
-        shifts.append(part)
-        pre = pre + convw[k : k + 1] * part
+        same = (segw[start : start + GROUP] == seg).astype(f32)
+        same = jnp.concatenate([same] * (plan.mixed // LANES), axis=1)
+        pre = pre + convw[k : k + 1] * win[start : start + GROUP] * same
     sig = sigmoid(pre)
     mixed = pre * sig
-    values = mixed[:, : plan.chan]
-    keys = mixed[:, plan.chan : plan.chan + STATE]
-    queries = mixed[:, plan.chan + STATE :]
-    dt_in = dt_ref[pl.ds(base, GROUP), :] + heads_ref[0:1, :LANES]
+    return mixed, sig + mixed * (1.0 - sig)
+
+
+def decays(dt_in, heads_ref):
     steps = softplus(dt_in)
-    decay = -steps * jnp.exp(heads_ref[1:2, :LANES])
     row = iota((GROUP, GROUP), 0)
     col = iota((GROUP, GROUP), 1)
-    tri = (row >= col).astype(f32)
-    cum = mask_mm(tri, decay)
+    decay = -steps * jnp.exp(heads_ref[1:2, :LANES])
+    cum = mask_mm(row >= col, decay)
     half = LANES // 2
     turned = jnp.where(col < half, cum, pltpu.roll(steps, half, 1)).T
-    cum_t = turned[:half]
-    steps_t = turned[half:]
-    segr = segr_ref[pl.ds(b, 1), :]
-    allowed = (seg == segr) & (row >= col)
-    scores = mm_nt(queries, keys)
+    return steps, cum, turned
+
+
+def edges(segc_ref, base, cum):
+    seg = segc_ref[pl.ds(aligned(base + LEAD, 8), GROUP), :]
+    prev = segc_ref[pl.ds(base, LEAD), :][LEAD - 1 :]
     keep = jnp.where(seg == prev, jnp.exp(cum), 0.0)
     last = cum[GROUP - 1 :]
     to_last = jnp.where(seg == seg[GROUP - 1 :], jnp.exp(last - cum), 0.0)
-    return dict(
-        base=base, seg=seg, shifts=shifts, pre=pre, sig=sig, values=values, keys=keys,
-        queries=queries, dt_in=dt_in, steps=steps, decay=decay, tri=tri, cum=cum, cum_t=cum_t,
-        steps_t=steps_t, allowed=allowed, scores=scores, keep=keep, to_last=to_last,
-    )
-
-
-def head_decay(v, h):
-    gap = v["cum"][:, h : h + 1] - v["cum_t"][h : h + 1, :]
-    return jnp.where(v["allowed"], jnp.exp(jnp.minimum(gap, 0.0)), 0.0)
+    return seg, keep, to_last
+
+
+def head_decay(cum, turned, h):
+    return jnp.exp(jnp.minimum(cum[:, h : h + 1] - turned[h : h + 1, :], 0.0))
 
 
 def split_pair(pair):
@@ -295,43 +288,56 @@
     x_ref, dt_ref, segc_ref, segr_ref, conv_ref, heads_ref = refs[:6]
     refs = refs[6:]
     if first:
-        early_y_ref, early_states_ref, early_ref = refs[:3]
-        refs = refs[3:]
-    y_ref, states_ref, state_ref = refs
+        early_y_ref, early_ref = refs[:2]
+        refs = refs[2:]
+    y_ref, state_ref, states_ref, mixed_ref, slope_ref, table_ref, scores_ref = refs
     if first:
         y_ref[: first * GROUP, :] = early_y_ref[...]
-        states_ref[:first] = early_states_ref[...]
         state_ref[...] = early_ref[...]
     else:
         state_ref[...] = jnp.zeros_like(state_ref)
     convw = conv_ref[0:KERNEL, :]
     convb = conv_ref[KERNEL : KERNEL + 1, :]
-
-    def step(b, carry):
-        v = block_values(plan, b, x_ref, segc_ref, segr_ref, dt_ref, convw, convb, heads_ref)
+    chan, half = plan.chan, LANES // 2
+    causal = iota((GROUP, GROUP), 0) >= iota((GROUP, GROUP), 1)
+
+    def step(turn, carry):
+        base = aligned((first + turn) * GROUP, GROUP)
+        here = pl.ds(aligned(turn * GROUP, GROUP), GROUP)
+        mixed, slope = convolved(plan, base, x_ref, segc_ref, convw, convb)
+        mixed_ref[here, :] = mixed
+        slope_ref[here, :] = slope
+        values = mixed[:, :chan]
+        keys = mixed[:, chan : chan + STATE]
+        queries = mixed[:, chan + STATE :]
+        dt_in = dt_ref[pl.ds(base, GROUP), :] + heads_ref[0:1, :LANES]
+        steps, cum, turned = decays(dt_in, heads_ref)
+        table_ref[0, here, :] = steps
+        table_ref[1, here, :] = cum
+        table_ref[2, here, :] = turned
+        seg, keep, to_last = edges(segc_ref, base, cum)
+        allowed = (seg == segr_ref[pl.ds(first + turn, 1), :]) & causal
+        scores = jnp.where(allowed, mm_nt(queries, keys), 0.0)
+        scores_ref[here, :] = scores
         state = state_ref[...]
-        states_ref[b] = state
+        states_ref[turn] = state
         parts = []
         for pair in range(plan.heads // 2):
             lanes = slice(pair * LANES, (pair + 1) * LANES)
             weights_pair = []
             for h in (2 * pair, 2 * pair + 1):
-                decay = head_decay(v, h)
-                weights_pair.append(decay * v["scores"] * v["steps_t"][h : h + 1, :])
-            parts.append(
-                mm(jnp.concatenate(weights_pair, axis=1), split_pair(v["values"][:, lanes]))
-            )
+                decay = head_decay(cum, turned, h)
+                weights_pair.append(decay * scores * turned[half + h : half + h + 1, :])
+            parts.append(mm(jnp.concatenate(weights_pair, axis=1), split_pair(values[:, lanes])))
         inside = jnp.concatenate(parts, axis=1)
-        spread = wide(
-            jnp.concatenate([v["keep"], v["to_last"] * v["steps"]], axis=0), plan.chan
-        )
+        spread = wide(jnp.concatenate([keep, to_last * steps], axis=0), chan)
         keep, to_end = spread[:GROUP], spread[GROUP:]
-        carried = mm(v["queries"], state) * keep
-        y_ref[pl.ds(v["base"], GROUP), :] = inside + carried + heads_ref[2:3, :] * v["values"]
-        state_ref[...] = state * keep[GROUP - 1 :] + mm_tn(v["keys"], v["values"] * to_end)
+        carried = mm(queries, state) * keep
+        y_ref[pl.ds(base, GROUP), :] = inside + carried + heads_ref[2:3, :] * values
+        state_ref[...] = state * keep[GROUP - 1 :] + mm_tn(keys, values * to_end)
         return carry
 
-    lax.fori_loop(first, last, step, 0, unroll=True)
+    lax.fori_loop(0, last - first, step, 0, unroll=True)
 
 
 def gate_kernel(plan, *refs):
@@ -474,13 +480,13 @@
 
 
 def scan_back_kernel(plan, first, last, *refs):
-    x_ref, dt_ref, states_ref, segc_ref, segr_ref, dy_ref, conv_ref, heads_ref = refs[:8]
-    refs = refs[8:]
+    x_ref, dt_ref, segc_ref, segr_ref, dy_ref, conv_ref, heads_ref = refs[:7]
+    states_ref, mixed_ref, slope_ref, table_ref, scores_ref = refs[7:12]
+    refs = refs[12:]
     later = last < plan.blocks
     if later:
         before, refs = refs[:5], refs[5:]
     gp_ref, adj_ref, edge_ref, acc_ref, head_ref = refs
-    low = first * GROUP
     if later:
         gp_ref[(last - first) * GROUP :, :] = before[0][...]
         adj_ref[...] = before[1][...]
@@ -493,33 +499,39 @@
         acc_ref[...] = jnp.zeros_like(acc_ref)
         head_ref[...] = jnp.zeros_like(head_ref)
     convw = conv_ref[0:KERNEL, :]
-    convb = conv_ref[KERNEL : KERNEL + 1, :]
+    chan, half = plan.chan, LANES // 2
     repeat = plan.mixed // LANES
-    pick = (iota((plan.chan, LANES), 0) // HEADDIM == iota((plan.chan, LANES), 1)).astype(f32)
+    pick = (iota((chan, LANES), 0) // HEADDIM == iota((chan, LANES), 1)).astype(f32)
+    row = iota((GROUP, LANES), 0)
     lane = iota((GROUP, LANES), 1)
 
     def step(turn, carry):
         b = last - 1 - turn
-        v = block_values(plan, b, x_ref, segc_ref, segr_ref, dt_ref, convw, convb, heads_ref)
-        base = v["base"]
-        state = states_ref[b]
+        base = aligned(b * GROUP, GROUP)
+        here = pl.ds(aligned((b - first) * GROUP, GROUP), GROUP)
+        values = mixed_ref[here, :chan]
+        keys = mixed_ref[here, chan : chan + STATE]
+        queries = mixed_ref[here, chan + STATE :]
+        steps = table_ref[0, here, :]
+        cum = table_ref[1, here, :]
+        turned = table_ref[2, here, :]
+        scores = scores_ref[here, :]
+        seg, keep_h, to_last = edges(segc_ref, base, cum)
+        state = states_ref[b - first]
         adj = adj_ref[...]
         dy = dy_ref[pl.ds(base, GROUP), :]
-        values = v["values"]
-        spread = wide(
-            jnp.concatenate([v["keep"], v["to_last"] * v["steps"]], axis=0), plan.chan
-        )
+        spread = wide(jnp.concatenate([keep_h, to_last * steps], axis=0), chan)
         keep, to_end = spread[:GROUP], spread[GROUP:]
         kept = dy * keep
         dq = mm_nt(kept, state)
-        cross = kept * mm(v["queries"], state)
-        fed = mm(v["keys"], adj)
+        cross = kept * mm(queries, state)
+        fed = mm(keys, adj)
         dk = mm_nt(values * to_end, adj)
-        adj_ref[...] = adj * keep[GROUP - 1 :] + mm_tn(v["queries"], kept)
+        adj_ref[...] = adj * keep[GROUP - 1 :] + mm_tn(queries, kept)
         ended = jnp.sum(state * adj, axis=0, keepdims=True)
         pushed = fed * values
         skipped = jnp.sum(dy * values, axis=0, keepdims=True)
-        few = jnp.concatenate([ended, skipped, jnp.zeros((6, plan.chan), f32)], axis=0)
+        few = jnp.concatenate([ended, skipped, jnp.zeros((6, chan), f32)], axis=0)
         high = few.astype(bf16).astype(f32)
         sums = mm(jnp.concatenate([cross, pushed, high, few - high], axis=0), pick)
         cross_h = sums[:GROUP]
@@ -527,11 +539,11 @@
         few_h = sums[2 * GROUP : 2 * GROUP + 8] + sums[2 * GROUP + 8 :]
         ended_h = few_h[0:1]
         skipped_h = few_h[1:2]
-        grad_steps = pushed_h * v["to_last"]
-        pulled = grad_steps * v["steps"]
+        grad_steps = pushed_h * to_last
+        pulled = grad_steps * steps
         dcum = cross_h - pulled
-        at_end = jnp.sum(pulled, axis=0, keepdims=True) + v["keep"][GROUP - 1 :] * ended_h
-        dscores = jnp.zeros((GROUP, GROUP), f32)
+        at_end = jnp.sum(pulled, axis=0, keepdims=True) + keep_h[GROUP - 1 :] * ended_h
+        dscores = None
         columns = []
         dvs = []
         for pair in range(plan.heads // 2):
@@ -540,49 +552,48 @@
             products = mm_nt(dy_pair, values[:, lanes])
             stacked = []
             for j, h in enumerate((2 * pair, 2 * pair + 1)):
-                decay = head_decay(v, h)
-                steps_row = v["steps_t"][h : h + 1, :]
-                weighted = decay * products[j * GROUP : (j + 1) * GROUP]
-                direct = weighted * v["scores"]
-                dscores = dscores + weighted * steps_row
-                rowsum = jnp.sum(direct * steps_row, axis=1, keepdims=True)
-                dcum = dcum + jnp.where(lane == h, rowsum, 0.0)
-                columns.append(jnp.sum(direct, axis=0, keepdims=True))
-                stacked.append(decay * v["scores"] * steps_row)
+                scaled = head_decay(cum, turned, h) * turned[half + h : half + h + 1, :]
+                weighted = scaled * products[j * GROUP : (j + 1) * GROUP]
+                both = weighted * scores
+                dscores = weighted if dscores is None else dscores + weighted
+                dcum = jnp.where(lane == h, dcum + jnp.sum(both, axis=1, keepdims=True), dcum)
+                columns.append(jnp.sum(both, axis=0, keepdims=True))
+                stacked.append(scaled * scores)
             dvs.append(mm_tn(jnp.concatenate(stacked, axis=0), dy_pair))
+        allowed = (seg == segr_ref[pl.ds(b, 1), :]) & (row >= lane)
+        dscores = jnp.where(allowed, dscores, 0.0)
         dv = jnp.concatenate(dvs, axis=1) + fed * to_end + heads_ref[2:3, :] * dy
         columns.append(jnp.zeros((LANES - plan.heads, GROUP), f32))
         down = jnp.concatenate(columns, axis=0).T
-        grad_steps = grad_steps + down
-        dcum = dcum - down * v["steps"]
-        row = iota((GROUP, LANES), 0)
+        grad_steps = grad_steps + down / jnp.maximum(steps, TINY)
+        dcum = dcum - down
         dcum = dcum + jnp.where(row == GROUP - 1, at_end, 0.0)
-        dk = dk + mm_tn(dscores, v["queries"])
-        dq = dq + mm(dscores, v["keys"])
-        ddecay = mask_mm(iota((GROUP, GROUP), 0) <= iota((GROUP, GROUP), 1), dcum)
-        grad_steps = grad_steps - ddecay * jnp.exp(heads_ref[1:2, :LANES])
-        grad_dt = grad_steps * sigmoid(v["dt_in"])
+        dk = dk + mm_tn(dscores, queries)
+        dq = dq + mm(dscores, keys)
+        ddecay = mask_mm(row <= lane, dcum)
+        rate = jnp.exp(heads_ref[1:2, :LANES])
+        grad_steps = grad_steps - ddecay * rate
+        dt_in = dt_ref[pl.ds(base, GROUP), :] + heads_ref[0:1, :LANES]
+        grad_dt = grad_steps * exact_sigmoid(dt_in)
         head_ref[0:1, :] += jnp.sum(grad_dt, axis=0, keepdims=True)
-        head_ref[1:2, :] += jnp.sum(ddecay * v["decay"], axis=0, keepdims=True)
+        head_ref[1:2, :] -= jnp.sum(ddecay * steps, axis=0, keepdims=True) * rate
         head_ref[2:3, :] += skipped_h
-        dmixed = jnp.concatenate([dv, dk, dq], axis=1)
-        pre, sig = v["pre"], v["sig"]
-        dpre = dmixed * (sig * (1.0 + pre * (1.0 - sig)))
-        acc_ref[4:5, :] += jnp.sum(dpre, axis=0, keepdims=True)
+        dpre = jnp.concatenate([dv, dk, dq], axis=1) * slope_ref[here, :]
         longer = jnp.concatenate([dpre, edge_ref[...]], axis=0)
         edge_ref[...] = dpre[:LEAD]
         segn = segc_ref[pl.ds(aligned(base + LEAD, 8), GROUP + LEAD), :]
-        dx = jnp.zeros((GROUP, plan.mixed), f32)
-        for k in range(KERNEL):
-            acc_ref[k : k + 1, :] += jnp.sum(dpre * v["shifts"][k], axis=0, keepdims=True)
+        x = x_ref[pl.ds(aligned(base + LEAD, 8), GROUP), :]
+        acc_ref[KERNEL : KERNEL + 1, :] += jnp.sum(dpre, axis=0, keepdims=True)
+        acc_ref[KERNEL - 1 : KERNEL, :] += jnp.sum(dpre * x, axis=0, keepdims=True)
+        dx = convw[KERNEL - 1 : KERNEL] * dpre
+        for k in range(KERNEL - 1):
             ahead = KERNEL - 1 - k
-            part = longer[ahead : ahead + GROUP]
-            if ahead:
-                same = (segn[ahead : ahead + GROUP] == v["seg"]).astype(f32)
-                part = part * jnp.concatenate([same] * repeat, axis=1)
+            same = (segn[ahead : ahead + GROUP] == seg).astype(f32)
+            part = longer[ahead : ahead + GROUP] * jnp.concatenate([same] * repeat, axis=1)
+            acc_ref[k : k + 1, :] += jnp.sum(part * x, axis=0, keepdims=True)
             dx = dx + convw[k : k + 1] * part
         live = jnp.where(lane < plan.heads, grad_dt, 0.0)
-        gp_ref[pl.ds(aligned(base - low, GROUP), GROUP), :] = jnp.concatenate([dx, live], axis=1).astype(bf16)
+        gp_ref[here, :] = jnp.concatenate([dx, live], axis=1).astype(bf16)
         return carry
 
     lax.fori_loop(0, last - first, step, 0, unroll=True)
@@ -762,13 +773,14 @@
         ],
         compiler_params=pltpu.CompilerParams(vmem_limit_bytes=mib * 2**20),
         cost_estimate=pl.CostEstimate(
-            flops=micros * FLOPS_PER_MICRO, bytes_accessed=size, transcendentals=0
+            flops=micros * FLOPS_PER_MICRO, bytes_accessed=0, transcendentals=0
         ),
         name=name,
     )(*args)
 
 
-FLOPS_PER_MICRO = 1_000_000_000
+FLOPS_PER_MICRO = 3_000_000_000
+LATE = 4
 
 
 def swap(value, axis, by):
@@ -846,17 +858,22 @@
     scan_in = (x, dt_raw, segc, segr, conv, per_head)
 
     def scan_part(first, last, *early):
-        return call(
+        count, size = last - first, (last - first) * GROUP
+        return list(call(
             lambda p, *refs: scan_kernel(p, first, last, *refs), plan,
-            [((last * GROUP, chan), f32), ((last,) + state_shape, f32), (state_shape, f32)], [],
-            *scan_in, *early, mib=12, micros=4, name="scan_forward",
-        )
-
-    early = list(scan_part(0, half))
-    gate_line = [after(one, early[2]) for one in gate_line]
+            [
+                ((last * GROUP, chan), f32), (state_shape, f32), ((count,) + state_shape, f32),
+                ((size, plan.mixed), f32), ((size, plan.mixed), f32), ((3, size, LANES), f32),
+                ((size, GROUP), f32),
+            ], [],
+            *scan_in, *early, mib=16, micros=4, name="scan_forward",
+        ))
+
+    early_y, early_state, *early = scan_part(0, half)
+    gate_line = [after(one, early_state) for one in gate_line]
     gate_parts = both_cores(gate_line)
-    early[2] = after(early[2], *gate_line, *cots[1:3])
-    y, states, _ = scan_part(half, plan.blocks, *early)
+    early_state = after(early_state, *gate_line, *cots[1:3])
+    y, _, *late = scan_part(half, plan.blocks, early_y, early_state)
     piece_shape = (rows, WIDTH)
     w_gate, z, du, stats, *outs = call(
         gate_kernel, plan,
@@ -885,7 +902,7 @@
     def reduce_line(keep, send, body, name):
         got = swap(send, "batch", 1)
         parts = call(
-            body, plan, [(keep.shape[1:], bf16)] * line, [], keep, got, name=name,
+            body, plan, [(keep.shape[1:], bf16)] * line, [], keep, got, name=name, micros=LATE,
         )
         return list(parts)
 
@@ -894,55 +911,55 @@
 
     gate_half = reduce_line(keep, send, gate_split_kernel, "gate_core_sum")
     dy = after(dy, *gate_half)
-    back_in = (x, dt_raw, states, segc, segr, dy, conv, per_head)
-
-    def scan_back_part(first, last, *before):
+    back_in = (x, dt_raw, segc, segr, dy, conv, per_head)
+
+    def scan_back_part(first, last, saved, *before):
         return call(
             lambda p, *refs: scan_back_kernel(p, first, last, *refs), plan,
             [
                 ((total - first * GROUP, plan.cols), bf16), (state_shape, f32),
                 ((LEAD, plan.mixed), f32), ((8, plan.mixed), f32), ((8, LANES), f32),
             ], [],
-            *back_in, *before, mib=16, micros=10, name="scan_backward",
+            *back_in, *saved, *before, mib=16, micros=7, name="scan_backward",
         )
 
-    before = list(scan_back_part(half, plan.blocks))
+    before = list(scan_back_part(half, plan.blocks, late))
     out_parts = [outs[0]] + [swap(outs[m], "seq", m) for m in range(1, n)]
     gate_half[-1] = after(gate_half[-1], before[1])
     gate_lines = line_exchange(gate_half)
     gate_rows, shard_out = call(
         gate_sum_kernel, plan,
         [((n * r // 2, WIDTH), bf16), ((plan.out_rows, WIDTH), f32)], [], *gate_lines,
-        name="gate_sum",
+        name="gate_sum", micros=LATE,
     )
     before[1] = after(before[1], *gate_lines[:-1])
-    gp, _, _, acc, head_acc = scan_back_part(0, half, *before)
+    gp, _, _, acc, head_acc = scan_back_part(0, half, early, *before)
     (result,) = call(
-        result_kernel, plan, [(piece_shape, bf16)], [], tok, scale, *out_parts, name="result"
+        result_kernel, plan, [(piece_shape, bf16)], [], tok, scale, *out_parts, name="result", micros=LATE
     )
 
     grads = call(
         normed_grads_kernel, plan, [(piece_shape, bf16)] * n, [], gp, w_main, dz, w_gate,
-        mib=12, micros=3, name="normed_grads",
+        mib=12, micros=3 * LATE, name="normed_grads",
     )
     gp_late = after(gp, *out_parts, *gate_lines, *grads)
     keep, send = call(
         main_grads_kernel, plan, [((line, n * r + 16, plan.cols), bf16)] * 2,
         [((WIDTH, plan.cols), f32), ((8, plan.cols), f32)],
         normed, gp_late, w_main, gain_row, share, gain_out_grad, acc, head_acc,
-        mib=12, micros=4, name="main_grads",
+        mib=12, micros=4 * LATE, name="main_grads",
     )
     main_half = reduce_line(keep, send, main_split_kernel, "main_core_sum")
     main_lines = line_exchange(main_half)
     grad_parts = [grads[0]] + [swap(grads[m], "seq", m) for m in range(1, n)]
     last = call(
         row_sum_kernel, plan, [((2 * r + 16, plan.cols), bf16)] * n, [], gate_rows, *main_lines,
-        name="main_sum",
+        name="main_sum", micros=LATE,
     )
     last = [last[0]] + [swap(last[m], "seq", m) for m in range(1, n)]
     (grad_tokens,) = call(
         token_kernel, plan, [(piece_shape, bf16)], [], tok, cot, gain_row, *grad_parts,
-        name="token_grad",
+        name="token_grad", micros=LATE,
     )
     shard_in, *smalls = call(
         columns_kernel, plan,
@@ -952,7 +969,7 @@
             ((1, HEADS), f32), ((1, HEADS), f32), ((INNER,), f32),
         ],
         [((n, r, chan), f32), ((n, r, plan.cols), f32), ((n, 8, plan.cols), f32)],
-        *last, name="columns",
+        *last, name="columns", micros=LATE,
     )
     return (
         result[None], grad_tokens[None], shard_in, shard_out, smalls[0], smalls[1],

time: 128 us -> 125 us (0.977)
  Pallas kernels: 41 us -> 35.9 us
  waiting for transfers between devices: 43.8 us -> 45.3 us
    pallas_call x19, Pallas kernels: 41 us -> 35.9 us  [call(): pl.pallas_call(functools.partial(body, plan), out_shape=shapes, in_specs=...]
    ppermute x43, waiting for transfers between devices: 43.8 us -> 45.3 us  [swap(): return lax.ppermute(value, axis, [(i, i ^ by) for i in range(size)])]
  transfers between devices with their start and end apart: 43 -> 43, of which waited for: 14 -> 21; matrix products, arithmetic and copies ran while one was open for 0% -> 0% of each run, Pallas kernels for 24% -> 20%
where the time goes in v4:
time: 125 us
  waiting for transfers between devices  45.3 us (36%)
  starting transfers between devices  41.8 us (33%)
  Pallas kernels  35.9 us (29%)
    ppermute x43, waiting for transfers between devices, swap(): return lax.ppermute(value, axis, [(i, i ^ by) for i in range(size)])  45.3 us
    ppermute x43, starting transfers between devices, swap(): return lax.ppermute(value, axis, [(i, i ^ by) for i in range(size)])  41.8 us
    pallas_call x19, Pallas kernels, call(): pl.pallas_call(functools.partial(body, plan), out_shape=shapes, in_specs=...  35.9 us
  transfers between devices with their start and end apart: 43, of which 21 were waited for; matrix products, arithmetic and copies ran while one was open for 0% of the time, Pallas kernels for 20%

profile of v4, /device:TPU:8, one launch (start us, length us, event | category | flops | bytes accessed | tf_op | source)
XLA Modules:
  0.0 125.0 jit_solution(4269057104552303899)
XLA Ops:
  0.7 1.8 %pack.1 = (bf16[32,1152]{1,0:T(8,128)(2,1)}, bf16[32,1152]{1,0:T(8,128)(2,1)}, bf16[32,1152]{1,0:T(8,128)(2,1)}, bf16[32,1152]{1,0:T(8,128)(2,1)}) custom-call(bf16[24,3352]{1,0:T(8,128)(2,1)} %w_any.1, s32[1,256]{1,0:T(1,128)} %seg_any.1), custom_call_target="tpu_custom_call" | custom-call | flops 3000000000 | tf_op jit(solution)/shard_map/pack/pallas_call | solution.py:765
  8.6 2.4 %collective-permute-done.2.refs_3_.refs_7_ = bf16[32,1152]{1,0:T(8,128)(2,1)S(1)} collective-permute-done((bf16[32,1152]{1,0:T(8,128)(2,1)}, bf16[32,1152]{1,0:T(8,128)(2,1)S(1)}, u32[]{:S(2)}, u32[]{:S(2)}) %collective-permute-start.2) | collective-permute-done | bytes 73760 | tf_op jit(solution)/shard_map/ppermute | solution.py:788
  18.1 7.1 %collective-permute-done.8.refs_11_ = bf16[96,768]{1,0:T(8,128)(2,1)S(1)} collective-permute-done((bf16[96,768]{1,0:T(8,128)(2,1)S(1)}, bf16[96,768]{1,0:T(8,128)(2,1)S(1)}, u32[]{:S(2)}, u32[]{:S(2)}) %collective-permute-start.8) | collective-permute-done | bytes 147488 | tf_op jit(solution)/shard_map/ppermute | solution.py:788
  27.0 2.4 %collective-permute-done.4.refs_2_ = bf16[256,768]{1,0:T(8,128)(2,1)S(1)} collective-permute-done((bf16[256,768]{1,0:T(8,128)(2,1)S(1)}, bf16[256,768]{1,0:T(8,128)(2,1)S(1)}, u32[]{:S(2)}, u32[]{:S(2)}) %collective-permute-start.4) | collective-permute-done | bytes 393248 | tf_op jit(solution)/shard_map/ppermute | solution.py:788
  29.8 3.2 %collective-permute-done.3.refs_1_ = bf16[256,768]{1,0:T(8,128)(2,1)S(1)} collective-permute-done((bf16[256,768]{1,0:T(8,128)(2,1)S(1)}, bf16[256,768]{1,0:T(8,128)(2,1)S(1)}, u32[]{:S(2)}, u32[]{:S(2)}) %collective-permute-start.3) | collective-permute-done | bytes 393248 | tf_op jit(solution)/shard_map/ppermute | solution.py:788
  33.0 2.1 %collective-permute-start.15 = (bf16[96,768]{1,0:T(8,128)(2,1)S(1)}, bf16[96,768]{1,0:T(8,128)(2,1)S(1)}, u32[]{:S(2)}, u32[]{:S(2)}) collective-permute-start(bf16[96,768]{1,0:T(8,128)(2,1)S(1)} %get-tuple-element.120.refs_2_), channel_id=1, source_target_pairs={{0,6},{1,7},{2,4},{3,5},{4,2},{5,3},{6,0},{7,1},{8,14},{9,15},{10,... | collective-permute-start | bytes 442376 | tf_op jit(solution)/shard_map/ppermute | solution.py:788
  38.2 1.7 %project.1 = (bf16[1024,768]{1,0:T(8,128)(2,1)S(1)}, bf16[768,768]{1,0:T(8,128)(2,1)S(1)}, f32[1032,640]{1,0:T(8,128)S(1)}, f32[1024,128]{1,0:T(8,128)S(1)}, f32...) custom-call(bf16[256,768]{1,0:T(8,128)(2,1)S(1)} %bitcast.13, bf16[256,768]{1,0:T(8,128)(2,1)S(1)} %collective-permute-done.3.refs_1_, ...), custom_call_target="tpu_custom_call" | custom-call | flops 15000000512 | tf_op jit(solution)/shard_map/project/pallas_call | solution.py:765
  39.9 3.1 %scan_forward.2 = (f32[512,384]{1,0:T(8,128)S(1)}, f32[128,384]{1,0:T(8,128)S(1)}, f32[4,128,384]{2,1,0:T(8,128)S(1)}, f32[512,640]{1,0:T(8,128)S(1)}, f32[512,6...) custom-call(f32[1032,640]{1,0:T(8,128)S(1)} %get-tuple-element.110.refs_0_, ...), custom_call_target="tpu_custom_call" | custom-call | flops 12000000000 | tf_op jit(solution)/shard_map/scan_forward/pallas_call | solution.py:765
  47.2 3.8 %scan_forward.3 = (f32[1024,384]{1,0:T(8,128)S(1)}, f32[128,384]{1,0:T(8,128)}, f32[4,128,384]{2,1,0:T(8,128)S(1)}, f32[512,640]{1,0:T(8,128)S(1)}, f32[512,640]...) custom-call(f32[1032,640]{1,0:T(8,128)S(1)} %get-tuple-element.110.refs_0_, ...), custom_call_target="tpu_custom_call" | custom-call | flops 12000000000 | tf_op jit(solution)/shard_map/scan_forward/pallas_call | solution.py:765
  51.1 3.4 %collective-permute-done.22.refs_13_.refs_12_ = bf16[256,768]{1,0:T(8,128)(2,1)S(1)} collective-permute-done((bf16[256,768]{1,0:T(8,128)(2,1)S(1)}, bf16[256,768]{1,0:T(8,128)(2,1)S(1)}, u32[]{:S(2)}, u32[]{:S(2)}) %collective-permute-start.22) | collective-permute-done | bytes 393248 | tf_op jit(solution)/shard_map/ppermute | solution.py:788
  54.5 3.2 %gate_forward.1 = (bf16[768,384]{1,0:T(8,128)(2,1)S(1)}, f32[1024,384]{1,0:T(8,128)S(1)}, f32[1024,384]{1,0:T(8,128)S(1)}, f32[16,128]{1,0:T(8,128)S(1)}, bf16[2...) custom-call(bf16[1024,768]{1,0:T(8,128)(2,1)S(1)} %get-tuple-element, ...), custom_call_target="tpu_custom_call" | custom-call | flops 17999998976 | tf_op jit(solution)/shard_map/gate_forward/pallas_call | solution.py:765
  63.8 2.9 %gate_backward.1 = (f32[1024,384]{1,0:T(8,128)S(1)}, bf16[1024,384]{1,0:T(8,128)(2,1)S(1)}, f32[1024,128]{1,0:T(8,128)S(1)}, f32[1,384]{1,0:T(1,128)S(1)}, f32[8...) custom-call(f32[16,128]{1,0:T(8,128)S(1)} %get-tuple-element.129.refs_0_, ...), custom_call_target="tpu_custom_call" | custom-call | flops 17999998976 | tf_op jit(solution)/shard_map/gate_backward/pallas_call | solution.py:765
  68.6 1.7 %collective-permute-start.28 = (bf16[256,768]{1,0:T(8,128)(2,1)S(1)}, bf16[256,768]{1,0:T(8,128)(2,1)S(1)}, u32[]{:S(2)}, u32[]{:S(2)}) collective-permute-start(bf16[256,768]{1,0:T(8,128)(2,1)S(1)} %get-tuple-element.137), channel_id=1, source_target_pairs={{0,24},{8,16},{16,8},{24,0},{1,25},{9,17},{17,9},{25,1},{2,26},{10... | collective-permute-start | bytes 1179656 | tf_op jit(solution)/shard_map/ppermute | solution.py:788
  71.1 2.8 %collective-permute-start.31 = (bf16[96,768]{1,0:T(8,128)(2,1)S(1)}, bf16[96,768]{1,0:T(8,128)(2,1)S(1)}, u32[]{:S(2)}, u32[]{:S(2)}) collective-permute-start(bf16[96,768]{1,0:T(8,128)(2,1)S(1)} %get-tuple-element.143), channel_id=1, source_target_pairs={{0,4},{1,5},{2,6},{3,7},{4,0},{5,1},{6,2},{7,3},{8,12},{9,13},{10,... | collective-permute-start | bytes 442376 | tf_op jit(solution)/shard_map/ppermute | solution.py:788
  74.0 5.1 %scan_backward.2 = (bf16[512,768]{1,0:T(8,128)(2,1)S(1)}, f32[128,384]{1,0:T(8,128)S(1)}, f32[8,640]{1,0:T(8,128)S(1)}, f32[8,640]{1,0:T(8,128)S(1)}, f32[8,128]{1,0:T(8,128)S(1)}) custom-call(f32[1032,640]{1,0:T(8,128)S(1)} %get-tuple-element.110.refs_0_, f32[1024,128]{1,0:T(8,128)S(1)} %get-tuple-element.111.refs_1_, ...), custom_call_target="tpu_custom_call" | custom-call | flops 20999999488 | tf_op jit(solution)/shard_map/scan_backward/pallas_call | solution.py:765
  79.3 3.0 %collective-permute-done.31.refs_2_ = bf16[96,768]{1,0:T(8,128)(2,1)S(1)} collective-permute-done((bf16[96,768]{1,0:T(8,128)(2,1)S(1)}, bf16[96,768]{1,0:T(8,128)(2,1)S(1)}, u32[]{:S(2)}, u32[]{:S(2)}) %collective-permute-start.31) | collective-permute-done | bytes 147488 | tf_op jit(solution)/shard_map/ppermute | solution.py:788
  82.3 5.8 %scan_backward.3 = (bf16[1024,768]{1,0:T(8,128)(2,1)S(1)}, f32[128,384]{1,0:T(8,128)}, f32[8,640]{1,0:T(8,128)}, f32[8,640]{1,0:T(8,128)S(1)}, f32[8,128]{1,0:T(8,128)S(1)}) custom-call(f32[1032,640]{1,0:T(8,128)S(1)} %get-tuple-element.110.refs_0_, f32[1024,128]{1,0:T(8,128)S(1)} %get-tuple-element.111.refs_1_, f32[1040,128]{1,0:T(8,128)S(1)} %get-tuple-element.112.refs_2_, ...), custom_call_target="tpu_custom_call" | custom-call | flops 20999999488 | tf_op jit(solution)/shard_map/scan_backward/pallas_call | solution.py:765
  88.1 2.2 %normed_grads.1 = (bf16[256,768]{1,0:T(8,128)(2,1)S(1)}, bf16[256,768]{1,0:T(8,128)(2,1)S(1)}, bf16[256,768]{1,0:T(8,128)(2,1)S(1)}, bf16[256,768]{1,0:T(8,128)(2,1)S(1)}) custom-call(bf16[1024,768]{1,0:T(8,128)(2,1)S(1)} %get-tuple-element.171.gp_ref, bf16[768,768]{1,0:T(8,128)(2,1)S(1)} %get-tuple-element.163.w_ref, ...), custom_call_target="tpu_custom_call" | custom-call | flops 35999997952 | tf_op jit(solution)/shard_map/normed_grads/pallas_call | solution.py:765
  95.3 4.4 %collective-permute-start.38 = (bf16[112,768]{1,0:T(8,128)(2,1)S(1)}, bf16[112,768]{1,0:T(8,128)(2,1)S(1)}, u32[]{:S(2)}, u32[]{:S(2)}) collective-permute-start(bf16[112,768]{1,0:T(8,128)(2,1)S(1)} %get-tuple-element.180), channel_id=1, source_target_pairs={{0,4},{1,5},{2,6},{3,7},{4,0},{5,1},{6,2},{7,3},{8,12},{9,13},{10,... | collective-permute-start | bytes 516104 | tf_op jit(solution)/shard_map/ppermute | solution.py:788
  101.5 1.8 %collective-permute-start.34 = (bf16[256,768]{1,0:T(8,128)(2,1)S(1)}, bf16[256,768]{1,0:T(8,128)(2,1)S(1)}, u32[]{:S(2)}, u32[]{:S(2)}) collective-permute-start(bf16[256,768]{1,0:T(8,128)(2,1)S(1)} %get-tuple-element.168), channel_id=1, source_target_pairs={{0,24},{8,16},{16,8},{24,0},{1,25},{9,17},{17,9},{25,1},{2,26},{10... | collective-permute-start | bytes 1179656 | tf_op jit(solution)/shard_map/ppermute | solution.py:788
  103.3 8.6 %collective-permute-done.38.refs_2_ = bf16[112,768]{1,0:T(8,128)(2,1)S(1)} collective-permute-done((bf16[112,768]{1,0:T(8,128)(2,1)S(1)}, bf16[112,768]{1,0:T(8,128)(2,1)S(1)}, u32[]{:S(2)}, u32[]{:S(2)}) %collective-permute-start.38) | collective-permute-done | bytes 172064 | tf_op jit(solution)/shard_map/ppermute | solution.py:788
  111.9 3.8 %collective-permute-done.39.refs_3_ = bf16[112,768]{1,0:T(8,128)(2,1)S(1)} collective-permute-done((bf16[112,768]{1,0:T(8,128)(2,1)S(1)}, bf16[112,768]{1,0:T(8,128)(2,1)S(1)}, u32[]{:S(2)}, u32[]{:S(2)}) %collective-permute-start.39) | collective-permute-done | bytes 172064 | tf_op jit(solution)/shard_map/ppermute | solution.py:788
  116.8 1.7 %collective-permute-start.41 = (bf16[64,768]{1,0:T(8,128)(2,1)S(1)}, bf16[64,768]{1,0:T(8,128)(2,1)S(1)}, u32[]{:S(2)}, u32[]{:S(2)}) collective-permute-start(bf16[64,768]{1,0:T(8,128)(2,1)S(1)} %get-tuple-element.184), channel_id=1, source_target_pairs={{0,16},{8,24},{16,0},{24,8},{1,17},{9,25},{17,1},{25,9},{2,18},{10... | collective-permute-start | bytes 294920 | tf_op jit(solution)/shard_map/ppermute | solution.py:788
  122.3 1.8 %collective-permute-done.42.refs_3_ = bf16[64,768]{1,0:T(8,128)(2,1)S(1)} collective-permute-done((bf16[64,768]{1,0:T(8,128)(2,1)S(1)}, bf16[64,768]{1,0:T(8,128)(2,1)S(1)}, u32[]{:S(2)}, u32[]{:S(2)}) %collective-permute-start.42) | collective-permute-done | bytes 98336 | tf_op jit(solution)/shard_map/ppermute | solution.py:788
  (114 shorter events, 44.0 us)
Async XLA Ops:
  11.0 15.9 %collective-permute-start.5 = (bf16[256,768]{1,0:T(8,128)(2,1)S(1)}, bf16[256,768]{1,0:T(8,128)(2,1)S(1)}, u32[]{:S(2)}, u32[]{:S(2)}) collective-permute-start(bf16[256,768]{1,0:T(8,128)(2,1)S(1)} %bitcast.10), channel_id=1, source_target_pairs={{0,24},{8,16},{16,8},{24,0},{1,25},{9,17},{17,9},{25,1},{2,26},{10... | collective-permute-start | bytes 1179656 | tf_op jit(solution)/shard_map/ppermute | solution.py:788
  11.6 17.9 %collective-permute-start.4 = (bf16[256,768]{1,0:T(8,128)(2,1)S(1)}, bf16[256,768]{1,0:T(8,128)(2,1)S(1)}, u32[]{:S(2)}, u32[]{:S(2)}) collective-permute-start(bf16[256,768]{1,0:T(8,128)(2,1)S(1)} %bitcast.11), channel_id=1, source_target_pairs={{0,16},{8,24},{16,0},{24,8},{1,17},{9,25},{17,1},{25,9},{2,18},{10... | collective-permute-start | bytes 1179656 | tf_op jit(solution)/shard_map/ppermute | solution.py:788
  14.0 11.2 %collective-permute-start.8 = (bf16[96,768]{1,0:T(8,128)(2,1)S(1)}, bf16[96,768]{1,0:T(8,128)(2,1)S(1)}, u32[]{:S(2)}, u32[]{:S(2)}) collective-permute-start(bf16[96,768]{1,0:T(8,128)(2,1)S(1)} %get-tuple-element.108.refs_8_), channel_id=1, source_target_pairs={{0,6},{1,7},{2,4},{3,5},{4,2},{5,3},{6,0},{7,1},{8,14},{9,15},{10,... | collective-permute-start | bytes 442376 | tf_op jit(solution)/shard_map/ppermute | solution.py:788
  15.6 10.8 %collective-permute-start.7 = (bf16[96,768]{1,0:T(8,128)(2,1)S(1)}, bf16[96,768]{1,0:T(8,128)(2,1)S(1)}, u32[]{:S(2)}, u32[]{:S(2)}) collective-permute-start(bf16[96,768]{1,0:T(8,128)(2,1)S(1)} %get-tuple-element.108.refs_8_), channel_id=1, source_target_pairs={{0,4},{1,5},{2,6},{3,7},{4,0},{5,1},{6,2},{7,3},{8,12},{9,13},{10,... | collective-permute-start | bytes 442376 | tf_op jit(solution)/shard_map/ppermute | solution.py:788
  16.9 9.6 %collective-permute-start.6 = (bf16[96,768]{1,0:T(8,128)(2,1)S(1)}, bf16[96,768]{1,0:T(8,128)(2,1)S(1)}, u32[]{:S(2)}, u32[]{:S(2)}) collective-permute-start(bf16[96,768]{1,0:T(8,128)(2,1)S(1)} %get-tuple-element.108.refs_8_), channel_id=1, source_target_pairs={{0,2},{1,3},{2,0},{3,1},{4,6},{5,7},{6,4},{7,5},{8,10},{9,11},{10,... | collective-permute-start | bytes 442376 | tf_op jit(solution)/shard_map/ppermute | solution.py:788
  26.5 8.7 %collective-permute-start.9 = (bf16[96,768]{1,0:T(8,128)(2,1)S(1)}, bf16[96,768]{1,0:T(8,128)(2,1)S(1)}, u32[]{:S(2)}, u32[]{:S(2)}) collective-permute-start(bf16[96,768]{1,0:T(8,128)(2,1)S(1)} %get-tuple-element.108.refs_8_), channel_id=1, source_target_pairs={{0,1},{1,0},{2,3},{3,2},{4,5},{5,4},{6,7},{7,6},{8,9},{9,8},{10,11... | collective-permute-start | bytes 442376 | tf_op jit(solution)/shard_map/ppermute | solution.py:788
  26.5 8.7 %collective-permute-start.12 = (bf16[96,768]{1,0:T(8,128)(2,1)S(1)}, bf16[96,768]{1,0:T(8,128)(2,1)S(1)}, u32[]{:S(2)}, u32[]{:S(2)}) collective-permute-start(bf16[96,768]{1,0:T(8,128)(2,1)S(1)} %collective-permute-done.8.refs_11_), channel_id=1, source_target_pairs={{0,1},{1,0},{2,3},{3,2},{4,5},{5,4},{6,7},{7,6},{8,9},{9,8},{10,11... | collective-permute-start | bytes 442376 | tf_op jit(solution)/shard_map/ppermute | solution.py:788
  27.0 9.6 %collective-permute-start.11 = (bf16[96,768]{1,0:T(8,128)(2,1)S(1)}, bf16[96,768]{1,0:T(8,128)(2,1)S(1)}, u32[]{:S(2)}, u32[]{:S(2)}) collective-permute-start(bf16[96,768]{1,0:T(8,128)(2,1)S(1)} %collective-permute-done.7.refs_10_), channel_id=1, source_target_pairs={{0,1},{1,0},{2,3},{3,2},{4,5},{5,4},{6,7},{7,6},{8,9},{9,8},{10,11... | collective-permute-start | bytes 442376 | tf_op jit(solution)/shard_map/ppermute | solution.py:788
  33.0 10.4 %collective-permute-start.15 = (bf16[96,768]{1,0:T(8,128)(2,1)S(1)}, bf16[96,768]{1,0:T(8,128)(2,1)S(1)}, u32[]{:S(2)}, u32[]{:S(2)}) collective-permute-start(bf16[96,768]{1,0:T(8,128)(2,1)S(1)} %get-tuple-element.120.refs_2_), channel_id=1, source_target_pairs={{0,6},{1,7},{2,4},{3,5},{4,2},{5,3},{6,0},{7,1},{8,14},{9,15},{10,... | collective-permute-start | bytes 442376 | tf_op jit(solution)/shard_map/ppermute | solution.py:788
  35.1 9.9 %collective-permute-start.14 = (bf16[96,768]{1,0:T(8,128)(2,1)S(1)}, bf16[96,768]{1,0:T(8,128)(2,1)S(1)}, u32[]{:S(2)}, u32[]{:S(2)}) collective-permute-start(bf16[96,768]{1,0:T(8,128)(2,1)S(1)} %get-tuple-element.120.refs_2_), channel_id=1, source_target_pairs={{0,4},{1,5},{2,6},{3,7},{4,0},{5,1},{6,2},{7,3},{8,12},{9,13},{10,... | collective-permute-start | bytes 442376 | tf_op jit(solution)/shard_map/ppermute | solution.py:788
  35.1 9.9 %collective-permute-start.13 = (bf16[96,768]{1,0:T(8,128)(2,1)S(1)}, bf16[96,768]{1,0:T(8,128)(2,1)S(1)}, u32[]{:S(2)}, u32[]{:S(2)}) collective-permute-start(bf16[96,768]{1,0:T(8,128)(2,1)S(1)} %get-tuple-element.120.refs_2_), channel_id=1, source_target_pairs={{0,2},{1,3},{2,0},{3,1},{4,6},{5,7},{6,4},{7,5},{8,10},{9,11},{10,... | collective-permute-start | bytes 442376 | tf_op jit(solution)/shard_map/ppermute | solution.py:788
  36.6 9.6 %collective-permute-start.17 = (bf16[256,768]{1,0:T(8,128)(2,1)S(1)}, bf16[256,768]{1,0:T(8,128)(2,1)S(1)}, u32[]{:S(2)}, u32[]{:S(2)}) collective-permute-start(bf16[256,768]{1,0:T(8,128)(2,1)S(1)} %bitcast.16), channel_id=1, source_target_pairs={{0,16},{8,24},{16,0},{24,8},{1,17},{9,25},{17,1},{25,9},{2,18},{10... | collective-permute-start | bytes 1179656 | tf_op jit(solution)/shard_map/ppermute | solution.py:788
  37.2 10.0 %collective-permute-start.16 = (bf16[256,768]{1,0:T(8,128)(2,1)S(1)}, bf16[256,768]{1,0:T(8,128)(2,1)S(1)}, u32[]{:S(2)}, u32[]{:S(2)}) collective-permute-start(bf16[256,768]{1,0:T(8,128)(2,1)S(1)} %bitcast.17), channel_id=1, source_target_pairs={{0,8},{8,0},{16,24},{24,16},{1,9},{9,1},{17,25},{25,17},{2,10},{10... | collective-permute-start | bytes 1179656 | tf_op jit(solution)/shard_map/ppermute | solution.py:788
  43.4 11.1 %collective-permute-start.22 = (bf16[256,768]{1,0:T(8,128)(2,1)S(1)}, bf16[256,768]{1,0:T(8,128)(2,1)S(1)}, u32[]{:S(2)}, u32[]{:S(2)}) collective-permute-start(bf16[256,768]{1,0:T(8,128)(2,1)S(1)} %bitcast.18), channel_id=1, source_target_pairs={{0,24},{8,16},{16,8},{24,0},{1,25},{9,17},{17,9},{25,1},{2,26},{10... | collective-permute-start | bytes 1179656 | tf_op jit(solution)/shard_map/ppermute | solution.py:788
  66.8 23.6 %collective-permute-start.26 = (bf16[256,768]{1,0:T(8,128)(2,1)S(1)}, bf16[256,768]{1,0:T(8,128)(2,1)S(1)}, u32[]{:S(2)}, u32[]{:S(2)}) collective-permute-start(bf16[256,768]{1,0:T(8,128)(2,1)S(1)} %get-tuple-element.135), channel_id=1, source_target_pairs={{0,8},{8,0},{16,24},{24,16},{1,9},{9,1},{17,25},{25,17},{2,10},{10... | collective-permute-start | bytes 1179656 | tf_op jit(solution)/shard_map/ppermute | solution.py:788
  67.9 22.4 %collective-permute-start.27 = (bf16[256,768]{1,0:T(8,128)(2,1)S(1)}, bf16[256,768]{1,0:T(8,128)(2,1)S(1)}, u32[]{:S(2)}, u32[]{:S(2)}) collective-permute-start(bf16[256,768]{1,0:T(8,128)(2,1)S(1)} %get-tuple-element.136), channel_id=1, source_target_pairs={{0,16},{8,24},{16,0},{24,8},{1,17},{9,25},{17,1},{25,9},{2,18},{10... | collective-permute-start | bytes 1179656 | tf_op jit(solution)/shard_map/ppermute | solution.py:788
  68.6 21.8 %collective-permute-start.28 = (bf16[256,768]{1,0:T(8,128)(2,1)S(1)}, bf16[256,768]{1,0:T(8,128)(2,1)S(1)}, u32[]{:S(2)}, u32[]{:S(2)}) collective-permute-start(bf16[256,768]{1,0:T(8,128)(2,1)S(1)} %get-tuple-element.137), channel_id=1, source_target_pairs={{0,24},{8,16},{16,8},{24,0},{1,25},{9,17},{17,9},{25,1},{2,26},{10... | collective-permute-start | bytes 1179656 | tf_op jit(solution)/shard_map/ppermute | solution.py:788
  71.1 11.1 %collective-permute-start.31 = (bf16[96,768]{1,0:T(8,128)(2,1)S(1)}, bf16[96,768]{1,0:T(8,128)(2,1)S(1)}, u32[]{:S(2)}, u32[]{:S(2)}) collective-permute-start(bf16[96,768]{1,0:T(8,128)(2,1)S(1)} %get-tuple-element.143), channel_id=1, source_target_pairs={{0,4},{1,5},{2,6},{3,7},{4,0},{5,1},{6,2},{7,3},{8,12},{9,13},{10,... | collective-permute-start | bytes 442376 | tf_op jit(solution)/shard_map/ppermute | solution.py:788
  79.1 11.3 %collective-permute-start.35 = (bf16[96,768]{1,0:T(8,128)(2,1)S(1)}, bf16[96,768]{1,0:T(8,128)(2,1)S(1)}, u32[]{:S(2)}, u32[]{:S(2)}) collective-permute-start(bf16[96,768]{1,0:T(8,128)(2,1)S(1)} %get-tuple-element.169), channel_id=1, source_target_pairs={{0,6},{1,7},{2,4},{3,5},{4,2},{5,3},{6,0},{7,1},{8,14},{9,15},{10,... | collective-permute-start | bytes 442376 | tf_op jit(solution)/shard_map/ppermute | solution.py:788
  93.2 25.3 %collective-permute-start.32 = (bf16[256,768]{1,0:T(8,128)(2,1)S(1)}, bf16[256,768]{1,0:T(8,128)(2,1)S(1)}, u32[]{:S(2)}, u32[]{:S(2)}) collective-permute-start(bf16[256,768]{1,0:T(8,128)(2,1)S(1)} %get-tuple-element.166), channel_id=1, source_target_pairs={{0,8},{8,0},{16,24},{24,16},{1,9},{9,1},{17,25},{25,17},{2,10},{10... | collective-permute-start | bytes 1179656 | tf_op jit(solution)/shard_map/ppermute | solution.py:788
  94.3 25.0 %collective-permute-start.33 = (bf16[256,768]{1,0:T(8,128)(2,1)S(1)}, bf16[256,768]{1,0:T(8,128)(2,1)S(1)}, u32[]{:S(2)}, u32[]{:S(2)}) collective-permute-start(bf16[256,768]{1,0:T(8,128)(2,1)S(1)} %get-tuple-element.167), channel_id=1, source_target_pairs={{0,16},{8,24},{16,0},{24,8},{1,17},{9,25},{17,1},{25,9},{2,18},{10... | collective-permute-start | bytes 1179656 | tf_op jit(solution)/shard_map/ppermute | solution.py:788
  95.3 16.6 %collective-permute-start.38 = (bf16[112,768]{1,0:T(8,128)(2,1)S(1)}, bf16[112,768]{1,0:T(8,128)(2,1)S(1)}, u32[]{:S(2)}, u32[]{:S(2)}) collective-permute-start(bf16[112,768]{1,0:T(8,128)(2,1)S(1)} %get-tuple-element.180), channel_id=1, source_target_pairs={{0,4},{1,5},{2,6},{3,7},{4,0},{5,1},{6,2},{7,3},{8,12},{9,13},{10,... | collective-permute-start | bytes 516104 | tf_op jit(solution)/shard_map/ppermute | solution.py:788
  99.7 15.9 %collective-permute-start.39 = (bf16[112,768]{1,0:T(8,128)(2,1)S(1)}, bf16[112,768]{1,0:T(8,128)(2,1)S(1)}, u32[]{:S(2)}, u32[]{:S(2)}) collective-permute-start(bf16[112,768]{1,0:T(8,128)(2,1)S(1)} %get-tuple-element.181), channel_id=1, source_target_pairs={{0,6},{1,7},{2,4},{3,5},{4,2},{5,3},{6,0},{7,1},{8,14},{9,15},{10,... | collective-permute-start | bytes 516104 | tf_op jit(solution)/shard_map/ppermute | solution.py:788
  101.5 17.8 %collective-permute-start.34 = (bf16[256,768]{1,0:T(8,128)(2,1)S(1)}, bf16[256,768]{1,0:T(8,128)(2,1)S(1)}, u32[]{:S(2)}, u32[]{:S(2)}) collective-permute-start(bf16[256,768]{1,0:T(8,128)(2,1)S(1)} %get-tuple-element.168), channel_id=1, source_target_pairs={{0,24},{8,16},{16,8},{24,0},{1,25},{9,17},{17,9},{25,1},{2,26},{10... | collective-permute-start | bytes 1179656 | tf_op jit(solution)/shard_map/ppermute | solution.py:788
  (34 other events, 268.9 us)

commit v5 on v4

--- a/solution.py
+++ b/solution.py
@@ -811,11 +811,10 @@
             (in_weight.shape, bf16), (segments.shape, jnp.int32), pltpu.SemaphoreType.DMA((2,)),
             ((n, r, plan.cols + chan), bf16),
         ],
-        in_weight, segments, mib=60, name="pack", kept=2,
+        in_weight, segments, name="pack", kept=2,
     )
     pieces = [own[0]] + [swap(own[m], "seq", m) for m in range(1, n)]
-    tok_later = after(tok, *pieces)
-    toks = [tok] + [swap(tok_later, "seq", m) for m in range(1, n)]
+    toks = [tok] + [swap(after(tok, pieces[m]), "seq", m) for m in range(1, n)]
     main_shard, gate_shard = call(
         regroup_kernel, plan,
         [((n * r, plan.cols), bf16), ((n * r // 2 + plan.out_rows, WIDTH), bf16)], [],

time: 125 us -> 120 us (0.960)
  waiting for transfers between devices: 45.3 us -> 42.8 us
  starting transfers between devices: 41.8 us -> 40 us
  Pallas kernels: 35.9 us -> 34.4 us
    ppermute x43, waiting for transfers between devices: 45.3 us -> 42.8 us  [swap(): return lax.ppermute(value, axis, [(i, i ^ by) for i in range(size)])]
    ppermute x43, starting transfers between devices: 41.8 us -> 40 us  [swap(): return lax.ppermute(value, axis, [(i, i ^ by) for i in range(size)])]
    pallas_call x19, Pallas kernels: 35.9 us -> 34.4 us  [call(): pl.pallas_call(functools.partial(body, plan), out_shape=shapes, in_specs=...]
  transfers between devices with their start and end apart: 43 -> 43, of which waited for: 21 -> 20; matrix products, arithmetic and copies ran while one was open for 0% -> 0% of each run, Pallas kernels for 20% -> 21%
where the time goes in v5:
time: 120 us
  waiting for transfers between devices  42.8 us (36%)
  starting transfers between devices  40 us (33%)
  Pallas kernels  34.4 us (29%)
  local copies, waits for them, and re-layouts  1.73 us (1%)
    ppermute x43, waiting for transfers between devices, swap(): return lax.ppermute(value, axis, [(i, i ^ by) for i in range(size)])  42.8 us
    ppermute x43, starting transfers between devices, swap(): return lax.ppermute(value, axis, [(i, i ^ by) for i in range(size)])  40 us
    pallas_call x19, Pallas kernels, call(): pl.pallas_call(functools.partial(body, plan), out_shape=shapes, in_specs=...  34.4 us
  transfers between devices with their start and end apart: 43, of which 20 were waited for; matrix products, arithmetic and copies ran while one was open for 0% of the time, Pallas kernels for 21%

profile of v5, /device:TPU:8, one launch (start us, length us, event | category | flops | bytes accessed | tf_op | source)
XLA Modules:
  0.0 119.9 jit_solution(1929624101491317714)
XLA Ops:
  7.0 3.0 %collective-permute-done.4.refs_3_.refs_7_ = bf16[32,1152]{1,0:T(8,128)(2,1)S(1)} collective-permute-done((bf16[32,1152]{1,0:T(8,128)(2,1)S(1)}, bf16[32,1152]{1,0:T(8,128)(2,1)S(1)}, u32[]{:S(2)}, u32[]{:S(2)}) %collective-permute-start.4) | collective-permute-done | bytes 73760 | tf_op jit(solution)/shard_map/ppermute | solution.py:788
  12.7 1.6 %collective-permute-start.8 = (bf16[96,768]{1,0:T(8,128)(2,1)S(1)}, bf16[96,768]{1,0:T(8,128)(2,1)S(1)}, u32[]{:S(2)}, u32[]{:S(2)}) collective-permute-start(bf16[96,768]{1,0:T(8,128)(2,1)S(1)} %get-tuple-element.112.refs_8_), channel_id=1, source_target_pairs={{0,6},{1,7},{2,4},{3,5},{4,2},{5,3},{6,0},{7,1},{8,14},{9,15},{10,... | collective-permute-start | bytes 442376 | tf_op jit(solution)/shard_map/ppermute | solution.py:788
  16.8 6.7 %collective-permute-done.8.refs_11_ = bf16[96,768]{1,0:T(8,128)(2,1)S(1)} collective-permute-done((bf16[96,768]{1,0:T(8,128)(2,1)S(1)}, bf16[96,768]{1,0:T(8,128)(2,1)S(1)}, u32[]{:S(2)}, u32[]{:S(2)}) %collective-permute-start.8) | collective-permute-done | bytes 147488 | tf_op jit(solution)/shard_map/ppermute | solution.py:788
  25.4 2.9 %collective-permute-done.3.refs_2_ = bf16[256,768]{1,0:T(8,128)(2,1)S(1)} collective-permute-done((bf16[256,768]{1,0:T(8,128)(2,1)S(1)}, bf16[256,768]{1,0:T(8,128)(2,1)S(1)}, u32[]{:S(2)}, u32[]{:S(2)}) %collective-permute-start.3) | collective-permute-done | bytes 393248 | tf_op jit(solution)/shard_map/ppermute | solution.py:788
  28.5 2.8 %collective-permute-done.1.refs_1_ = bf16[256,768]{1,0:T(8,128)(2,1)S(1)} collective-permute-done((bf16[256,768]{1,0:T(8,128)(2,1)S(1)}, bf16[256,768]{1,0:T(8,128)(2,1)S(1)}, u32[]{:S(2)}, u32[]{:S(2)}) %collective-permute-start.1) | collective-permute-done | bytes 393248 | tf_op jit(solution)/shard_map/ppermute | solution.py:788
  31.3 2.1 %collective-permute-start.15 = (bf16[96,768]{1,0:T(8,128)(2,1)S(1)}, bf16[96,768]{1,0:T(8,128)(2,1)S(1)}, u32[]{:S(2)}, u32[]{:S(2)}) collective-permute-start(bf16[96,768]{1,0:T(8,128)(2,1)S(1)} %get-tuple-element.124.refs_2_), channel_id=1, source_target_pairs={{0,6},{1,7},{2,4},{3,5},{4,2},{5,3},{6,0},{7,1},{8,14},{9,15},{10,... | collective-permute-start | bytes 442376 | tf_op jit(solution)/shard_map/ppermute | solution.py:788
  36.0 1.7 %project.1 = (bf16[1024,768]{1,0:T(8,128)(2,1)S(1)}, bf16[768,768]{1,0:T(8,128)(2,1)S(1)}, f32[1032,640]{1,0:T(8,128)S(1)}, f32[1024,128]{1,0:T(8,128)S(1)}, f32...) custom-call(bf16[256,768]{1,0:T(8,128)(2,1)S(1)} %bitcast.13, bf16[256,768]{1,0:T(8,128)(2,1)S(1)} %collective-permute-done.1.refs_1_, ...), custom_call_target="tpu_custom_call" | custom-call | flops 15000000512 | tf_op jit(solution)/shard_map/project/pallas_call | solution.py:765
  37.8 3.1 %scan_forward.2 = (f32[512,384]{1,0:T(8,128)S(1)}, f32[128,384]{1,0:T(8,128)S(1)}, f32[4,128,384]{2,1,0:T(8,128)S(1)}, f32[512,640]{1,0:T(8,128)S(1)}, f32[512,6...) custom-call(f32[1032,640]{1,0:T(8,128)S(1)} %get-tuple-element.114.refs_0_, ...), custom_call_target="tpu_custom_call" | custom-call | flops 12000000000 | tf_op jit(solution)/shard_map/scan_forward/pallas_call | solution.py:765
  45.9 3.8 %scan_forward.3 = (f32[1024,384]{1,0:T(8,128)S(1)}, f32[128,384]{1,0:T(8,128)}, f32[4,128,384]{2,1,0:T(8,128)S(1)}, f32[512,640]{1,0:T(8,128)S(1)}, f32[512,640]...) custom-call(f32[1032,640]{1,0:T(8,128)S(1)} %get-tuple-element.114.refs_0_, ...), custom_call_target="tpu_custom_call" | custom-call | flops 12000000000 | tf_op jit(solution)/shard_map/scan_forward/pallas_call | solution.py:765
  49.8 3.5 %collective-permute-done.22.refs_13_.refs_12_ = bf16[256,768]{1,0:T(8,128)(2,1)S(1)} collective-permute-done((bf16[256,768]{1,0:T(8,128)(2,1)S(1)}, bf16[256,768]{1,0:T(8,128)(2,1)S(1)}, u32[]{:S(2)}, u32[]{:S(2)}) %collective-permute-start.22) | collective-permute-done | bytes 393248 | tf_op jit(solution)/shard_map/ppermute | solution.py:788
  53.2 3.2 %gate_forward.1 = (bf16[768,384]{1,0:T(8,128)(2,1)S(1)}, f32[1024,384]{1,0:T(8,128)S(1)}, f32[1024,384]{1,0:T(8,128)S(1)}, f32[16,128]{1,0:T(8,128)S(1)}, bf16[2...) custom-call(bf16[1024,768]{1,0:T(8,128)(2,1)S(1)} %get-tuple-element, ...), custom_call_target="tpu_custom_call" | custom-call | flops 17999998976 | tf_op jit(solution)/shard_map/gate_forward/pallas_call | solution.py:765
  62.5 2.9 %gate_backward.1 = (f32[1024,384]{1,0:T(8,128)S(1)}, bf16[1024,384]{1,0:T(8,128)(2,1)S(1)}, f32[1024,128]{1,0:T(8,128)S(1)}, f32[1,384]{1,0:T(1,128)S(1)}, f32[8...) custom-call(f32[16,128]{1,0:T(8,128)S(1)} %get-tuple-element.133.refs_0_, ...), custom_call_target="tpu_custom_call" | custom-call | flops 17999998976 | tf_op jit(solution)/shard_map/gate_backward/pallas_call | solution.py:765
  67.3 1.7 %collective-permute-start.28 = (bf16[256,768]{1,0:T(8,128)(2,1)S(1)}, bf16[256,768]{1,0:T(8,128)(2,1)S(1)}, u32[]{:S(2)}, u32[]{:S(2)}) collective-permute-start(bf16[256,768]{1,0:T(8,128)(2,1)S(1)} %get-tuple-element.141), channel_id=1, source_target_pairs={{0,24},{8,16},{16,8},{24,0},{1,25},{9,17},{17,9},{25,1},{2,26},{10... | collective-permute-start | bytes 1179656 | tf_op jit(solution)/shard_map/ppermute | solution.py:788
  69.8 2.4 %collective-permute-start.31 = (bf16[96,768]{1,0:T(8,128)(2,1)S(1)}, bf16[96,768]{1,0:T(8,128)(2,1)S(1)}, u32[]{:S(2)}, u32[]{:S(2)}) collective-permute-start(bf16[96,768]{1,0:T(8,128)(2,1)S(1)} %get-tuple-element.147), channel_id=1, source_target_pairs={{0,4},{1,5},{2,6},{3,7},{4,0},{5,1},{6,2},{7,3},{8,12},{9,13},{10,... | collective-permute-start | bytes 442376 | tf_op jit(solution)/shard_map/ppermute | solution.py:788
  72.2 5.0 %scan_backward.2 = (bf16[512,768]{1,0:T(8,128)(2,1)S(1)}, f32[128,384]{1,0:T(8,128)S(1)}, f32[8,640]{1,0:T(8,128)S(1)}, f32[8,640]{1,0:T(8,128)S(1)}, f32[8,128]{1,0:T(8,128)S(1)}) custom-call(f32[1032,640]{1,0:T(8,128)S(1)} %get-tuple-element.114.refs_0_, f32[1024,128]{1,0:T(8,128)S(1)} %get-tuple-element.115.refs_1_, ...), custom_call_target="tpu_custom_call" | custom-call | flops 20999999488 | tf_op jit(solution)/shard_map/scan_backward/pallas_call | solution.py:765
  78.9 5.8 %scan_backward.3 = (bf16[1024,768]{1,0:T(8,128)(2,1)S(1)}, f32[128,384]{1,0:T(8,128)}, f32[8,640]{1,0:T(8,128)}, f32[8,640]{1,0:T(8,128)S(1)}, f32[8,128]{1,0:T(8,128)S(1)}) custom-call(f32[1032,640]{1,0:T(8,128)S(1)} %get-tuple-element.114.refs_0_, f32[1024,128]{1,0:T(8,128)S(1)} %get-tuple-element.115.refs_1_, f32[1040,128]{1,0:T(8,128)S(1)} %get-tuple-element.116.refs_2_, ...), custom_call_target="tpu_custom_call" | custom-call | flops 20999999488 | tf_op jit(solution)/shard_map/scan_backward/pallas_call | solution.py:765
  84.7 2.2 %normed_grads.1 = (bf16[256,768]{1,0:T(8,128)(2,1)S(1)}, bf16[256,768]{1,0:T(8,128)(2,1)S(1)}, bf16[256,768]{1,0:T(8,128)(2,1)S(1)}, bf16[256,768]{1,0:T(8,128)(2,1)S(1)}) custom-call(bf16[1024,768]{1,0:T(8,128)(2,1)S(1)} %get-tuple-element.175.gp_ref, bf16[768,768]{1,0:T(8,128)(2,1)S(1)} %get-tuple-element.167.w_ref, ...), custom_call_target="tpu_custom_call" | custom-call | flops 35999997952 | tf_op jit(solution)/shard_map/normed_grads/pallas_call | solution.py:765
  87.0 1.7 %main_grads.1 = (bf16[4,112,768]{2,1,0:T(8,128)(2,1)S(1)}, bf16[4,112,768]{2,1,0:T(8,128)(2,1)S(1)}) custom-call(bf16[1024,768]{1,0:T(8,128)(2,1)S(1)} %get-tuple-element.113.refs_0_.refs_4_.normed_ref, bf16[1024,768]{1,0:T(8,128)(2,1)S(1)} %get-tuple-element.175.gp_ref, bf16[768,768]{1,0:T(8,128)(2,1)S(1)} %get-tuple-element.167.w_ref, ...), custom_call_target="tpu_custom_call" | custom-call | flops 48000000000 | tf_op jit(solution)/shard_map/main_grads/pallas_call | solution.py:765
  91.7 1.8 %collective-permute-start.37 = (bf16[112,768]{1,0:T(8,128)(2,1)S(1)}, bf16[112,768]{1,0:T(8,128)(2,1)S(1)}, u32[]{:S(2)}, u32[]{:S(2)}) collective-permute-start(bf16[112,768]{1,0:T(8,128)(2,1)S(1)} %get-tuple-element.183), channel_id=1, source_target_pairs={{0,2},{1,3},{2,0},{3,1},{4,6},{5,7},{6,4},{7,5},{8,10},{9,11},{10,... | collective-permute-start | bytes 516104 | tf_op jit(solution)/shard_map/ppermute | solution.py:788
  93.4 1.8 %collective-permute-start.38 = (bf16[112,768]{1,0:T(8,128)(2,1)S(1)}, bf16[112,768]{1,0:T(8,128)(2,1)S(1)}, u32[]{:S(2)}, u32[]{:S(2)}) collective-permute-start(bf16[112,768]{1,0:T(8,128)(2,1)S(1)} %get-tuple-element.184), channel_id=1, source_target_pairs={{0,4},{1,5},{2,6},{3,7},{4,0},{5,1},{6,2},{7,3},{8,12},{9,13},{10,... | collective-permute-start | bytes 516104 | tf_op jit(solution)/shard_map/ppermute | solution.py:788
  96.4 3.8 %collective-permute-done.37.refs_1_ = bf16[112,768]{1,0:T(8,128)(2,1)S(1)} collective-permute-done((bf16[112,768]{1,0:T(8,128)(2,1)S(1)}, bf16[112,768]{1,0:T(8,128)(2,1)S(1)}, u32[]{:S(2)}, u32[]{:S(2)}) %collective-permute-start.37) | collective-permute-done | bytes 172064 | tf_op jit(solution)/shard_map/ppermute | solution.py:788
  100.2 1.7 %collective-permute-start.34 = (bf16[256,768]{1,0:T(8,128)(2,1)S(1)}, bf16[256,768]{1,0:T(8,128)(2,1)S(1)}, u32[]{:S(2)}, u32[]{:S(2)}) collective-permute-start(bf16[256,768]{1,0:T(8,128)(2,1)S(1)} %get-tuple-element.172), channel_id=1, source_target_pairs={{0,24},{8,16},{16,8},{24,0},{1,25},{9,17},{17,9},{25,1},{2,26},{10... | collective-permute-start | bytes 1179656 | tf_op jit(solution)/shard_map/ppermute | solution.py:788
  102.0 5.4 %collective-permute-done.38.refs_2_ = bf16[112,768]{1,0:T(8,128)(2,1)S(1)} collective-permute-done((bf16[112,768]{1,0:T(8,128)(2,1)S(1)}, bf16[112,768]{1,0:T(8,128)(2,1)S(1)}, u32[]{:S(2)}, u32[]{:S(2)}) %collective-permute-start.38) | collective-permute-done | bytes 172064 | tf_op jit(solution)/shard_map/ppermute | solution.py:788
  107.4 3.6 %collective-permute-done.39.refs_3_ = bf16[112,768]{1,0:T(8,128)(2,1)S(1)} collective-permute-done((bf16[112,768]{1,0:T(8,128)(2,1)S(1)}, bf16[112,768]{1,0:T(8,128)(2,1)S(1)}, u32[]{:S(2)}, u32[]{:S(2)}) %collective-permute-start.39) | collective-permute-done | bytes 172064 | tf_op jit(solution)/shard_map/ppermute | solution.py:788
  (116 shorter events, 44.5 us)
Async XLA Ops:
  10.0 15.2 %collective-permute-start.5 = (bf16[256,768]{1,0:T(8,128)(2,1)S(1)}, bf16[256,768]{1,0:T(8,128)(2,1)S(1)}, u32[]{:S(2)}, u32[]{:S(2)}) collective-permute-start(bf16[256,768]{1,0:T(8,128)(2,1)S(1)} %bitcast.10), channel_id=1, source_target_pairs={{0,24},{8,16},{16,8},{24,0},{1,25},{9,17},{17,9},{25,1},{2,26},{10... | collective-permute-start | bytes 1179656 | tf_op jit(solution)/shard_map/ppermute | solution.py:788
  11.1 17.2 %collective-permute-start.3 = (bf16[256,768]{1,0:T(8,128)(2,1)S(1)}, bf16[256,768]{1,0:T(8,128)(2,1)S(1)}, u32[]{:S(2)}, u32[]{:S(2)}) collective-permute-start(bf16[256,768]{1,0:T(8,128)(2,1)S(1)} %bitcast.11), channel_id=1, source_target_pairs={{0,16},{8,24},{16,0},{24,8},{1,17},{9,25},{17,1},{25,9},{2,18},{10... | collective-permute-start | bytes 1179656 | tf_op jit(solution)/shard_map/ppermute | solution.py:788
  12.7 10.8 %collective-permute-start.8 = (bf16[96,768]{1,0:T(8,128)(2,1)S(1)}, bf16[96,768]{1,0:T(8,128)(2,1)S(1)}, u32[]{:S(2)}, u32[]{:S(2)}) collective-permute-start(bf16[96,768]{1,0:T(8,128)(2,1)S(1)} %get-tuple-element.112.refs_8_), channel_id=1, source_target_pairs={{0,6},{1,7},{2,4},{3,5},{4,2},{5,3},{6,0},{7,1},{8,14},{9,15},{10,... | collective-permute-start | bytes 442376 | tf_op jit(solution)/shard_map/ppermute | solution.py:788
  14.3 10.4 %collective-permute-start.7 = (bf16[96,768]{1,0:T(8,128)(2,1)S(1)}, bf16[96,768]{1,0:T(8,128)(2,1)S(1)}, u32[]{:S(2)}, u32[]{:S(2)}) collective-permute-start(bf16[96,768]{1,0:T(8,128)(2,1)S(1)} %get-tuple-element.112.refs_8_), channel_id=1, source_target_pairs={{0,4},{1,5},{2,6},{3,7},{4,0},{5,1},{6,2},{7,3},{8,12},{9,13},{10,... | collective-permute-start | bytes 442376 | tf_op jit(solution)/shard_map/ppermute | solution.py:788
  15.6 9.2 %collective-permute-start.6 = (bf16[96,768]{1,0:T(8,128)(2,1)S(1)}, bf16[96,768]{1,0:T(8,128)(2,1)S(1)}, u32[]{:S(2)}, u32[]{:S(2)}) collective-permute-start(bf16[96,768]{1,0:T(8,128)(2,1)S(1)} %get-tuple-element.112.refs_8_), channel_id=1, source_target_pairs={{0,2},{1,3},{2,0},{3,1},{4,6},{5,7},{6,4},{7,5},{8,10},{9,11},{10,... | collective-permute-start | bytes 442376 | tf_op jit(solution)/shard_map/ppermute | solution.py:788
  24.8 8.7 %collective-permute-start.9 = (bf16[96,768]{1,0:T(8,128)(2,1)S(1)}, bf16[96,768]{1,0:T(8,128)(2,1)S(1)}, u32[]{:S(2)}, u32[]{:S(2)}) collective-permute-start(bf16[96,768]{1,0:T(8,128)(2,1)S(1)} %get-tuple-element.112.refs_8_), channel_id=1, source_target_pairs={{0,1},{1,0},{2,3},{3,2},{4,5},{5,4},{6,7},{7,6},{8,9},{9,8},{10,11... | collective-permute-start | bytes 442376 | tf_op jit(solution)/shard_map/ppermute | solution.py:788
  24.8 8.7 %collective-permute-start.12 = (bf16[96,768]{1,0:T(8,128)(2,1)S(1)}, bf16[96,768]{1,0:T(8,128)(2,1)S(1)}, u32[]{:S(2)}, u32[]{:S(2)}) collective-permute-start(bf16[96,768]{1,0:T(8,128)(2,1)S(1)} %collective-permute-done.8.refs_11_), channel_id=1, source_target_pairs={{0,1},{1,0},{2,3},{3,2},{4,5},{5,4},{6,7},{7,6},{8,9},{9,8},{10,11... | collective-permute-start | bytes 442376 | tf_op jit(solution)/shard_map/ppermute | solution.py:788
  25.3 9.6 %collective-permute-start.11 = (bf16[96,768]{1,0:T(8,128)(2,1)S(1)}, bf16[96,768]{1,0:T(8,128)(2,1)S(1)}, u32[]{:S(2)}, u32[]{:S(2)}) collective-permute-start(bf16[96,768]{1,0:T(8,128)(2,1)S(1)} %collective-permute-done.7.refs_10_), channel_id=1, source_target_pairs={{0,1},{1,0},{2,3},{3,2},{4,5},{5,4},{6,7},{7,6},{8,9},{9,8},{10,11... | collective-permute-start | bytes 442376 | tf_op jit(solution)/shard_map/ppermute | solution.py:788
  31.3 10.8 %collective-permute-start.15 = (bf16[96,768]{1,0:T(8,128)(2,1)S(1)}, bf16[96,768]{1,0:T(8,128)(2,1)S(1)}, u32[]{:S(2)}, u32[]{:S(2)}) collective-permute-start(bf16[96,768]{1,0:T(8,128)(2,1)S(1)} %get-tuple-element.124.refs_2_), channel_id=1, source_target_pairs={{0,6},{1,7},{2,4},{3,5},{4,2},{5,3},{6,0},{7,1},{8,14},{9,15},{10,... | collective-permute-start | bytes 442376 | tf_op jit(solution)/shard_map/ppermute | solution.py:788
  33.4 10.2 %collective-permute-start.14 = (bf16[96,768]{1,0:T(8,128)(2,1)S(1)}, bf16[96,768]{1,0:T(8,128)(2,1)S(1)}, u32[]{:S(2)}, u32[]{:S(2)}) collective-permute-start(bf16[96,768]{1,0:T(8,128)(2,1)S(1)} %get-tuple-element.124.refs_2_), channel_id=1, source_target_pairs={{0,4},{1,5},{2,6},{3,7},{4,0},{5,1},{6,2},{7,3},{8,12},{9,13},{10,... | collective-permute-start | bytes 442376 | tf_op jit(solution)/shard_map/ppermute | solution.py:788
  33.5 10.2 %collective-permute-start.13 = (bf16[96,768]{1,0:T(8,128)(2,1)S(1)}, bf16[96,768]{1,0:T(8,128)(2,1)S(1)}, u32[]{:S(2)}, u32[]{:S(2)}) collective-permute-start(bf16[96,768]{1,0:T(8,128)(2,1)S(1)} %get-tuple-element.124.refs_2_), channel_id=1, source_target_pairs={{0,2},{1,3},{2,0},{3,1},{4,6},{5,7},{6,4},{7,5},{8,10},{9,11},{10,... | collective-permute-start | bytes 442376 | tf_op jit(solution)/shard_map/ppermute | solution.py:788
  34.9 9.6 %collective-permute-start.17 = (bf16[256,768]{1,0:T(8,128)(2,1)S(1)}, bf16[256,768]{1,0:T(8,128)(2,1)S(1)}, u32[]{:S(2)}, u32[]{:S(2)}) collective-permute-start(bf16[256,768]{1,0:T(8,128)(2,1)S(1)} %bitcast.16), channel_id=1, source_target_pairs={{0,16},{8,24},{16,0},{24,8},{1,17},{9,25},{17,1},{25,9},{2,18},{10... | collective-permute-start | bytes 1179656 | tf_op jit(solution)/shard_map/ppermute | solution.py:788
  35.5 10.4 %collective-permute-start.16 = (bf16[256,768]{1,0:T(8,128)(2,1)S(1)}, bf16[256,768]{1,0:T(8,128)(2,1)S(1)}, u32[]{:S(2)}, u32[]{:S(2)}) collective-permute-start(bf16[256,768]{1,0:T(8,128)(2,1)S(1)} %bitcast.17), channel_id=1, source_target_pairs={{0,8},{8,0},{16,24},{24,16},{1,9},{9,1},{17,25},{25,17},{2,10},{10... | collective-permute-start | bytes 1179656 | tf_op jit(solution)/shard_map/ppermute | solution.py:788
  42.1 11.1 %collective-permute-start.22 = (bf16[256,768]{1,0:T(8,128)(2,1)S(1)}, bf16[256,768]{1,0:T(8,128)(2,1)S(1)}, u32[]{:S(2)}, u32[]{:S(2)}) collective-permute-start(bf16[256,768]{1,0:T(8,128)(2,1)S(1)} %bitcast.18), channel_id=1, source_target_pairs={{0,24},{8,16},{16,8},{24,0},{1,25},{9,17},{17,9},{25,1},{2,26},{10... | collective-permute-start | bytes 1179656 | tf_op jit(solution)/shard_map/ppermute | solution.py:788
  65.4 21.5 %collective-permute-start.26 = (bf16[256,768]{1,0:T(8,128)(2,1)S(1)}, bf16[256,768]{1,0:T(8,128)(2,1)S(1)}, u32[]{:S(2)}, u32[]{:S(2)}) collective-permute-start(bf16[256,768]{1,0:T(8,128)(2,1)S(1)} %get-tuple-element.139), channel_id=1, source_target_pairs={{0,8},{8,0},{16,24},{24,16},{1,9},{9,1},{17,25},{25,17},{2,10},{10... | collective-permute-start | bytes 1179656 | tf_op jit(solution)/shard_map/ppermute | solution.py:788
  66.7 20.3 %collective-permute-start.27 = (bf16[256,768]{1,0:T(8,128)(2,1)S(1)}, bf16[256,768]{1,0:T(8,128)(2,1)S(1)}, u32[]{:S(2)}, u32[]{:S(2)}) collective-permute-start(bf16[256,768]{1,0:T(8,128)(2,1)S(1)} %get-tuple-element.140), channel_id=1, source_target_pairs={{0,16},{8,24},{16,0},{24,8},{1,17},{9,25},{17,1},{25,9},{2,18},{10... | collective-permute-start | bytes 1179656 | tf_op jit(solution)/shard_map/ppermute | solution.py:788
  67.3 19.7 %collective-permute-start.28 = (bf16[256,768]{1,0:T(8,128)(2,1)S(1)}, bf16[256,768]{1,0:T(8,128)(2,1)S(1)}, u32[]{:S(2)}, u32[]{:S(2)}) collective-permute-start(bf16[256,768]{1,0:T(8,128)(2,1)S(1)} %get-tuple-element.141), channel_id=1, source_target_pairs={{0,24},{8,16},{16,8},{24,0},{1,25},{9,17},{17,9},{25,1},{2,26},{10... | collective-permute-start | bytes 1179656 | tf_op jit(solution)/shard_map/ppermute | solution.py:788
  69.8 9.1 %collective-permute-start.31 = (bf16[96,768]{1,0:T(8,128)(2,1)S(1)}, bf16[96,768]{1,0:T(8,128)(2,1)S(1)}, u32[]{:S(2)}, u32[]{:S(2)}) collective-permute-start(bf16[96,768]{1,0:T(8,128)(2,1)S(1)} %get-tuple-element.147), channel_id=1, source_target_pairs={{0,4},{1,5},{2,6},{3,7},{4,0},{5,1},{6,2},{7,3},{8,12},{9,13},{10,... | collective-permute-start | bytes 442376 | tf_op jit(solution)/shard_map/ppermute | solution.py:788
  77.2 9.7 %collective-permute-start.35 = (bf16[96,768]{1,0:T(8,128)(2,1)S(1)}, bf16[96,768]{1,0:T(8,128)(2,1)S(1)}, u32[]{:S(2)}, u32[]{:S(2)}) collective-permute-start(bf16[96,768]{1,0:T(8,128)(2,1)S(1)} %get-tuple-element.173), channel_id=1, source_target_pairs={{0,6},{1,7},{2,4},{3,5},{4,2},{5,3},{6,0},{7,1},{8,14},{9,15},{10,... | collective-permute-start | bytes 442376 | tf_op jit(solution)/shard_map/ppermute | solution.py:788
  89.8 23.7 %collective-permute-start.32 = (bf16[256,768]{1,0:T(8,128)(2,1)S(1)}, bf16[256,768]{1,0:T(8,128)(2,1)S(1)}, u32[]{:S(2)}, u32[]{:S(2)}) collective-permute-start(bf16[256,768]{1,0:T(8,128)(2,1)S(1)} %get-tuple-element.170), channel_id=1, source_target_pairs={{0,8},{8,0},{16,24},{24,16},{1,9},{9,1},{17,25},{25,17},{2,10},{10... | collective-permute-start | bytes 1179656 | tf_op jit(solution)/shard_map/ppermute | solution.py:788
  90.9 23.7 %collective-permute-start.33 = (bf16[256,768]{1,0:T(8,128)(2,1)S(1)}, bf16[256,768]{1,0:T(8,128)(2,1)S(1)}, u32[]{:S(2)}, u32[]{:S(2)}) collective-permute-start(bf16[256,768]{1,0:T(8,128)(2,1)S(1)} %get-tuple-element.171), channel_id=1, source_target_pairs={{0,16},{8,24},{16,0},{24,8},{1,17},{9,25},{17,1},{25,9},{2,18},{10... | collective-permute-start | bytes 1179656 | tf_op jit(solution)/shard_map/ppermute | solution.py:788
  93.4 13.9 %collective-permute-start.38 = (bf16[112,768]{1,0:T(8,128)(2,1)S(1)}, bf16[112,768]{1,0:T(8,128)(2,1)S(1)}, u32[]{:S(2)}, u32[]{:S(2)}) collective-permute-start(bf16[112,768]{1,0:T(8,128)(2,1)S(1)} %get-tuple-element.184), channel_id=1, source_target_pairs={{0,4},{1,5},{2,6},{3,7},{4,0},{5,1},{6,2},{7,3},{8,12},{9,13},{10,... | collective-permute-start | bytes 516104 | tf_op jit(solution)/shard_map/ppermute | solution.py:788
  95.2 15.8 %collective-permute-start.39 = (bf16[112,768]{1,0:T(8,128)(2,1)S(1)}, bf16[112,768]{1,0:T(8,128)(2,1)S(1)}, u32[]{:S(2)}, u32[]{:S(2)}) collective-permute-start(bf16[112,768]{1,0:T(8,128)(2,1)S(1)} %get-tuple-element.185), channel_id=1, source_target_pairs={{0,6},{1,7},{2,4},{3,5},{4,2},{5,3},{6,0},{7,1},{8,14},{9,15},{10,... | collective-permute-start | bytes 516104 | tf_op jit(solution)/shard_map/ppermute | solution.py:788
  100.2 14.4 %collective-permute-start.34 = (bf16[256,768]{1,0:T(8,128)(2,1)S(1)}, bf16[256,768]{1,0:T(8,128)(2,1)S(1)}, u32[]{:S(2)}, u32[]{:S(2)}) collective-permute-start(bf16[256,768]{1,0:T(8,128)(2,1)S(1)} %get-tuple-element.172), channel_id=1, source_target_pairs={{0,24},{8,16},{16,8},{24,0},{1,25},{9,17},{17,9},{25,1},{2,26},{10... | collective-permute-start | bytes 1179656 | tf_op jit(solution)/shard_map/ppermute | solution.py:788
  (35 other events, 249.2 us)

commit v6 on v5

--- a/solution.py
+++ b/solution.py
@@ -347,9 +347,7 @@
     cots = refs[2 + 2 * plan.line : 2 + 2 * plan.line + n]
     gain_ref = refs[2 + 2 * plan.line + n]
     outs = refs[3 + 2 * plan.line + n :]
-    wz_ref, z_ref, du_ref, stats_ref = outs[:4]
-    parts = outs[4 : 4 + n]
-    wf_ref, wo_ref = outs[4 + n :]
+    wz_ref, z_ref, du_ref, stats_ref, scaled_ref, wo_ref, wf_ref = outs
     ids = place()
     s, z, c = ids
     half = plan.in_rows * n // 2
@@ -381,7 +379,7 @@
         z_ref[pl.ds(start, plan.rows), :] = gate
         gated = y_ref[pl.ds(start, plan.rows), :] * gate * sigmoid(gate)
         scaled = gated * gain
-        parts[m][...] = mm(scaled, wo_ref[...]).astype(parts[m].dtype)
+        scaled_ref[pl.ds(start, plan.rows), :] = scaled.astype(bf16)
         du = mm_nt(cots[m][...], wo_ref[...])
         du_ref[pl.ds(start, plan.rows), :] = du
         norm = jnp.sum(gated * gated, axis=1, keepdims=True)
@@ -392,6 +390,13 @@
             square = square + jnp.where(lane == b, norm[rows], 0.0)
             square = square + jnp.where(lane == b + plan.blocks, dots[rows], 0.0)
     stats_ref[...] = square.T[: 2 * plan.blocks]
+
+
+def out_kernel(plan, scaled_ref, wo_ref, *parts):
+    s = lax.axis_index("seq")
+    for m in range(plan.seq):
+        rows = pl.ds(aligned((s ^ m) * plan.rows, plan.rows), plan.rows)
+        parts[m][...] = mm(scaled_ref[rows, :], wo_ref[...]).astype(bf16)
 
 
 def emit_rows(plan, ids, source_ref, put):
@@ -874,15 +879,19 @@
     early_state = after(early_state, *gate_line, *cots[1:3])
     y, _, *late = scan_part(half, plan.blocks, early_y, early_state)
     piece_shape = (rows, WIDTH)
-    w_gate, z, du, stats, *outs = call(
+    w_gate, z, du, stats, scaled, w_out = call(
         gate_kernel, plan,
         [
             ((WIDTH, chan), bf16), ((total, chan), f32), ((total, chan), f32),
-            ((2 * plan.blocks, GROUP), f32),
-        ] + [(piece_shape, bf16)] * n,
-        [((WIDTH, chan), f32), ((chan, WIDTH), bf16)],
+            ((2 * plan.blocks, GROUP), f32), ((total, chan), bf16), ((chan, WIDTH), bf16),
+        ],
+        [((WIDTH, chan), f32)],
         normed, y, *gate_parts, *cots, own_gain,
         mib=16, micros=6, name="gate_forward",
+    )
+    outs = call(
+        out_kernel, plan, [(piece_shape, bf16)] * n, [], scaled, w_out, mib=8, micros=2,
+        name="out_partial",
     )
     all_stats = [stats] + [swap(stats, "seq", m) for m in range(1, n)]
     dy, dz, scale, gain_out_grad, share, keep, send = call(
@@ -894,7 +903,7 @@
             ((line, n * r // 2 + plan.out_rows, WIDTH), bf16),
         ],
         [((total, chan), bf16), ((WIDTH, chan), f32), ((chan, WIDTH), f32)],
-        *all_stats, normed, y, z, du, w_gate, *cots, own_gain,
+        *all_stats, after(normed, *outs), y, z, du, w_gate, *cots, own_gain,
         mib=16, micros=6, name="gate_backward",
     )
 

time: 120 us -> 119 us (level)
    ppermute x43, waiting for transfers between devices: 42.8 us -> 41.6 us  [swap(): return lax.ppermute(value, axis, [(i, i ^ by) for i in range(size)])]
    pallas_call x19 -> x20, Pallas kernels: 34.4 us -> 34.5 us  [call(): pl.pallas_call(functools.partial(body, plan), out_shape=shapes, in_specs=...]
  transfers between devices with their start and end apart: 43 -> 43, of which waited for: 20 -> 19; matrix products, arithmetic and copies ran while one was open for 0% -> 0% of each run, Pallas kernels for 21% -> 22%
where the time goes in v6:
time: 119 us
  waiting for transfers between devices  41.6 us (35%)
  starting transfers between devices  40 us (34%)
  Pallas kernels  34.5 us (29%)
  local copies, waits for them, and re-layouts  1.73 us (1%)
    ppermute x43, waiting for transfers between devices, swap(): return lax.ppermute(value, axis, [(i, i ^ by) for i in range(size)])  41.6 us
    ppermute x43, starting transfers between devices, swap(): return lax.ppermute(value, axis, [(i, i ^ by) for i in range(size)])  40 us
    pallas_call x20, Pallas kernels, call(): pl.pallas_call(functools.partial(body, plan), out_shape=shapes, in_specs=...  34.5 us
  transfers between devices with their start and end apart: 43, of which 19 were waited for; matrix products, arithmetic and copies ran while one was open for 0% of the time, Pallas kernels for 22%

profile of v6, /device:TPU:8, one launch (start us, length us, event | category | flops | bytes accessed | tf_op | source)
XLA Modules:
  0.0 118.8 jit_solution(12282966471211342073)
XLA Ops:
  7.0 3.0 %collective-permute-done.4.refs_3_.refs_7_ = bf16[32,1152]{1,0:T(8,128)(2,1)S(1)} collective-permute-done((bf16[32,1152]{1,0:T(8,128)(2,1)S(1)}, bf16[32,1152]{1,0:T(8,128)(2,1)S(1)}, u32[]{:S(2)}, u32[]{:S(2)}) %collective-permute-start.4) | collective-permute-done | bytes 73760 | tf_op jit(solution)/shard_map/ppermute | solution.py:793
  12.7 1.6 %collective-permute-start.8 = (bf16[96,768]{1,0:T(8,128)(2,1)S(1)}, bf16[96,768]{1,0:T(8,128)(2,1)S(1)}, u32[]{:S(2)}, u32[]{:S(2)}) collective-permute-start(bf16[96,768]{1,0:T(8,128)(2,1)S(1)} %get-tuple-element.115.refs_8_), channel_id=1, source_target_pairs={{0,6},{1,7},{2,4},{3,5},{4,2},{5,3},{6,0},{7,1},{8,14},{9,15},{10,... | collective-permute-start | bytes 442376 | tf_op jit(solution)/shard_map/ppermute | solution.py:793
  16.8 6.7 %collective-permute-done.8.refs_11_ = bf16[96,768]{1,0:T(8,128)(2,1)S(1)} collective-permute-done((bf16[96,768]{1,0:T(8,128)(2,1)S(1)}, bf16[96,768]{1,0:T(8,128)(2,1)S(1)}, u32[]{:S(2)}, u32[]{:S(2)}) %collective-permute-start.8) | collective-permute-done | bytes 147488 | tf_op jit(solution)/shard_map/ppermute | solution.py:793
  25.4 2.9 %collective-permute-done.3.refs_2_ = bf16[256,768]{1,0:T(8,128)(2,1)S(1)} collective-permute-done((bf16[256,768]{1,0:T(8,128)(2,1)S(1)}, bf16[256,768]{1,0:T(8,128)(2,1)S(1)}, u32[]{:S(2)}, u32[]{:S(2)}) %collective-permute-start.3) | collective-permute-done | bytes 393248 | tf_op jit(solution)/shard_map/ppermute | solution.py:793
  28.5 2.8 %collective-permute-done.1.refs_1_ = bf16[256,768]{1,0:T(8,128)(2,1)S(1)} collective-permute-done((bf16[256,768]{1,0:T(8,128)(2,1)S(1)}, bf16[256,768]{1,0:T(8,128)(2,1)S(1)}, u32[]{:S(2)}, u32[]{:S(2)}) %collective-permute-start.1) | collective-permute-done | bytes 393248 | tf_op jit(solution)/shard_map/ppermute | solution.py:793
  31.3 2.1 %collective-permute-start.15 = (bf16[96,768]{1,0:T(8,128)(2,1)S(1)}, bf16[96,768]{1,0:T(8,128)(2,1)S(1)}, u32[]{:S(2)}, u32[]{:S(2)}) collective-permute-start(bf16[96,768]{1,0:T(8,128)(2,1)S(1)} %get-tuple-element.127.refs_2_), channel_id=1, source_target_pairs={{0,6},{1,7},{2,4},{3,5},{4,2},{5,3},{6,0},{7,1},{8,14},{9,15},{10,... | collective-permute-start | bytes 442376 | tf_op jit(solution)/shard_map/ppermute | solution.py:793
  36.0 1.7 %project.1 = (bf16[1024,768]{1,0:T(8,128)(2,1)S(1)}, bf16[768,768]{1,0:T(8,128)(2,1)S(1)}, f32[1032,640]{1,0:T(8,128)S(1)}, f32[1024,128]{1,0:T(8,128)S(1)}, f32...) custom-call(bf16[256,768]{1,0:T(8,128)(2,1)S(1)} %bitcast.13, bf16[256,768]{1,0:T(8,128)(2,1)S(1)} %collective-permute-done.1.refs_1_, ...), custom_call_target="tpu_custom_call" | custom-call | flops 15000000512 | tf_op jit(solution)/shard_map/project/pallas_call | solution.py:770
  37.8 3.1 %scan_forward.2 = (f32[512,384]{1,0:T(8,128)S(1)}, f32[128,384]{1,0:T(8,128)S(1)}, f32[4,128,384]{2,1,0:T(8,128)S(1)}, f32[512,640]{1,0:T(8,128)S(1)}, f32[512,6...) custom-call(f32[1032,640]{1,0:T(8,128)S(1)} %get-tuple-element.117.refs_0_, ...), custom_call_target="tpu_custom_call" | custom-call | flops 12000000000 | tf_op jit(solution)/shard_map/scan_forward/pallas_call | solution.py:770
  45.9 3.8 %scan_forward.3 = (f32[1024,384]{1,0:T(8,128)S(1)}, f32[128,384]{1,0:T(8,128)}, f32[4,128,384]{2,1,0:T(8,128)S(1)}, f32[512,640]{1,0:T(8,128)S(1)}, f32[512,640]...) custom-call(f32[1032,640]{1,0:T(8,128)S(1)} %get-tuple-element.117.refs_0_, ...), custom_call_target="tpu_custom_call" | custom-call | flops 12000000000 | tf_op jit(solution)/shard_map/scan_forward/pallas_call | solution.py:770
  49.7 3.5 %collective-permute-done.22.refs_13_.refs_12_ = bf16[256,768]{1,0:T(8,128)(2,1)S(1)} collective-permute-done((bf16[256,768]{1,0:T(8,128)(2,1)S(1)}, bf16[256,768]{1,0:T(8,128)(2,1)S(1)}, u32[]{:S(2)}, u32[]{:S(2)}) %collective-permute-start.22) | collective-permute-done | bytes 393248 | tf_op jit(solution)/shard_map/ppermute | solution.py:793
  53.2 2.1 %gate_forward.1 = (bf16[768,384]{1,0:T(8,128)(2,1)S(1)}, f32[1024,384]{1,0:T(8,128)S(1)}, f32[1024,384]{1,0:T(8,128)S(1)}, f32[16,128]{1,0:T(8,128)S(1)}, bf16[1...) custom-call(bf16[1024,768]{1,0:T(8,128)(2,1)S(1)} %get-tuple-element.143.refs_0_.refs_4_.normed_ref, ...), custom_call_target="tpu_custom_call" | custom-call | flops 17999998976 | tf_op jit(solution)/shard_map/gate_forward/pallas_call | solution.py:770
  61.4 2.9 %gate_backward.1 = (f32[1024,384]{1,0:T(8,128)S(1)}, bf16[1024,384]{1,0:T(8,128)(2,1)S(1)}, f32[1024,128]{1,0:T(8,128)S(1)}, f32[1,384]{1,0:T(1,128)S(1)}, f32[8...) custom-call(f32[16,128]{1,0:T(8,128)S(1)} %get-tuple-element.136.refs_0_, ...), custom_call_target="tpu_custom_call" | custom-call | flops 17999998976 | tf_op jit(solution)/shard_map/gate_backward/pallas_call | solution.py:770
  66.1 1.7 %collective-permute-start.28 = (bf16[256,768]{1,0:T(8,128)(2,1)S(1)}, bf16[256,768]{1,0:T(8,128)(2,1)S(1)}, u32[]{:S(2)}, u32[]{:S(2)}) collective-permute-start(bf16[256,768]{1,0:T(8,128)(2,1)S(1)} %get-tuple-element.142), channel_id=1, source_target_pairs={{0,24},{8,16},{16,8},{24,0},{1,25},{9,17},{17,9},{25,1},{2,26},{10... | collective-permute-start | bytes 1179656 | tf_op jit(solution)/shard_map/ppermute | solution.py:793
  68.7 2.4 %collective-permute-start.31 = (bf16[96,768]{1,0:T(8,128)(2,1)S(1)}, bf16[96,768]{1,0:T(8,128)(2,1)S(1)}, u32[]{:S(2)}, u32[]{:S(2)}) collective-permute-start(bf16[96,768]{1,0:T(8,128)(2,1)S(1)} %get-tuple-element.153), channel_id=1, source_target_pairs={{0,4},{1,5},{2,6},{3,7},{4,0},{5,1},{6,2},{7,3},{8,12},{9,13},{10,... | collective-permute-start | bytes 442376 | tf_op jit(solution)/shard_map/ppermute | solution.py:793
  71.0 5.1 %scan_backward.2 = (bf16[512,768]{1,0:T(8,128)(2,1)S(1)}, f32[128,384]{1,0:T(8,128)S(1)}, f32[8,640]{1,0:T(8,128)S(1)}, f32[8,640]{1,0:T(8,128)S(1)}, f32[8,128]{1,0:T(8,128)S(1)}) custom-call(f32[1032,640]{1,0:T(8,128)S(1)} %get-tuple-element.117.refs_0_, f32[1024,128]{1,0:T(8,128)S(1)} %get-tuple-element.118.refs_1_, ...), custom_call_target="tpu_custom_call" | custom-call | flops 20999999488 | tf_op jit(solution)/shard_map/scan_backward/pallas_call | solution.py:770
  77.7 5.9 %scan_backward.3 = (bf16[1024,768]{1,0:T(8,128)(2,1)S(1)}, f32[128,384]{1,0:T(8,128)}, f32[8,640]{1,0:T(8,128)}, f32[8,640]{1,0:T(8,128)S(1)}, f32[8,128]{1,0:T(8,128)S(1)}) custom-call(f32[1032,640]{1,0:T(8,128)S(1)} %get-tuple-element.117.refs_0_, f32[1024,128]{1,0:T(8,128)S(1)} %get-tuple-element.118.refs_1_, f32[1040,128]{1,0:T(8,128)S(1)} %get-tuple-element.119.refs_2_, ...), custom_call_target="tpu_custom_call" | custom-call | flops 20999999488 | tf_op jit(solution)/shard_map/scan_backward/pallas_call | solution.py:770
  83.6 2.2 %normed_grads.1 = (bf16[256,768]{1,0:T(8,128)(2,1)S(1)}, bf16[256,768]{1,0:T(8,128)(2,1)S(1)}, bf16[256,768]{1,0:T(8,128)(2,1)S(1)}, bf16[256,768]{1,0:T(8,128)(2,1)S(1)}) custom-call(bf16[1024,768]{1,0:T(8,128)(2,1)S(1)} %get-tuple-element.181.gp_ref, bf16[768,768]{1,0:T(8,128)(2,1)S(1)} %get-tuple-element.173.w_ref, ...), custom_call_target="tpu_custom_call" | custom-call | flops 35999997952 | tf_op jit(solution)/shard_map/normed_grads/pallas_call | solution.py:770
  85.9 1.7 %main_grads.1 = (bf16[4,112,768]{2,1,0:T(8,128)(2,1)S(1)}, bf16[4,112,768]{2,1,0:T(8,128)(2,1)S(1)}) custom-call(bf16[1024,768]{1,0:T(8,128)(2,1)S(1)} %get-tuple-element.143.refs_0_.refs_4_.normed_ref, bf16[1024,768]{1,0:T(8,128)(2,1)S(1)} %get-tuple-element.181.gp_ref, bf16[768,768]{1,0:T(8,128)(2,1)S(1)} %get-tuple-element.173.w_ref, ...), custom_call_target="tpu_custom_call" | custom-call | flops 48000000000 | tf_op jit(solution)/shard_map/main_grads/pallas_call | solution.py:770
  90.6 1.8 %collective-permute-start.37 = (bf16[112,768]{1,0:T(8,128)(2,1)S(1)}, bf16[112,768]{1,0:T(8,128)(2,1)S(1)}, u32[]{:S(2)}, u32[]{:S(2)}) collective-permute-start(bf16[112,768]{1,0:T(8,128)(2,1)S(1)} %get-tuple-element.189), channel_id=1, source_target_pairs={{0,2},{1,3},{2,0},{3,1},{4,6},{5,7},{6,4},{7,5},{8,10},{9,11},{10,... | collective-permute-start | bytes 516104 | tf_op jit(solution)/shard_map/ppermute | solution.py:793
  92.3 1.8 %collective-permute-start.38 = (bf16[112,768]{1,0:T(8,128)(2,1)S(1)}, bf16[112,768]{1,0:T(8,128)(2,1)S(1)}, u32[]{:S(2)}, u32[]{:S(2)}) collective-permute-start(bf16[112,768]{1,0:T(8,128)(2,1)S(1)} %get-tuple-element.190), channel_id=1, source_target_pairs={{0,4},{1,5},{2,6},{3,7},{4,0},{5,1},{6,2},{7,3},{8,12},{9,13},{10,... | collective-permute-start | bytes 516104 | tf_op jit(solution)/shard_map/ppermute | solution.py:793
  95.3 3.8 %collective-permute-done.37.refs_1_ = bf16[112,768]{1,0:T(8,128)(2,1)S(1)} collective-permute-done((bf16[112,768]{1,0:T(8,128)(2,1)S(1)}, bf16[112,768]{1,0:T(8,128)(2,1)S(1)}, u32[]{:S(2)}, u32[]{:S(2)}) %collective-permute-start.37) | collective-permute-done | bytes 172064 | tf_op jit(solution)/shard_map/ppermute | solution.py:793
  99.1 1.7 %collective-permute-start.34 = (bf16[256,768]{1,0:T(8,128)(2,1)S(1)}, bf16[256,768]{1,0:T(8,128)(2,1)S(1)}, u32[]{:S(2)}, u32[]{:S(2)}) collective-permute-start(bf16[256,768]{1,0:T(8,128)(2,1)S(1)} %get-tuple-element.178), channel_id=1, source_target_pairs={{0,24},{8,16},{16,8},{24,0},{1,25},{9,17},{17,9},{25,1},{2,26},{10... | collective-permute-start | bytes 1179656 | tf_op jit(solution)/shard_map/ppermute | solution.py:793
  100.9 5.4 %collective-permute-done.38.refs_2_ = bf16[112,768]{1,0:T(8,128)(2,1)S(1)} collective-permute-done((bf16[112,768]{1,0:T(8,128)(2,1)S(1)}, bf16[112,768]{1,0:T(8,128)(2,1)S(1)}, u32[]{:S(2)}, u32[]{:S(2)}) %collective-permute-start.38) | collective-permute-done | bytes 172064 | tf_op jit(solution)/shard_map/ppermute | solution.py:793
  106.3 3.6 %collective-permute-done.39.refs_3_ = bf16[112,768]{1,0:T(8,128)(2,1)S(1)} collective-permute-done((bf16[112,768]{1,0:T(8,128)(2,1)S(1)}, bf16[112,768]{1,0:T(8,128)(2,1)S(1)}, u32[]{:S(2)}, u32[]{:S(2)}) %collective-permute-start.39) | collective-permute-done | bytes 172064 | tf_op jit(solution)/shard_map/ppermute | solution.py:793
  (117 shorter events, 44.5 us)
Async XLA Ops:
  10.0 15.2 %collective-permute-start.5 = (bf16[256,768]{1,0:T(8,128)(2,1)S(1)}, bf16[256,768]{1,0:T(8,128)(2,1)S(1)}, u32[]{:S(2)}, u32[]{:S(2)}) collective-permute-start(bf16[256,768]{1,0:T(8,128)(2,1)S(1)} %bitcast.10), channel_id=1, source_target_pairs={{0,24},{8,16},{16,8},{24,0},{1,25},{9,17},{17,9},{25,1},{2,26},{10... | collective-permute-start | bytes 1179656 | tf_op jit(solution)/shard_map/ppermute | solution.py:793
  11.1 17.2 %collective-permute-start.3 = (bf16[256,768]{1,0:T(8,128)(2,1)S(1)}, bf16[256,768]{1,0:T(8,128)(2,1)S(1)}, u32[]{:S(2)}, u32[]{:S(2)}) collective-permute-start(bf16[256,768]{1,0:T(8,128)(2,1)S(1)} %bitcast.11), channel_id=1, source_target_pairs={{0,16},{8,24},{16,0},{24,8},{1,17},{9,25},{17,1},{25,9},{2,18},{10... | collective-permute-start | bytes 1179656 | tf_op jit(solution)/shard_map/ppermute | solution.py:793
  12.7 10.8 %collective-permute-start.8 = (bf16[96,768]{1,0:T(8,128)(2,1)S(1)}, bf16[96,768]{1,0:T(8,128)(2,1)S(1)}, u32[]{:S(2)}, u32[]{:S(2)}) collective-permute-start(bf16[96,768]{1,0:T(8,128)(2,1)S(1)} %get-tuple-element.115.refs_8_), channel_id=1, source_target_pairs={{0,6},{1,7},{2,4},{3,5},{4,2},{5,3},{6,0},{7,1},{8,14},{9,15},{10,... | collective-permute-start | bytes 442376 | tf_op jit(solution)/shard_map/ppermute | solution.py:793
  14.3 10.4 %collective-permute-start.7 = (bf16[96,768]{1,0:T(8,128)(2,1)S(1)}, bf16[96,768]{1,0:T(8,128)(2,1)S(1)}, u32[]{:S(2)}, u32[]{:S(2)}) collective-permute-start(bf16[96,768]{1,0:T(8,128)(2,1)S(1)} %get-tuple-element.115.refs_8_), channel_id=1, source_target_pairs={{0,4},{1,5},{2,6},{3,7},{4,0},{5,1},{6,2},{7,3},{8,12},{9,13},{10,... | collective-permute-start | bytes 442376 | tf_op jit(solution)/shard_map/ppermute | solution.py:793
  15.6 9.2 %collective-permute-start.6 = (bf16[96,768]{1,0:T(8,128)(2,1)S(1)}, bf16[96,768]{1,0:T(8,128)(2,1)S(1)}, u32[]{:S(2)}, u32[]{:S(2)}) collective-permute-start(bf16[96,768]{1,0:T(8,128)(2,1)S(1)} %get-tuple-element.115.refs_8_), channel_id=1, source_target_pairs={{0,2},{1,3},{2,0},{3,1},{4,6},{5,7},{6,4},{7,5},{8,10},{9,11},{10,... | collective-permute-start | bytes 442376 | tf_op jit(solution)/shard_map/ppermute | solution.py:793
  24.8 8.7 %collective-permute-start.9 = (bf16[96,768]{1,0:T(8,128)(2,1)S(1)}, bf16[96,768]{1,0:T(8,128)(2,1)S(1)}, u32[]{:S(2)}, u32[]{:S(2)}) collective-permute-start(bf16[96,768]{1,0:T(8,128)(2,1)S(1)} %get-tuple-element.115.refs_8_), channel_id=1, source_target_pairs={{0,1},{1,0},{2,3},{3,2},{4,5},{5,4},{6,7},{7,6},{8,9},{9,8},{10,11... | collective-permute-start | bytes 442376 | tf_op jit(solution)/shard_map/ppermute | solution.py:793
  24.8 8.7 %collective-permute-start.12 = (bf16[96,768]{1,0:T(8,128)(2,1)S(1)}, bf16[96,768]{1,0:T(8,128)(2,1)S(1)}, u32[]{:S(2)}, u32[]{:S(2)}) collective-permute-start(bf16[96,768]{1,0:T(8,128)(2,1)S(1)} %collective-permute-done.8.refs_11_), channel_id=1, source_target_pairs={{0,1},{1,0},{2,3},{3,2},{4,5},{5,4},{6,7},{7,6},{8,9},{9,8},{10,11... | collective-permute-start | bytes 442376 | tf_op jit(solution)/shard_map/ppermute | solution.py:793
  25.3 9.6 %collective-permute-start.11 = (bf16[96,768]{1,0:T(8,128)(2,1)S(1)}, bf16[96,768]{1,0:T(8,128)(2,1)S(1)}, u32[]{:S(2)}, u32[]{:S(2)}) collective-permute-start(bf16[96,768]{1,0:T(8,128)(2,1)S(1)} %collective-permute-done.7.refs_10_), channel_id=1, source_target_pairs={{0,1},{1,0},{2,3},{3,2},{4,5},{5,4},{6,7},{7,6},{8,9},{9,8},{10,11... | collective-permute-start | bytes 442376 | tf_op jit(solution)/shard_map/ppermute | solution.py:793
  31.3 10.8 %collective-permute-start.15 = (bf16[96,768]{1,0:T(8,128)(2,1)S(1)}, bf16[96,768]{1,0:T(8,128)(2,1)S(1)}, u32[]{:S(2)}, u32[]{:S(2)}) collective-permute-start(bf16[96,768]{1,0:T(8,128)(2,1)S(1)} %get-tuple-element.127.refs_2_), channel_id=1, source_target_pairs={{0,6},{1,7},{2,4},{3,5},{4,2},{5,3},{6,0},{7,1},{8,14},{9,15},{10,... | collective-permute-start | bytes 442376 | tf_op jit(solution)/shard_map/ppermute | solution.py:793
  33.4 10.2 %collective-permute-start.14 = (bf16[96,768]{1,0:T(8,128)(2,1)S(1)}, bf16[96,768]{1,0:T(8,128)(2,1)S(1)}, u32[]{:S(2)}, u32[]{:S(2)}) collective-permute-start(bf16[96,768]{1,0:T(8,128)(2,1)S(1)} %get-tuple-element.127.refs_2_), channel_id=1, source_target_pairs={{0,4},{1,5},{2,6},{3,7},{4,0},{5,1},{6,2},{7,3},{8,12},{9,13},{10,... | collective-permute-start | bytes 442376 | tf_op jit(solution)/shard_map/ppermute | solution.py:793
  33.5 10.2 %collective-permute-start.13 = (bf16[96,768]{1,0:T(8,128)(2,1)S(1)}, bf16[96,768]{1,0:T(8,128)(2,1)S(1)}, u32[]{:S(2)}, u32[]{:S(2)}) collective-permute-start(bf16[96,768]{1,0:T(8,128)(2,1)S(1)} %get-tuple-element.127.refs_2_), channel_id=1, source_target_pairs={{0,2},{1,3},{2,0},{3,1},{4,6},{5,7},{6,4},{7,5},{8,10},{9,11},{10,... | collective-permute-start | bytes 442376 | tf_op jit(solution)/shard_map/ppermute | solution.py:793
  34.9 9.6 %collective-permute-start.17 = (bf16[256,768]{1,0:T(8,128)(2,1)S(1)}, bf16[256,768]{1,0:T(8,128)(2,1)S(1)}, u32[]{:S(2)}, u32[]{:S(2)}) collective-permute-start(bf16[256,768]{1,0:T(8,128)(2,1)S(1)} %bitcast.16), channel_id=1, source_target_pairs={{0,16},{8,24},{16,0},{24,8},{1,17},{9,25},{17,1},{25,9},{2,18},{10... | collective-permute-start | bytes 1179656 | tf_op jit(solution)/shard_map/ppermute | solution.py:793
  35.5 10.4 %collective-permute-start.16 = (bf16[256,768]{1,0:T(8,128)(2,1)S(1)}, bf16[256,768]{1,0:T(8,128)(2,1)S(1)}, u32[]{:S(2)}, u32[]{:S(2)}) collective-permute-start(bf16[256,768]{1,0:T(8,128)(2,1)S(1)} %bitcast.17), channel_id=1, source_target_pairs={{0,8},{8,0},{16,24},{24,16},{1,9},{9,1},{17,25},{25,17},{2,10},{10... | collective-permute-start | bytes 1179656 | tf_op jit(solution)/shard_map/ppermute | solution.py:793
  42.1 11.1 %collective-permute-start.22 = (bf16[256,768]{1,0:T(8,128)(2,1)S(1)}, bf16[256,768]{1,0:T(8,128)(2,1)S(1)}, u32[]{:S(2)}, u32[]{:S(2)}) collective-permute-start(bf16[256,768]{1,0:T(8,128)(2,1)S(1)} %bitcast.18), channel_id=1, source_target_pairs={{0,24},{8,16},{16,8},{24,0},{1,25},{9,17},{17,9},{25,1},{2,26},{10... | collective-permute-start | bytes 1179656 | tf_op jit(solution)/shard_map/ppermute | solution.py:793
  64.3 21.5 %collective-permute-start.26 = (bf16[256,768]{1,0:T(8,128)(2,1)S(1)}, bf16[256,768]{1,0:T(8,128)(2,1)S(1)}, u32[]{:S(2)}, u32[]{:S(2)}) collective-permute-start(bf16[256,768]{1,0:T(8,128)(2,1)S(1)} %get-tuple-element.140), channel_id=1, source_target_pairs={{0,8},{8,0},{16,24},{24,16},{1,9},{9,1},{17,25},{25,17},{2,10},{10... | collective-permute-start | bytes 1179656 | tf_op jit(solution)/shard_map/ppermute | solution.py:793
  65.5 20.3 %collective-permute-start.27 = (bf16[256,768]{1,0:T(8,128)(2,1)S(1)}, bf16[256,768]{1,0:T(8,128)(2,1)S(1)}, u32[]{:S(2)}, u32[]{:S(2)}) collective-permute-start(bf16[256,768]{1,0:T(8,128)(2,1)S(1)} %get-tuple-element.141), channel_id=1, source_target_pairs={{0,16},{8,24},{16,0},{24,8},{1,17},{9,25},{17,1},{25,9},{2,18},{10... | collective-permute-start | bytes 1179656 | tf_op jit(solution)/shard_map/ppermute | solution.py:793
  66.1 19.7 %collective-permute-start.28 = (bf16[256,768]{1,0:T(8,128)(2,1)S(1)}, bf16[256,768]{1,0:T(8,128)(2,1)S(1)}, u32[]{:S(2)}, u32[]{:S(2)}) collective-permute-start(bf16[256,768]{1,0:T(8,128)(2,1)S(1)} %get-tuple-element.142), channel_id=1, source_target_pairs={{0,24},{8,16},{16,8},{24,0},{1,25},{9,17},{17,9},{25,1},{2,26},{10... | collective-permute-start | bytes 1179656 | tf_op jit(solution)/shard_map/ppermute | solution.py:793
  68.7 9.1 %collective-permute-start.31 = (bf16[96,768]{1,0:T(8,128)(2,1)S(1)}, bf16[96,768]{1,0:T(8,128)(2,1)S(1)}, u32[]{:S(2)}, u32[]{:S(2)}) collective-permute-start(bf16[96,768]{1,0:T(8,128)(2,1)S(1)} %get-tuple-element.153), channel_id=1, source_target_pairs={{0,4},{1,5},{2,6},{3,7},{4,0},{5,1},{6,2},{7,3},{8,12},{9,13},{10,... | collective-permute-start | bytes 442376 | tf_op jit(solution)/shard_map/ppermute | solution.py:793
  76.1 9.7 %collective-permute-start.35 = (bf16[96,768]{1,0:T(8,128)(2,1)S(1)}, bf16[96,768]{1,0:T(8,128)(2,1)S(1)}, u32[]{:S(2)}, u32[]{:S(2)}) collective-permute-start(bf16[96,768]{1,0:T(8,128)(2,1)S(1)} %get-tuple-element.179), channel_id=1, source_target_pairs={{0,6},{1,7},{2,4},{3,5},{4,2},{5,3},{6,0},{7,1},{8,14},{9,15},{10,... | collective-permute-start | bytes 442376 | tf_op jit(solution)/shard_map/ppermute | solution.py:793
  88.7 23.7 %collective-permute-start.32 = (bf16[256,768]{1,0:T(8,128)(2,1)S(1)}, bf16[256,768]{1,0:T(8,128)(2,1)S(1)}, u32[]{:S(2)}, u32[]{:S(2)}) collective-permute-start(bf16[256,768]{1,0:T(8,128)(2,1)S(1)} %get-tuple-element.176), channel_id=1, source_target_pairs={{0,8},{8,0},{16,24},{24,16},{1,9},{9,1},{17,25},{25,17},{2,10},{10... | collective-permute-start | bytes 1179656 | tf_op jit(solution)/shard_map/ppermute | solution.py:793
  89.8 23.7 %collective-permute-start.33 = (bf16[256,768]{1,0:T(8,128)(2,1)S(1)}, bf16[256,768]{1,0:T(8,128)(2,1)S(1)}, u32[]{:S(2)}, u32[]{:S(2)}) collective-permute-start(bf16[256,768]{1,0:T(8,128)(2,1)S(1)} %get-tuple-element.177), channel_id=1, source_target_pairs={{0,16},{8,24},{16,0},{24,8},{1,17},{9,25},{17,1},{25,9},{2,18},{10... | collective-permute-start | bytes 1179656 | tf_op jit(solution)/shard_map/ppermute | solution.py:793
  92.3 13.9 %collective-permute-start.38 = (bf16[112,768]{1,0:T(8,128)(2,1)S(1)}, bf16[112,768]{1,0:T(8,128)(2,1)S(1)}, u32[]{:S(2)}, u32[]{:S(2)}) collective-permute-start(bf16[112,768]{1,0:T(8,128)(2,1)S(1)} %get-tuple-element.190), channel_id=1, source_target_pairs={{0,4},{1,5},{2,6},{3,7},{4,0},{5,1},{6,2},{7,3},{8,12},{9,13},{10,... | collective-permute-start | bytes 516104 | tf_op jit(solution)/shard_map/ppermute | solution.py:793
  94.1 15.8 %collective-permute-start.39 = (bf16[112,768]{1,0:T(8,128)(2,1)S(1)}, bf16[112,768]{1,0:T(8,128)(2,1)S(1)}, u32[]{:S(2)}, u32[]{:S(2)}) collective-permute-start(bf16[112,768]{1,0:T(8,128)(2,1)S(1)} %get-tuple-element.191), channel_id=1, source_target_pairs={{0,6},{1,7},{2,4},{3,5},{4,2},{5,3},{6,0},{7,1},{8,14},{9,15},{10,... | collective-permute-start | bytes 516104 | tf_op jit(solution)/shard_map/ppermute | solution.py:793
  99.1 14.4 %collective-permute-start.34 = (bf16[256,768]{1,0:T(8,128)(2,1)S(1)}, bf16[256,768]{1,0:T(8,128)(2,1)S(1)}, u32[]{:S(2)}, u32[]{:S(2)}) collective-permute-start(bf16[256,768]{1,0:T(8,128)(2,1)S(1)} %get-tuple-element.178), channel_id=1, source_target_pairs={{0,24},{8,16},{16,8},{24,0},{1,25},{9,17},{17,9},{25,1},{2,26},{10... | collective-permute-start | bytes 1179656 | tf_op jit(solution)/shard_map/ppermute | solution.py:793
  (35 other events, 249.3 us)

commit v7 on v6

--- a/solution.py
+++ b/solution.py
@@ -943,7 +943,7 @@
     before[1] = after(before[1], *gate_lines[:-1])
     gp, _, _, acc, head_acc = scan_back_part(0, half, early, *before)
     (result,) = call(
-        result_kernel, plan, [(piece_shape, bf16)], [], tok, scale, *out_parts, name="result", micros=LATE
+        result_kernel, plan, [(piece_shape, bf16)], [], tok, scale, *out_parts, name="result"
     )
 
     grads = call(

time: 119 us -> 119 us (level)
  no operation moved by 1% of the time
where the time goes in v7:
time: 119 us
  waiting for transfers between devices  41.5 us (35%)
  starting transfers between devices  40 us (34%)
  Pallas kernels  34.6 us (29%)
  local copies, waits for them, and re-layouts  1.73 us (1%)
    ppermute x43, waiting for transfers between devices, swap(): return lax.ppermute(value, axis, [(i, i ^ by) for i in range(size)])  41.5 us
    ppermute x43, starting transfers between devices, swap(): return lax.ppermute(value, axis, [(i, i ^ by) for i in range(size)])  40 us
    pallas_call x20, Pallas kernels, call(): pl.pallas_call(functools.partial(body, plan), out_shape=shapes, in_specs=...  34.6 us
  transfers between devices with their start and end apart: 43, of which 19 were waited for; matrix products, arithmetic and copies ran while one was open for 0% of the time, Pallas kernels for 22%

profile of v7, /device:TPU:8, one launch (start us, length us, event | category | flops | bytes accessed | tf_op | source)
XLA Modules:
  0.0 118.8 jit_solution(651993887864940382)
XLA Ops:
  7.0 3.0 %collective-permute-done.4.refs_3_.refs_7_ = bf16[32,1152]{1,0:T(8,128)(2,1)S(1)} collective-permute-done((bf16[32,1152]{1,0:T(8,128)(2,1)S(1)}, bf16[32,1152]{1,0:T(8,128)(2,1)S(1)}, u32[]{:S(2)}, u32[]{:S(2)}) %collective-permute-start.4) | collective-permute-done | bytes 73760 | tf_op jit(solution)/shard_map/ppermute | solution.py:793
  12.7 1.6 %collective-permute-start.8 = (bf16[96,768]{1,0:T(8,128)(2,1)S(1)}, bf16[96,768]{1,0:T(8,128)(2,1)S(1)}, u32[]{:S(2)}, u32[]{:S(2)}) collective-permute-start(bf16[96,768]{1,0:T(8,128)(2,1)S(1)} %get-tuple-element.115.refs_8_), channel_id=1, source_target_pairs={{0,6},{1,7},{2,4},{3,5},{4,2},{5,3},{6,0},{7,1},{8,14},{9,15},{10,... | collective-permute-start | bytes 442376 | tf_op jit(solution)/shard_map/ppermute | solution.py:793
  16.8 6.7 %collective-permute-done.8.refs_11_ = bf16[96,768]{1,0:T(8,128)(2,1)S(1)} collective-permute-done((bf16[96,768]{1,0:T(8,128)(2,1)S(1)}, bf16[96,768]{1,0:T(8,128)(2,1)S(1)}, u32[]{:S(2)}, u32[]{:S(2)}) %collective-permute-start.8) | collective-permute-done | bytes 147488 | tf_op jit(solution)/shard_map/ppermute | solution.py:793
  25.4 2.9 %collective-permute-done.3.refs_2_ = bf16[256,768]{1,0:T(8,128)(2,1)S(1)} collective-permute-done((bf16[256,768]{1,0:T(8,128)(2,1)S(1)}, bf16[256,768]{1,0:T(8,128)(2,1)S(1)}, u32[]{:S(2)}, u32[]{:S(2)}) %collective-permute-start.3) | collective-permute-done | bytes 393248 | tf_op jit(solution)/shard_map/ppermute | solution.py:793
  28.5 2.8 %collective-permute-done.1.refs_1_ = bf16[256,768]{1,0:T(8,128)(2,1)S(1)} collective-permute-done((bf16[256,768]{1,0:T(8,128)(2,1)S(1)}, bf16[256,768]{1,0:T(8,128)(2,1)S(1)}, u32[]{:S(2)}, u32[]{:S(2)}) %collective-permute-start.1) | collective-permute-done | bytes 393248 | tf_op jit(solution)/shard_map/ppermute | solution.py:793
  31.3 2.1 %collective-permute-start.15 = (bf16[96,768]{1,0:T(8,128)(2,1)S(1)}, bf16[96,768]{1,0:T(8,128)(2,1)S(1)}, u32[]{:S(2)}, u32[]{:S(2)}) collective-permute-start(bf16[96,768]{1,0:T(8,128)(2,1)S(1)} %get-tuple-element.127.refs_2_), channel_id=1, source_target_pairs={{0,6},{1,7},{2,4},{3,5},{4,2},{5,3},{6,0},{7,1},{8,14},{9,15},{10,... | collective-permute-start | bytes 442376 | tf_op jit(solution)/shard_map/ppermute | solution.py:793
  36.0 1.7 %project.1 = (bf16[1024,768]{1,0:T(8,128)(2,1)S(1)}, bf16[768,768]{1,0:T(8,128)(2,1)S(1)}, f32[1032,640]{1,0:T(8,128)S(1)}, f32[1024,128]{1,0:T(8,128)S(1)}, f32...) custom-call(bf16[256,768]{1,0:T(8,128)(2,1)S(1)} %bitcast.13, bf16[256,768]{1,0:T(8,128)(2,1)S(1)} %collective-permute-done.1.refs_1_, ...), custom_call_target="tpu_custom_call" | custom-call | flops 15000000512 | tf_op jit(solution)/shard_map/project/pallas_call | solution.py:770
  37.8 3.1 %scan_forward.2 = (f32[512,384]{1,0:T(8,128)S(1)}, f32[128,384]{1,0:T(8,128)S(1)}, f32[4,128,384]{2,1,0:T(8,128)S(1)}, f32[512,640]{1,0:T(8,128)S(1)}, f32[512,6...) custom-call(f32[1032,640]{1,0:T(8,128)S(1)} %get-tuple-element.117.refs_0_, ...), custom_call_target="tpu_custom_call" | custom-call | flops 12000000000 | tf_op jit(solution)/shard_map/scan_forward/pallas_call | solution.py:770
  45.9 3.8 %scan_forward.3 = (f32[1024,384]{1,0:T(8,128)S(1)}, f32[128,384]{1,0:T(8,128)}, f32[4,128,384]{2,1,0:T(8,128)S(1)}, f32[512,640]{1,0:T(8,128)S(1)}, f32[512,640]...) custom-call(f32[1032,640]{1,0:T(8,128)S(1)} %get-tuple-element.117.refs_0_, ...), custom_call_target="tpu_custom_call" | custom-call | flops 12000000000 | tf_op jit(solution)/shard_map/scan_forward/pallas_call | solution.py:770
  49.7 3.5 %collective-permute-done.22.refs_13_.refs_12_ = bf16[256,768]{1,0:T(8,128)(2,1)S(1)} collective-permute-done((bf16[256,768]{1,0:T(8,128)(2,1)S(1)}, bf16[256,768]{1,0:T(8,128)(2,1)S(1)}, u32[]{:S(2)}, u32[]{:S(2)}) %collective-permute-start.22) | collective-permute-done | bytes 393248 | tf_op jit(solution)/shard_map/ppermute | solution.py:793
  53.2 2.2 %gate_forward.1 = (bf16[768,384]{1,0:T(8,128)(2,1)S(1)}, f32[1024,384]{1,0:T(8,128)S(1)}, f32[1024,384]{1,0:T(8,128)S(1)}, f32[16,128]{1,0:T(8,128)S(1)}, bf16[1...) custom-call(bf16[1024,768]{1,0:T(8,128)(2,1)S(1)} %get-tuple-element.143.refs_0_.refs_4_.normed_ref, ...), custom_call_target="tpu_custom_call" | custom-call | flops 17999998976 | tf_op jit(solution)/shard_map/gate_forward/pallas_call | solution.py:770
  61.4 2.9 %gate_backward.1 = (f32[1024,384]{1,0:T(8,128)S(1)}, bf16[1024,384]{1,0:T(8,128)(2,1)S(1)}, f32[1024,128]{1,0:T(8,128)S(1)}, f32[1,384]{1,0:T(1,128)S(1)}, f32[8...) custom-call(f32[16,128]{1,0:T(8,128)S(1)} %get-tuple-element.136.refs_0_, ...), custom_call_target="tpu_custom_call" | custom-call | flops 17999998976 | tf_op jit(solution)/shard_map/gate_backward/pallas_call | solution.py:770
  66.2 1.7 %collective-permute-start.28 = (bf16[256,768]{1,0:T(8,128)(2,1)S(1)}, bf16[256,768]{1,0:T(8,128)(2,1)S(1)}, u32[]{:S(2)}, u32[]{:S(2)}) collective-permute-start(bf16[256,768]{1,0:T(8,128)(2,1)S(1)} %get-tuple-element.142), channel_id=1, source_target_pairs={{0,24},{8,16},{16,8},{24,0},{1,25},{9,17},{17,9},{25,1},{2,26},{10... | collective-permute-start | bytes 1179656 | tf_op jit(solution)/shard_map/ppermute | solution.py:793
  68.7 2.4 %collective-permute-start.31 = (bf16[96,768]{1,0:T(8,128)(2,1)S(1)}, bf16[96,768]{1,0:T(8,128)(2,1)S(1)}, u32[]{:S(2)}, u32[]{:S(2)}) collective-permute-start(bf16[96,768]{1,0:T(8,128)(2,1)S(1)} %get-tuple-element.153), channel_id=1, source_target_pairs={{0,4},{1,5},{2,6},{3,7},{4,0},{5,1},{6,2},{7,3},{8,12},{9,13},{10,... | collective-permute-start | bytes 442376 | tf_op jit(solution)/shard_map/ppermute | solution.py:793
  71.1 5.1 %scan_backward.2 = (bf16[512,768]{1,0:T(8,128)(2,1)S(1)}, f32[128,384]{1,0:T(8,128)S(1)}, f32[8,640]{1,0:T(8,128)S(1)}, f32[8,640]{1,0:T(8,128)S(1)}, f32[8,128]{1,0:T(8,128)S(1)}) custom-call(f32[1032,640]{1,0:T(8,128)S(1)} %get-tuple-element.117.refs_0_, f32[1024,128]{1,0:T(8,128)S(1)} %get-tuple-element.118.refs_1_, ...), custom_call_target="tpu_custom_call" | custom-call | flops 20999999488 | tf_op jit(solution)/shard_map/scan_backward/pallas_call | solution.py:770
  77.8 5.8 %scan_backward.3 = (bf16[1024,768]{1,0:T(8,128)(2,1)S(1)}, f32[128,384]{1,0:T(8,128)}, f32[8,640]{1,0:T(8,128)}, f32[8,640]{1,0:T(8,128)S(1)}, f32[8,128]{1,0:T(8,128)S(1)}) custom-call(f32[1032,640]{1,0:T(8,128)S(1)} %get-tuple-element.117.refs_0_, f32[1024,128]{1,0:T(8,128)S(1)} %get-tuple-element.118.refs_1_, f32[1040,128]{1,0:T(8,128)S(1)} %get-tuple-element.119.refs_2_, ...), custom_call_target="tpu_custom_call" | custom-call | flops 20999999488 | tf_op jit(solution)/shard_map/scan_backward/pallas_call | solution.py:770
  83.6 2.2 %normed_grads.1 = (bf16[256,768]{1,0:T(8,128)(2,1)S(1)}, bf16[256,768]{1,0:T(8,128)(2,1)S(1)}, bf16[256,768]{1,0:T(8,128)(2,1)S(1)}, bf16[256,768]{1,0:T(8,128)(2,1)S(1)}) custom-call(bf16[1024,768]{1,0:T(8,128)(2,1)S(1)} %get-tuple-element.181.gp_ref, bf16[768,768]{1,0:T(8,128)(2,1)S(1)} %get-tuple-element.173.w_ref, ...), custom_call_target="tpu_custom_call" | custom-call | flops 35999997952 | tf_op jit(solution)/shard_map/normed_grads/pallas_call | solution.py:770
  85.9 1.7 %main_grads.1 = (bf16[4,112,768]{2,1,0:T(8,128)(2,1)S(1)}, bf16[4,112,768]{2,1,0:T(8,128)(2,1)S(1)}) custom-call(bf16[1024,768]{1,0:T(8,128)(2,1)S(1)} %get-tuple-element.143.refs_0_.refs_4_.normed_ref, bf16[1024,768]{1,0:T(8,128)(2,1)S(1)} %get-tuple-element.181.gp_ref, bf16[768,768]{1,0:T(8,128)(2,1)S(1)} %get-tuple-element.173.w_ref, ...), custom_call_target="tpu_custom_call" | custom-call | flops 48000000000 | tf_op jit(solution)/shard_map/main_grads/pallas_call | solution.py:770
  90.6 1.8 %collective-permute-start.37 = (bf16[112,768]{1,0:T(8,128)(2,1)S(1)}, bf16[112,768]{1,0:T(8,128)(2,1)S(1)}, u32[]{:S(2)}, u32[]{:S(2)}) collective-permute-start(bf16[112,768]{1,0:T(8,128)(2,1)S(1)} %get-tuple-element.189), channel_id=1, source_target_pairs={{0,2},{1,3},{2,0},{3,1},{4,6},{5,7},{6,4},{7,5},{8,10},{9,11},{10,... | collective-permute-start | bytes 516104 | tf_op jit(solution)/shard_map/ppermute | solution.py:793
  92.4 1.8 %collective-permute-start.38 = (bf16[112,768]{1,0:T(8,128)(2,1)S(1)}, bf16[112,768]{1,0:T(8,128)(2,1)S(1)}, u32[]{:S(2)}, u32[]{:S(2)}) collective-permute-start(bf16[112,768]{1,0:T(8,128)(2,1)S(1)} %get-tuple-element.190), channel_id=1, source_target_pairs={{0,4},{1,5},{2,6},{3,7},{4,0},{5,1},{6,2},{7,3},{8,12},{9,13},{10,... | collective-permute-start | bytes 516104 | tf_op jit(solution)/shard_map/ppermute | solution.py:793
  95.4 3.8 %collective-permute-done.37.refs_1_ = bf16[112,768]{1,0:T(8,128)(2,1)S(1)} collective-permute-done((bf16[112,768]{1,0:T(8,128)(2,1)S(1)}, bf16[112,768]{1,0:T(8,128)(2,1)S(1)}, u32[]{:S(2)}, u32[]{:S(2)}) %collective-permute-start.37) | collective-permute-done | bytes 172064 | tf_op jit(solution)/shard_map/ppermute | solution.py:793
  99.2 1.8 %collective-permute-start.34 = (bf16[256,768]{1,0:T(8,128)(2,1)S(1)}, bf16[256,768]{1,0:T(8,128)(2,1)S(1)}, u32[]{:S(2)}, u32[]{:S(2)}) collective-permute-start(bf16[256,768]{1,0:T(8,128)(2,1)S(1)} %get-tuple-element.178), channel_id=1, source_target_pairs={{0,24},{8,16},{16,8},{24,0},{1,25},{9,17},{17,9},{25,1},{2,26},{10... | collective-permute-start | bytes 1179656 | tf_op jit(solution)/shard_map/ppermute | solution.py:793
  101.0 5.4 %collective-permute-done.38.refs_2_ = bf16[112,768]{1,0:T(8,128)(2,1)S(1)} collective-permute-done((bf16[112,768]{1,0:T(8,128)(2,1)S(1)}, bf16[112,768]{1,0:T(8,128)(2,1)S(1)}, u32[]{:S(2)}, u32[]{:S(2)}) %collective-permute-start.38) | collective-permute-done | bytes 172064 | tf_op jit(solution)/shard_map/ppermute | solution.py:793
  106.3 3.6 %collective-permute-done.39.refs_3_ = bf16[112,768]{1,0:T(8,128)(2,1)S(1)} collective-permute-done((bf16[112,768]{1,0:T(8,128)(2,1)S(1)}, bf16[112,768]{1,0:T(8,128)(2,1)S(1)}, u32[]{:S(2)}, u32[]{:S(2)}) %collective-permute-start.39) | collective-permute-done | bytes 172064 | tf_op jit(solution)/shard_map/ppermute | solution.py:793
  (117 shorter events, 44.4 us)
Async XLA Ops:
  10.0 15.2 %collective-permute-start.5 = (bf16[256,768]{1,0:T(8,128)(2,1)S(1)}, bf16[256,768]{1,0:T(8,128)(2,1)S(1)}, u32[]{:S(2)}, u32[]{:S(2)}) collective-permute-start(bf16[256,768]{1,0:T(8,128)(2,1)S(1)} %bitcast.10), channel_id=1, source_target_pairs={{0,24},{8,16},{16,8},{24,0},{1,25},{9,17},{17,9},{25,1},{2,26},{10... | collective-permute-start | bytes 1179656 | tf_op jit(solution)/shard_map/ppermute | solution.py:793
  11.1 17.2 %collective-permute-start.3 = (bf16[256,768]{1,0:T(8,128)(2,1)S(1)}, bf16[256,768]{1,0:T(8,128)(2,1)S(1)}, u32[]{:S(2)}, u32[]{:S(2)}) collective-permute-start(bf16[256,768]{1,0:T(8,128)(2,1)S(1)} %bitcast.11), channel_id=1, source_target_pairs={{0,16},{8,24},{16,0},{24,8},{1,17},{9,25},{17,1},{25,9},{2,18},{10... | collective-permute-start | bytes 1179656 | tf_op jit(solution)/shard_map/ppermute | solution.py:793
  12.7 10.8 %collective-permute-start.8 = (bf16[96,768]{1,0:T(8,128)(2,1)S(1)}, bf16[96,768]{1,0:T(8,128)(2,1)S(1)}, u32[]{:S(2)}, u32[]{:S(2)}) collective-permute-start(bf16[96,768]{1,0:T(8,128)(2,1)S(1)} %get-tuple-element.115.refs_8_), channel_id=1, source_target_pairs={{0,6},{1,7},{2,4},{3,5},{4,2},{5,3},{6,0},{7,1},{8,14},{9,15},{10,... | collective-permute-start | bytes 442376 | tf_op jit(solution)/shard_map/ppermute | solution.py:793
  14.3 10.4 %collective-permute-start.7 = (bf16[96,768]{1,0:T(8,128)(2,1)S(1)}, bf16[96,768]{1,0:T(8,128)(2,1)S(1)}, u32[]{:S(2)}, u32[]{:S(2)}) collective-permute-start(bf16[96,768]{1,0:T(8,128)(2,1)S(1)} %get-tuple-element.115.refs_8_), channel_id=1, source_target_pairs={{0,4},{1,5},{2,6},{3,7},{4,0},{5,1},{6,2},{7,3},{8,12},{9,13},{10,... | collective-permute-start | bytes 442376 | tf_op jit(solution)/shard_map/ppermute | solution.py:793
  15.6 9.2 %collective-permute-start.6 = (bf16[96,768]{1,0:T(8,128)(2,1)S(1)}, bf16[96,768]{1,0:T(8,128)(2,1)S(1)}, u32[]{:S(2)}, u32[]{:S(2)}) collective-permute-start(bf16[96,768]{1,0:T(8,128)(2,1)S(1)} %get-tuple-element.115.refs_8_), channel_id=1, source_target_pairs={{0,2},{1,3},{2,0},{3,1},{4,6},{5,7},{6,4},{7,5},{8,10},{9,11},{10,... | collective-permute-start | bytes 442376 | tf_op jit(solution)/shard_map/ppermute | solution.py:793
  24.8 8.7 %collective-permute-start.9 = (bf16[96,768]{1,0:T(8,128)(2,1)S(1)}, bf16[96,768]{1,0:T(8,128)(2,1)S(1)}, u32[]{:S(2)}, u32[]{:S(2)}) collective-permute-start(bf16[96,768]{1,0:T(8,128)(2,1)S(1)} %get-tuple-element.115.refs_8_), channel_id=1, source_target_pairs={{0,1},{1,0},{2,3},{3,2},{4,5},{5,4},{6,7},{7,6},{8,9},{9,8},{10,11... | collective-permute-start | bytes 442376 | tf_op jit(solution)/shard_map/ppermute | solution.py:793
  24.8 8.7 %collective-permute-start.12 = (bf16[96,768]{1,0:T(8,128)(2,1)S(1)}, bf16[96,768]{1,0:T(8,128)(2,1)S(1)}, u32[]{:S(2)}, u32[]{:S(2)}) collective-permute-start(bf16[96,768]{1,0:T(8,128)(2,1)S(1)} %collective-permute-done.8.refs_11_), channel_id=1, source_target_pairs={{0,1},{1,0},{2,3},{3,2},{4,5},{5,4},{6,7},{7,6},{8,9},{9,8},{10,11... | collective-permute-start | bytes 442376 | tf_op jit(solution)/shard_map/ppermute | solution.py:793
  25.3 9.6 %collective-permute-start.11 = (bf16[96,768]{1,0:T(8,128)(2,1)S(1)}, bf16[96,768]{1,0:T(8,128)(2,1)S(1)}, u32[]{:S(2)}, u32[]{:S(2)}) collective-permute-start(bf16[96,768]{1,0:T(8,128)(2,1)S(1)} %collective-permute-done.7.refs_10_), channel_id=1, source_target_pairs={{0,1},{1,0},{2,3},{3,2},{4,5},{5,4},{6,7},{7,6},{8,9},{9,8},{10,11... | collective-permute-start | bytes 442376 | tf_op jit(solution)/shard_map/ppermute | solution.py:793
  31.3 10.8 %collective-permute-start.15 = (bf16[96,768]{1,0:T(8,128)(2,1)S(1)}, bf16[96,768]{1,0:T(8,128)(2,1)S(1)}, u32[]{:S(2)}, u32[]{:S(2)}) collective-permute-start(bf16[96,768]{1,0:T(8,128)(2,1)S(1)} %get-tuple-element.127.refs_2_), channel_id=1, source_target_pairs={{0,6},{1,7},{2,4},{3,5},{4,2},{5,3},{6,0},{7,1},{8,14},{9,15},{10,... | collective-permute-start | bytes 442376 | tf_op jit(solution)/shard_map/ppermute | solution.py:793
  33.4 10.2 %collective-permute-start.14 = (bf16[96,768]{1,0:T(8,128)(2,1)S(1)}, bf16[96,768]{1,0:T(8,128)(2,1)S(1)}, u32[]{:S(2)}, u32[]{:S(2)}) collective-permute-start(bf16[96,768]{1,0:T(8,128)(2,1)S(1)} %get-tuple-element.127.refs_2_), channel_id=1, source_target_pairs={{0,4},{1,5},{2,6},{3,7},{4,0},{5,1},{6,2},{7,3},{8,12},{9,13},{10,... | collective-permute-start | bytes 442376 | tf_op jit(solution)/shard_map/ppermute | solution.py:793
  33.5 10.2 %collective-permute-start.13 = (bf16[96,768]{1,0:T(8,128)(2,1)S(1)}, bf16[96,768]{1,0:T(8,128)(2,1)S(1)}, u32[]{:S(2)}, u32[]{:S(2)}) collective-permute-start(bf16[96,768]{1,0:T(8,128)(2,1)S(1)} %get-tuple-element.127.refs_2_), channel_id=1, source_target_pairs={{0,2},{1,3},{2,0},{3,1},{4,6},{5,7},{6,4},{7,5},{8,10},{9,11},{10,... | collective-permute-start | bytes 442376 | tf_op jit(solution)/shard_map/ppermute | solution.py:793
  34.9 9.6 %collective-permute-start.17 = (bf16[256,768]{1,0:T(8,128)(2,1)S(1)}, bf16[256,768]{1,0:T(8,128)(2,1)S(1)}, u32[]{:S(2)}, u32[]{:S(2)}) collective-permute-start(bf16[256,768]{1,0:T(8,128)(2,1)S(1)} %bitcast.16), channel_id=1, source_target_pairs={{0,16},{8,24},{16,0},{24,8},{1,17},{9,25},{17,1},{25,9},{2,18},{10... | collective-permute-start | bytes 1179656 | tf_op jit(solution)/shard_map/ppermute | solution.py:793
  35.5 10.4 %collective-permute-start.16 = (bf16[256,768]{1,0:T(8,128)(2,1)S(1)}, bf16[256,768]{1,0:T(8,128)(2,1)S(1)}, u32[]{:S(2)}, u32[]{:S(2)}) collective-permute-start(bf16[256,768]{1,0:T(8,128)(2,1)S(1)} %bitcast.17), channel_id=1, source_target_pairs={{0,8},{8,0},{16,24},{24,16},{1,9},{9,1},{17,25},{25,17},{2,10},{10... | collective-permute-start | bytes 1179656 | tf_op jit(solution)/shard_map/ppermute | solution.py:793
  42.1 11.1 %collective-permute-start.22 = (bf16[256,768]{1,0:T(8,128)(2,1)S(1)}, bf16[256,768]{1,0:T(8,128)(2,1)S(1)}, u32[]{:S(2)}, u32[]{:S(2)}) collective-permute-start(bf16[256,768]{1,0:T(8,128)(2,1)S(1)} %bitcast.18), channel_id=1, source_target_pairs={{0,24},{8,16},{16,8},{24,0},{1,25},{9,17},{17,9},{25,1},{2,26},{10... | collective-permute-start | bytes 1179656 | tf_op jit(solution)/shard_map/ppermute | solution.py:793
  64.4 21.5 %collective-permute-start.26 = (bf16[256,768]{1,0:T(8,128)(2,1)S(1)}, bf16[256,768]{1,0:T(8,128)(2,1)S(1)}, u32[]{:S(2)}, u32[]{:S(2)}) collective-permute-start(bf16[256,768]{1,0:T(8,128)(2,1)S(1)} %get-tuple-element.140), channel_id=1, source_target_pairs={{0,8},{8,0},{16,24},{24,16},{1,9},{9,1},{17,25},{25,17},{2,10},{10... | collective-permute-start | bytes 1179656 | tf_op jit(solution)/shard_map/ppermute | solution.py:793
  65.6 20.3 %collective-permute-start.27 = (bf16[256,768]{1,0:T(8,128)(2,1)S(1)}, bf16[256,768]{1,0:T(8,128)(2,1)S(1)}, u32[]{:S(2)}, u32[]{:S(2)}) collective-permute-start(bf16[256,768]{1,0:T(8,128)(2,1)S(1)} %get-tuple-element.141), channel_id=1, source_target_pairs={{0,16},{8,24},{16,0},{24,8},{1,17},{9,25},{17,1},{25,9},{2,18},{10... | collective-permute-start | bytes 1179656 | tf_op jit(solution)/shard_map/ppermute | solution.py:793
  66.2 19.7 %collective-permute-start.28 = (bf16[256,768]{1,0:T(8,128)(2,1)S(1)}, bf16[256,768]{1,0:T(8,128)(2,1)S(1)}, u32[]{:S(2)}, u32[]{:S(2)}) collective-permute-start(bf16[256,768]{1,0:T(8,128)(2,1)S(1)} %get-tuple-element.142), channel_id=1, source_target_pairs={{0,24},{8,16},{16,8},{24,0},{1,25},{9,17},{17,9},{25,1},{2,26},{10... | collective-permute-start | bytes 1179656 | tf_op jit(solution)/shard_map/ppermute | solution.py:793
  68.7 9.0 %collective-permute-start.31 = (bf16[96,768]{1,0:T(8,128)(2,1)S(1)}, bf16[96,768]{1,0:T(8,128)(2,1)S(1)}, u32[]{:S(2)}, u32[]{:S(2)}) collective-permute-start(bf16[96,768]{1,0:T(8,128)(2,1)S(1)} %get-tuple-element.153), channel_id=1, source_target_pairs={{0,4},{1,5},{2,6},{3,7},{4,0},{5,1},{6,2},{7,3},{8,12},{9,13},{10,... | collective-permute-start | bytes 442376 | tf_op jit(solution)/shard_map/ppermute | solution.py:793
  76.2 9.7 %collective-permute-start.35 = (bf16[96,768]{1,0:T(8,128)(2,1)S(1)}, bf16[96,768]{1,0:T(8,128)(2,1)S(1)}, u32[]{:S(2)}, u32[]{:S(2)}) collective-permute-start(bf16[96,768]{1,0:T(8,128)(2,1)S(1)} %get-tuple-element.179), channel_id=1, source_target_pairs={{0,6},{1,7},{2,4},{3,5},{4,2},{5,3},{6,0},{7,1},{8,14},{9,15},{10,... | collective-permute-start | bytes 442376 | tf_op jit(solution)/shard_map/ppermute | solution.py:793
  88.7 23.7 %collective-permute-start.32 = (bf16[256,768]{1,0:T(8,128)(2,1)S(1)}, bf16[256,768]{1,0:T(8,128)(2,1)S(1)}, u32[]{:S(2)}, u32[]{:S(2)}) collective-permute-start(bf16[256,768]{1,0:T(8,128)(2,1)S(1)} %get-tuple-element.176), channel_id=1, source_target_pairs={{0,8},{8,0},{16,24},{24,16},{1,9},{9,1},{17,25},{25,17},{2,10},{10... | collective-permute-start | bytes 1179656 | tf_op jit(solution)/shard_map/ppermute | solution.py:793
  89.9 23.7 %collective-permute-start.33 = (bf16[256,768]{1,0:T(8,128)(2,1)S(1)}, bf16[256,768]{1,0:T(8,128)(2,1)S(1)}, u32[]{:S(2)}, u32[]{:S(2)}) collective-permute-start(bf16[256,768]{1,0:T(8,128)(2,1)S(1)} %get-tuple-element.177), channel_id=1, source_target_pairs={{0,16},{8,24},{16,0},{24,8},{1,17},{9,25},{17,1},{25,9},{2,18},{10... | collective-permute-start | bytes 1179656 | tf_op jit(solution)/shard_map/ppermute | solution.py:793
  92.4 13.9 %collective-permute-start.38 = (bf16[112,768]{1,0:T(8,128)(2,1)S(1)}, bf16[112,768]{1,0:T(8,128)(2,1)S(1)}, u32[]{:S(2)}, u32[]{:S(2)}) collective-permute-start(bf16[112,768]{1,0:T(8,128)(2,1)S(1)} %get-tuple-element.190), channel_id=1, source_target_pairs={{0,4},{1,5},{2,6},{3,7},{4,0},{5,1},{6,2},{7,3},{8,12},{9,13},{10,... | collective-permute-start | bytes 516104 | tf_op jit(solution)/shard_map/ppermute | solution.py:793
  94.2 15.8 %collective-permute-start.39 = (bf16[112,768]{1,0:T(8,128)(2,1)S(1)}, bf16[112,768]{1,0:T(8,128)(2,1)S(1)}, u32[]{:S(2)}, u32[]{:S(2)}) collective-permute-start(bf16[112,768]{1,0:T(8,128)(2,1)S(1)} %get-tuple-element.191), channel_id=1, source_target_pairs={{0,6},{1,7},{2,4},{3,5},{4,2},{5,3},{6,0},{7,1},{8,14},{9,15},{10,... | collective-permute-start | bytes 516104 | tf_op jit(solution)/shard_map/ppermute | solution.py:793
  99.2 14.4 %collective-permute-start.34 = (bf16[256,768]{1,0:T(8,128)(2,1)S(1)}, bf16[256,768]{1,0:T(8,128)(2,1)S(1)}, u32[]{:S(2)}, u32[]{:S(2)}) collective-permute-start(bf16[256,768]{1,0:T(8,128)(2,1)S(1)} %get-tuple-element.178), channel_id=1, source_target_pairs={{0,24},{8,16},{16,8},{24,0},{1,25},{9,17},{17,9},{25,1},{2,26},{10... | collective-permute-start | bytes 1179656 | tf_op jit(solution)/shard_map/ppermute | solution.py:793
  (35 other events, 249.4 us)
